TPU v7x, 128 devices: a whole 4x4x4 slice. The times are simulated.
128 devices in a mesh: lat: 8 (over x, y_hi), lon: 16 (over z, y_lo, core).
Axes of the slice: x: 4, y: 4 (y_hi: 2, y_lo: 2; y = y_hi * 2 + y_lo), z: 4, core: 2. Of those that a mesh axis runs over, the one named last changes fastest.
Arguments:
- features: bfloat16 [256, 384, 2048], P('lat', 'lon'), may hold values from -6 to 6
- atrous_weight: bfloat16 [3, 3, 2048, 256], replicated, may hold values from -0.046875 to 0.046875
- norm_gain: float32 [256], replicated, may hold values from 0.1 to 1.9
- norm_bias: float32 [256], replicated, may hold values from -0.5 to 0.5
- head_weight: float32 [3, 256], replicated, may hold values from -1.5 to 1.5
- labels: int32 [256, 384], P('lat', 'lon'), may hold values from 0 to 2
Outputs:
- mean_loss: float32 [], replicated
- grad_features: bfloat16 [256, 384, 2048], P('lat', 'lon')
- grad_weight: float32 [2048, 3, 3, 256], P('lat', None, None, 'lon')
- grad_gain: float32 [256], replicated
- grad_bias: float32 [256], replicated
- grad_head: float32 [3, 256], replicated
All inputs are finite; a program needn't handle non-finite values.
Results may differ from a plain program's by a relative error of at most 0.022.
Values may be sent and summed in bfloat16 or wider, within the bound.
No kernel may reach another device: no remote copies, remote signals or barrier semaphores. Data moves between devices by JAX's collectives and lax.ppermute only.
A program may use at most 192 MiB of HBM per device.

v0:
```python
import jax
import jax.numpy as jnp
from jax import lax
from jax.sharding import PartitionSpec as P

RATE = 12


epsilon = 1e-05


def padded_2(block, sides, width, periodic):
    for axis, dim in sides:
        count = lax.axis_size(axis)
        forward = [(i, i + 1) for i in range(count - 1)]
        if periodic:
            forward.append((count - 1, 0))
        backward = [(target, source) for source, target in forward]
        low = lax.ppermute(
            lax.slice_in_dim(block, block.shape[dim] - width, None, axis=dim), axis, forward
        )
        high = lax.ppermute(lax.slice_in_dim(block, 0, width, axis=dim), axis, backward)
        block = jnp.concatenate([low, block, high], axis=dim)
    return block


def shards(features, atrous_weight, norm_gain, norm_bias, head_weight, labels):
    height, breadth, channels = features.shape
    filters = atrous_weight.shape[3]
    local_cells = height * breadth
    total_cells = local_cells * lax.axis_size("lat") * lax.axis_size("lon")
    flat_input = features.reshape(local_cells, channels)
    lon_padded = padded_2(features, (("lon", 1),), RATE, True)
    padded = padded_2(lon_padded, (("lat", 0),), RATE, False)
    summed = jnp.zeros((local_cells, filters), jnp.float32)
    for tap_row in range(3):
        for tap_col in range(3):
            window = padded[
                tap_row * RATE : tap_row * RATE + height, tap_col * RATE : tap_col * RATE + breadth
            ]
            summed = summed + jnp.dot(
                window.reshape(local_cells, channels),
                atrous_weight[tap_row, tap_col],
                preferred_element_type=jnp.float32,
            )
    moments = lax.psum((jnp.sum(summed, 0), jnp.sum(summed * summed, 0)), ("lat", "lon"))
    average = moments[0] / total_cells
    variance = moments[1] / total_cells - average * average
    inverse = lax.rsqrt(variance + epsilon)
    normed = (summed - average) * inverse
    preact = norm_gain * normed + norm_bias
    hidden = jnp.maximum(preact, 0.0).astype(jnp.bfloat16)
    hidden_wide = hidden.astype(jnp.float32)
    logits = jnp.dot(hidden_wide, head_weight.T, precision=lax.Precision.HIGHEST)
    one_hot = (
        labels.reshape(local_cells)[:, None]
        == jnp.arange(head_weight.shape[0], dtype=jnp.int32)[None, :]
    ).astype(jnp.float32)
    exponent = jnp.exp(logits)
    partition = jnp.sum(exponent, 1, keepdims=True)
    loss_terms = jnp.sum(jnp.log(partition)[:, 0] - jnp.sum(logits * one_hot, 1))
    grad_logits = exponent / partition - one_hot
    head_term = jnp.dot(grad_logits.T, hidden_wide, precision=lax.Precision.HIGHEST)
    d_hidden = jnp.dot(grad_logits, head_weight, precision=lax.Precision.HIGHEST)
    d_preact = jnp.where(preact > 0, d_hidden, 0.0)
    totals = lax.psum(
        (jnp.sum(d_preact, 0), jnp.sum(d_preact * normed, 0), head_term, loss_terms), ("lat", "lon")
    )
    grad_bias = totals[0] / total_cells
    grad_gain = totals[1] / total_cells
    grad_head = totals[2] / total_cells
    mean_loss = totals[3] / total_cells
    d_summed = (norm_gain * inverse * (d_preact - grad_bias - normed * grad_gain)).astype(
        jnp.bfloat16
    )
    d_grid = d_summed.reshape(height, breadth, filters)
    grad_lon = padded_2(d_grid, (("lon", 1),), RATE, True)
    grad_padded = padded_2(grad_lon, (("lat", 0),), RATE, False)
    grad_acc = jnp.zeros((local_cells, channels), jnp.float32)
    shifted_taps = []
    for tap_row in range(3):
        for tap_col in range(3):
            row_first = (2 - tap_row) * RATE
            col_first = (2 - tap_col) * RATE
            shifted = grad_padded[
                row_first : row_first + height, col_first : col_first + breadth
            ].reshape(local_cells, filters)
            shifted_taps.append(shifted)
            grad_acc = grad_acc + lax.dot_general(
                shifted,
                atrous_weight[tap_row, tap_col],
                (((1,), (1,)), ((), ())),
                preferred_element_type=jnp.float32,
            )
    grad_features = grad_acc.astype(jnp.bfloat16).reshape(height, breadth, channels)
    channel_block = channels // lax.axis_size("lat")
    filter_block = filters // lax.axis_size("lon")
    shifted_all = jnp.stack(shifted_taps, 0)
    lon_summed = lax.psum_scatter(
        jnp.einsum(
            "tqf,qc->ftc", shifted_all, flat_input, preferred_element_type=jnp.float32
        ).astype(jnp.bfloat16),
        "lon",
        scatter_dimension=0,
        tiled=True,
    )
    weight_block = jnp.transpose(
        lax.psum_scatter(lon_summed, "lat", scatter_dimension=2, tiled=True).astype(jnp.float32),
        (2, 1, 0),
    )
    grad_weight = (weight_block / total_cells).reshape(channel_block, 3, 3, filter_block)
    return (mean_loss, grad_features, grad_weight, grad_gain, grad_bias, grad_head)


def solution(mesh):
    return jax.shard_map(
        shards,
        mesh=mesh,
        in_specs=(P("lat", "lon", None), P(), P(), P(), P(), P("lat", "lon")),
        out_specs=(P(), P("lat", "lon", None), P("lat", None, None, "lon"), P(), P(), P()),
        check_vma=False,
    )
```

profile of v0, /device:TPU:1, one launch (start us, length us, event | category | flops | bytes accessed | tf_op | source)
XLA Modules:
  0.0 565.9 jit_solution(16156541013725347236)
XLA Ops:
  14.9 31.5 %collective-permute-done.1 = bf16[32,12,2048]{2,0,1:T(8,128)(2,1)S(1)} collective-permute-done((bf16[32,12,2048]{2,0,1:T(8,128)(2,1)S(1)}, bf16[32,12,2048]{2,0,1:T(8,128)(2,1)S(1)}, u32[]{:S(2)}, u32[]{:S(2)}) %collective-permute-start.1) | collective-permute-done | bytes 1572896 | tf_op jit(solution)/shard_map/ppermute | solution.py:22
  48.3 4.8 pad_maximum_fusion.5
  53.1 6.3 %collective-permute-start.2 = (bf16[12,48,2048]{2,1,0:T(8,128)(2,1)}, bf16[12,48,2048]{2,1,0:T(8,128)(2,1)}, u32[]{:S(2)}, u32[]{:S(2)}) collective-permute-start(bf16[12,48,2048]{2,1,0:T(8,128)(2,1)} %get-tuple-element.26), channel_id=1, source_target_pairs={{0,16},{16,32},{32,48},{48,64},{64,80},{80,96},{96,112},{1,17},{17... | collective-permute-start | bytes 7077896 | tf_op jit(solution)/shard_map/ppermute | solution.py:19
  63.4 3.9 pad_maximum_fusion.1
  70.4 85.6 %collective-permute-done.2 = bf16[12,48,2048]{2,1,0:T(8,128)(2,1)} collective-permute-done((bf16[12,48,2048]{2,1,0:T(8,128)(2,1)}, bf16[12,48,2048]{2,1,0:T(8,128)(2,1)}, u32[]{:S(2)}, u32[]{:S(2)}) %collective-permute-start.2) | collective-permute-done | bytes 2359328 | tf_op jit(solution)/shard_map/ppermute | solution.py:19
  156.0 10.6 %maximum_maximum_fusion = (bf16[44,48,2048]{2,1,0:T(8,128)(2,1)S(1)}, bf16[44,48,2048]{2,1,0:T(8,128)(2,1)}) fusion(bf16[32,12,2048]{2,1,0:T(8,128)(2,1)S(1)} %copy-done.4, bf16[32,24,2048]{2,1,0:T(8,128)(2,1)S(1)} %copy-done.2, bf16[32,12,2048]{2,1,0:T(8,128)(2,1)S(1)} %copy-done.6, bf16[12,48,2048]{2,1,0:T(8,128)(2,1)} %collective-permute-done.2, ...), kind=kLoop, calls=%fused_computation.1 | loop fusion | flops 69206016 | bytes 28311552 | tf_op jit(solution)/shard_map/concatenate | solution.py:23
  166.6 10.5 %fusion.61 = (bf16[32,24,2048]{2,1,0:T(8,128)(2,1)}, bf16[32,24,2048]{2,1,0:T(8,128)(2,1)}, bf16[32,24,2048]{2,1,0:T(8,128)(2,1)}, bf16[32,24,2048]{2,1,0:T(8,12...) fusion(bf16[44,48,2048]{2,1,0:T(8,128)(2,1)S(1)} %get-tuple-element.24, ...), kind=kLoop, calls=%fused_computation.106 | loop fusion | bytes 37748736 | tf_op jit(solution)/shard_map/slice | solution.py:38
  195.7 74.2 %all-reduce.1 = (f32[256]{0:T(256)S(1)}, f32[256]{0:T(256)S(1)}) all-reduce(f32[256]{0:T(256)S(1)} %get-tuple-element.9, f32[256]{0:T(256)S(1)} %get-tuple-element.8), channel_id=1, replica_groups=mesh['lat'=8,'lon'=16] {'lat','lon'}, use_global_device_ids=true, to_apply=%region_3.0 | all-reduce | flops 512 | bytes 4096 | tf_op jit(solution)/shard_map/psum | solution.py:46
  276.1 62.9 %all-reduce = (f32[]{:T(128)}, f32[256]{0:T(256)S(1)}, f32[256]{0:T(256)S(1)}, f32[3,256]{1,0:T(4,128)}) all-reduce(f32[]{:T(128)} %subtract_reduce_fusion, f32[256]{0:T(256)S(1)} %get-tuple-element.7, f32[256]{0:T(256)S(1)} %get-tuple-element.6, f32[3,256]{1,0:T(4,128)S(1)} %fusion.58), channel_id=1, replica_groups=mesh['lat'=8,'lon'=16] {'lat','lon'}, use_global_device_ids=true, to_apply=%region_7.8 | all-reduce | flops 1281 | bytes 10248 | tf_op jit(solution)/shard_map/psum | solution.py:66
  346.0 4.1 collective-permute-done.5
  351.6 5.5 collective-permute-start.7
  360.6 6.9 %collective-permute-done.7 = bf16[12,48,256]{2,1,0:T(8,128)(2,1)S(1)} collective-permute-done((bf16[12,48,256]{2,1,0:T(8,128)(2,1)S(1)}, bf16[12,48,256]{2,1,0:T(8,128)(2,1)S(1)}, u32[]{:S(2)}, u32[]{:S(2)}) %collective-permute-start.7) | collective-permute-done | bytes 294944 | tf_op jit(solution)/shard_map/ppermute | solution.py:19
  369.4 9.8 %convert_bitcast_fusion = bf16[256,9,2048]{2,0,1:T(8,128)(2,1)} fusion(bf16[9,768,256]{2,1,0:T(8,128)(2,1)S(1)} %bitcast_dynamic-update-slice_fusion, bf16[768,2048,1]{1,0,2:T(8,128)(2,1)S(1)} %bitcast.124), kind=kOutput, calls=%fused_computation | convolution fusion | flops 7252475904 | bytes 16121856 | tf_op jit(solution)/shard_map/tqf,qc->ftc/dot_general | solution.py:100
  380.8 5.1 fusion.20
  385.9 5.0 fusion.17
  390.9 3.7 fusion.24
  394.6 3.6 fusion.13
  398.2 3.6 fusion.9
  401.8 3.7 fusion.36
  405.5 3.6 fusion.28
  409.1 3.6 fusion.32
  412.8 72.8 %reduce-scatter.3.cloned.1.call-done = bf16[16,9,2048]{2,0,1:T(8,128)(2,1)} async-done(((bf16[256,9,2048]{2,0,1:T(8,128)(2,1)}), bf16[16,9,2048]{2,0,1:T(8,128)(2,1)}) %reduce-scatter.3.cloned.1.call-update) | async-done | bytes 589840 | tf_op jit(solution)/shard_map/reduce_scatter | solution.py:99
  485.7 18.9 %add_convert_fusion = bf16[768,2048]{1,0:T(8,128)(2,1)} fusion(f32[768,2048]{1,0:T(8,128)} %fusion.9, f32[768,2048]{1,0:T(8,128)} %fusion.13, f32[768,2048]{1,0:T(8,128)} %fusion.17, f32[768,2048]{1,0:T(8,128)} %fusion.20, f32[768,2048]{1,0:T(8,128)} %fusion.24, f32[768,2048]{1,0:T(8,128)} %fusion.28, f32[768,2048]{1,0:T(8,128)} %fusion.36, ...), kind=kOutput, calls=%fused_computation.3 | convolution fusion | flops 819462144 | bytes 54919168 | tf_op jit(solution)/shard_map/dot_general | solution.py:89
  504.5 51.4 %reduce-scatter.5.cloned.1.call-done = bf16[16,9,256]{2,0,1:T(8,128)(2,1)} async-done(((bf16[16,9,2048]{2,0,1:T(8,128)(2,1)}), bf16[16,9,256]{2,0,1:T(8,128)(2,1)}) %reduce-scatter.5.cloned.1.call-update) | async-done | bytes 73744 | tf_op jit(solution)/shard_map/reduce_scatter | solution.py:108
  (135 shorter events, 57.5 us)
Async XLA Ops:
  7.2 264.5 %copy-start = (f32[3,256]{1,0:T(4,128)S(1)}, f32[3,256]{1,0:T(4,128)}, u32[]{:S(2)}) copy-start(f32[3,256]{1,0:T(4,128)} %param.10) | copy-start | bytes 9220
  7.2 478.4 %reduce-scatter.3.cloned.1.call-start = ((), (), s32[]{:S(2)}) async-start(), calls=%async_computation.2 | async-start | bytes 10027008 | tf_op jit(solution)/shard_map/reduce_scatter | solution.py:99
  11.2 35.2 %collective-permute-start.1 = (bf16[32,12,2048]{2,0,1:T(8,128)(2,1)S(1)}, bf16[32,12,2048]{2,0,1:T(8,128)(2,1)S(1)}, u32[]{:S(2)}, u32[]{:S(2)}) collective-permute-start(bf16[32,12,2048]{2,0,1:T(8,128)(2,1)S(1)} %copy.25), channel_id=1, source_target_pairs={{1,0},{2,1},{3,2},{4,3},{5,4},{6,5},{7,6},{8,7},{9,8},{10,9},{11,1... | collective-permute-start | bytes 4718600 | tf_op jit(solution)/shard_map/ppermute | solution.py:22
  13.6 34.6 %copy-start.2 = (bf16[32,24,2048]{2,1,0:T(8,128)(2,1)S(1)}, bf16[32,24,2048]{2,1,0:T(8,128)(2,1)}, u32[]{:S(2)}) copy-start(bf16[32,24,2048]{2,1,0:T(8,128)(2,1)} %param.6) | copy-start | bytes 9437188
  13.6 33.7 %collective-permute-start = (bf16[32,12,2048]{2,0,1:T(8,128)(2,1)S(1)}, bf16[32,12,2048]{2,0,1:T(8,128)(2,1)S(1)}, u32[]{:S(2)}, u32[]{:S(2)}) collective-permute-start(bf16[32,12,2048]{2,0,1:T(8,128)(2,1)S(1)} %copy.24), channel_id=1, source_target_pairs={{0,1},{1,2},{2,3},{3,4},{4,5},{5,6},{6,7},{7,8},{8,9},{9,10},{10,1... | collective-permute-start | bytes 4718600 | tf_op jit(solution)/shard_map/ppermute | solution.py:19
  47.3 5.8 %copy-start.3 = (bf16[32,12,2048]{2,1,0:T(8,128)(2,1)}, bf16[32,12,2048]{2,1,0:T(8,128)(2,1)S(1)}, u32[]{:S(2)}) copy-start(bf16[32,12,2048]{2,1,0:T(8,128)(2,1)S(1)} %copy.18) | copy-start | bytes 4718596
  48.2 12.5 %copy-start.30 = (s32[32,24]{0,1:T(8,128)S(1)}, s32[32,24]{0,1:T(8,128)}, u32[]{:S(2)}) copy-start(s32[32,24]{0,1:T(8,128)} %param.11) | copy-start | bytes 9220
  53.1 102.9 %collective-permute-start.2 = (bf16[12,48,2048]{2,1,0:T(8,128)(2,1)}, bf16[12,48,2048]{2,1,0:T(8,128)(2,1)}, u32[]{:S(2)}, u32[]{:S(2)}) collective-permute-start(bf16[12,48,2048]{2,1,0:T(8,128)(2,1)} %get-tuple-element.26), channel_id=1, source_target_pairs={{0,16},{16,32},{32,48},{48,64},{64,80},{80,96},{96,112},{1,17},{17... | collective-permute-start | bytes 7077896 | tf_op jit(solution)/shard_map/ppermute | solution.py:19
  59.4 96.6 %collective-permute-start.3 = (bf16[12,48,2048]{2,1,0:T(8,128)(2,1)}, bf16[12,48,2048]{2,1,0:T(8,128)(2,1)}, u32[]{:S(2)}, u32[]{:S(2)}) collective-permute-start(bf16[12,48,2048]{2,1,0:T(8,128)(2,1)} %get-tuple-element.27), channel_id=1, source_target_pairs={{16,0},{32,16},{48,32},{64,48},{80,64},{96,80},{112,96},{17,1},{33... | collective-permute-start | bytes 7077896 | tf_op jit(solution)/shard_map/ppermute | solution.py:22
  192.5 77.3 %copy-start.33 = (f32[256]{0:T(256)S(1)}, f32[256]{0:T(256)}, u32[]{:S(2)}) copy-start(f32[256]{0:T(256)} %param.8) | copy-start | bytes 3076
  192.5 77.9 %copy-start.35 = (f32[256]{0:T(256)S(1)}, f32[256]{0:T(256)}, u32[]{:S(2)}) copy-start(f32[256]{0:T(256)} %param.9) | copy-start | bytes 3076
  338.9 28.8 %copy-start.31 = (f32[256]{0:T(256)}, f32[256]{0:T(256)S(1)}, u32[]{:S(2)}) copy-start(f32[256]{0:T(256)S(1)} %broadcast_multiply_fusion.1) | copy-start | bytes 3076
  339.0 28.9 %copy-start.32 = (f32[256]{0:T(256)}, f32[256]{0:T(256)S(1)}, u32[]{:S(2)}) copy-start(f32[256]{0:T(256)S(1)} %broadcast_multiply_fusion.2) | copy-start | bytes 3076
  340.6 5.4 collective-permute-start.4
  342.7 7.4 %collective-permute-start.5 = (bf16[32,12,256]{2,1,0:T(8,128)(2,1)S(1)}, bf16[32,12,256]{2,1,0:T(8,128)(2,1)S(1)}, u32[]{:S(2)}, u32[]{:S(2)}) collective-permute-start(bf16[32,12,256]{2,1,0:T(8,128)(2,1)S(1)} %get-tuple-element.45), channel_id=1, source_target_pairs={{1,0},{2,1},{3,2},{4,3},{5,4},{6,5},{7,6},{8,7},{9,8},{10,9},{11,1... | collective-permute-start | bytes 589832 | tf_op jit(solution)/shard_map/ppermute | solution.py:22
  350.3 10.3 %collective-permute-start.6 = (bf16[12,48,256]{2,1,0:T(8,128)(2,1)S(1)}, bf16[12,48,256]{2,1,0:T(8,128)(2,1)S(1)}, u32[]{:S(2)}, u32[]{:S(2)}) collective-permute-start(bf16[12,48,256]{2,1,0:T(8,128)(2,1)S(1)} %get-tuple-element.40), channel_id=1, source_target_pairs={{16,0},{32,16},{48,32},{64,48},{80,64},{96,80},{112,96},{17,1},{33... | collective-permute-start | bytes 884744 | tf_op jit(solution)/shard_map/ppermute | solution.py:22
  351.6 15.8 %collective-permute-start.7 = (bf16[12,48,256]{2,1,0:T(8,128)(2,1)S(1)}, bf16[12,48,256]{2,1,0:T(8,128)(2,1)S(1)}, u32[]{:S(2)}, u32[]{:S(2)}) collective-permute-start(bf16[12,48,256]{2,1,0:T(8,128)(2,1)S(1)} %get-tuple-element.41), channel_id=1, source_target_pairs={{0,16},{16,32},{32,48},{48,64},{64,80},{80,96},{96,112},{1,17},{17... | collective-permute-start | bytes 884744 | tf_op jit(solution)/shard_map/ppermute | solution.py:19
  357.4 10.9 %copy-start.19 = (bf16[32,24,256]{2,1,0:T(8,128)(2,1)}, bf16[32,24,256]{2,1,0:T(8,128)(2,1)S(1)}, u32[]{:S(2)}) copy-start(bf16[32,24,256]{2,1,0:T(8,128)(2,1)S(1)} %get-tuple-element.42) | copy-start | bytes 1179652
  357.4 11.0 %copy-start.21 = (bf16[32,24,256]{2,1,0:T(8,128)(2,1)}, bf16[32,24,256]{2,1,0:T(8,128)(2,1)S(1)}, u32[]{:S(2)}) copy-start(bf16[32,24,256]{2,1,0:T(8,128)(2,1)S(1)} %get-tuple-element.43) | copy-start | bytes 1179652
  379.3 176.7 %reduce-scatter.5.cloned.1.call-start = ((), (), s32[]{:S(2)}) async-start(), calls=%async_computation.3 | async-start | bytes 663552 | tf_op jit(solution)/shard_map/reduce_scatter | solution.py:108
  380.8 10.1 %slice-start = ((s8[9437184]{0:T(1024)(128)(4,1)}), s8[4194304]{0:T(1024)(128)(4,1)S(1)}, s32[]{:S(2)}) async-start(s8[9437184]{0:T(1024)(128)(4,1)} %bitcast.131), calls=%async_computation.4 | async-start | bytes 8388608
  380.8 10.1 %slice-start.1 = ((s8[9437184]{0:T(1024)(128)(4,1)}), s8[4194304]{0:T(1024)(128)(4,1)S(1)}, s32[]{:S(2)}) async-start(s8[9437184]{0:T(1024)(128)(4,1)} %bitcast.131), calls=%async_computation.5 | async-start | bytes 8388608
  409.1 76.5 %copy-start.24 = (bf16[32,24,256]{2,1,0:T(8,128)(2,1)S(1)}, bf16[32,24,256]{2,1,0:T(8,128)(2,1)}, u32[]{:S(2)}) copy-start(bf16[32,24,256]{2,1,0:T(8,128)(2,1)} %copy-done.23) | copy-start | bytes 1179652
  485.6 71.8 %copy-start.1 = (f32[3,256]{1,0:T(4,128)S(1)}, f32[3,256]{1,0:T(4,128)}, u32[]{:S(2)}) copy-start(f32[3,256]{1,0:T(4,128)} %param.10) | copy-start | bytes 9220
  (25 other events, 67.5 us)
Sparse Core Ops, SparseCore 0:
  379.4 106.1 reduce-scatter.2
  489.2 66.6 reduce-scatter.4
where the time goes:
time: 574 us; the launch traced here: 566 us
  waiting for transfers between devices  259 us (45%)
  blocking collectives  137 us (24%)
  matrix products  88.1 us (15%)
  other arithmetic  26.4 us (5%)
  starting transfers between devices  19.7 us (3%)
  local copies, waits for them, and re-layouts  19.1 us (3%)
  between operations  16.9 us (3%)
    ppermute x4, waiting for transfers between devices, padded_2(): lax.ppermute(lax.slice_in_dim(block, block.shape[dim] - width, None, axis...  95.8 us
    psum x1, blocking collectives, shards(): lax.psum((jnp.sum(summed, 0), jnp.sum(summed * summed, 0)), ('lat', 'lon'))  74.2 us
    reduce_scatter x1, waiting for transfers between devices, shards(): lax.psum_scatter(jnp.einsum('tqf,qc->ftc', shifted_all, flat_input, prefe...  72.8 us
    psum x1, blocking collectives, shards(): lax.psum((jnp.sum(d_preact, 0), jnp.sum(d_preact * normed, 0), head_term,...  62.9 us
    reduce_scatter x1, waiting for transfers between devices, shards(): lax.psum_scatter(lon_summed, 'lat', scatter_dimension=2, tiled=True)  51.4 us
    dot_general x9, matrix products, shards(): lax.dot_general(shifted, atrous_weight[tap_row, tap_col], (((1,), (1,)),...  50.7 us
    ppermute x4, waiting for transfers between devices, padded_2(): lax.ppermute(lax.slice_in_dim(block, 0, width, axis=dim), axis, backward)  38.7 us
    dot_general x9, matrix products, shards(): jnp.dot(window.reshape(local_cells, channels), atrous_weight[tap_row, tap...  23.8 us
  transfers between devices with their start and end apart: 10, of which 8 were waited for; matrix products, arithmetic and copies ran while one was open for 11% of the time, Pallas kernels for 0%

commit v1 on v0

v1 whole, which is shorter than its diff:
```python
import jax
import jax.numpy as jnp
from jax import lax
from jax.experimental import pallas as pl
from jax.experimental.pallas import tpu as pltpu
from jax.sharding import PartitionSpec as P

RATE = 12
epsilon = 1e-05
BF = jnp.bfloat16
F32 = jnp.float32


def ring(x, axis, step, periodic):
    count = lax.axis_size(axis)
    pairs = [(i, (i + step) % count) for i in range(count)]
    if not periodic:
        pairs = [(i, i + step) for i in range(count) if 0 <= i + step < count]
    return lax.ppermute(x, axis, pairs)


def core_swap(x):
    count = lax.axis_size("lon")
    return lax.ppermute(x, "lon", [(i, i ^ 1) for i in range(count)])


def total(x):
    count = lax.axis_size("lat") * lax.axis_size("lon")
    spread = jnp.broadcast_to(x[None], (count,) + x.shape)
    return jnp.sum(lax.all_to_all(spread, ("lat", "lon"), 0, 0), 0)


def taps_forward(flat, weight, cols, height, breadth):
    cells, channels = flat.shape
    filters = weight.shape[2]
    step_rows = RATE * breadth
    ext = cells + 2 * step_rows
    first, stride = cols[0], (cols[1] - cols[0]) if len(cols) > 1 else 1

    def body(x_ref, w_ref, o_ref):
        r = pl.program_id(1)

        @pl.when(r == 0)
        def _():
            o_ref[...] = jnp.zeros_like(o_ref)

        part = jnp.dot(x_ref[...], w_ref[0], preferred_element_type=F32)
        at = pl.ds(pl.multiple_of((2 - r) * step_rows, step_rows), cells)
        o_ref[0, at, :] += part

    return pl.pallas_call(
        body,
        grid=(len(cols), 3),
        in_specs=[
            pl.BlockSpec((cells, channels), lambda c, r: (0, 0)),
            pl.BlockSpec((1, channels, filters), lambda c, r: (r * 3 + first + c * stride, 0, 0)),
        ],
        out_specs=pl.BlockSpec((1, ext, filters), lambda c, r: (c, 0, 0)),
        out_shape=jax.ShapeDtypeStruct((len(cols), ext, filters), F32),
        compiler_params=pltpu.CompilerParams(vmem_limit_bytes=48 * 1024 * 1024),
    )(flat, weight)


def grad_input(dcols, weight, cells, step_rows):
    channels, filters = weight.shape[1:]
    block = 512

    def body(d_ref, w_ref, o_ref):
        acc = None
        for r in range(3):
            for c in range(3):
                win = d_ref[2 - c, (2 - r) * step_rows : (2 - r) * step_rows + cells, :]
                part = lax.dot_general(
                    win, w_ref[r * 3 + c], (((1,), (1,)), ((), ())), preferred_element_type=F32
                )
                acc = part if acc is None else acc + part
        o_ref[...] = acc.astype(BF)

    return pl.pallas_call(
        body,
        grid=(channels // block,),
        in_specs=[
            pl.BlockSpec(dcols.shape, lambda n: (0, 0, 0)),
            pl.BlockSpec((9, block, filters), lambda n: (0, n, 0)),
        ],
        out_specs=pl.BlockSpec((cells, block), lambda n: (0, n)),
        out_shape=jax.ShapeDtypeStruct((cells, channels), BF),
        compiler_params=pltpu.CompilerParams(vmem_limit_bytes=48 * 1024 * 1024),
    )(dcols, weight)


def head(preact, labels, head_weight):
    hidden = jnp.maximum(preact, 0.0).astype(BF).astype(F32)
    logits = jnp.dot(hidden, head_weight.T, precision=lax.Precision.HIGHEST)
    classes = head_weight.shape[0]
    one_hot = (labels[:, None] == jnp.arange(classes, dtype=jnp.int32)[None, :]).astype(F32)
    exponent = jnp.exp(logits)
    partition = jnp.sum(exponent, 1, keepdims=True)
    grad_logits = exponent / partition - one_hot
    d_hidden = jnp.dot(grad_logits, head_weight, precision=lax.Precision.HIGHEST)
    d_preact = jnp.where(preact > 0, d_hidden, 0.0)
    return hidden, logits, one_hot, partition, grad_logits, d_preact


def shards(features, atrous_weight, norm_gain, norm_bias, head_weight, labels):
    height, breadth, channels = features.shape
    filters = atrous_weight.shape[3]
    classes = head_weight.shape[0]
    lats, lons = lax.axis_size("lat"), lax.axis_size("lon")
    lat = lax.axis_index("lat")
    core = lax.axis_index("lon") % 2
    cells = height * breadth
    total_cells = cells * lats * lons
    step_rows = RATE * breadth
    ext_rows = height + 2 * RATE
    weight = atrous_weight.reshape(9, channels, filters)
    flat = features.reshape(cells, channels)

    half = channels // (2 * lats)
    by_half = flat.reshape(cells, lats, 2, half)
    mine = lax.dynamic_index_in_dim(by_half, core, 2, False).reshape(cells, lats * half)
    other = lax.dynamic_index_in_dim(by_half, 1 - core, 2, False).reshape(cells, lats * half)
    theirs = core_swap(other)

    lab_w = ring(labels[:, breadth - RATE :], "lon", 1, True)
    lab_e = ring(labels[:, :RATE], "lon", -1, True)
    lab_row = jnp.concatenate([lab_w, labels, lab_e], 1)
    lab_n = ring(lab_row[height - RATE :], "lat", 1, False)
    lab_s = ring(lab_row[:RATE], "lat", -1, False)

    sides = taps_forward(flat, weight, (0, 2), height, breadth).reshape(2, ext_rows, breadth, filters)
    from_w = ring(sides[0, :, RATE:], "lon", 1, True)
    from_e = ring(sides[1, :, :RATE], "lon", -1, True)
    centre = taps_forward(flat, weight, (1,), height, breadth).reshape(ext_rows, breadth, filters)
    centre = centre + jnp.concatenate([sides[1, :, RATE:] + from_w, sides[0, :, :RATE] + from_e], 1)
    from_n = ring(centre[height + RATE :], "lat", 1, False)
    from_s = ring(centre[:RATE], "lat", -1, False)
    zero = jnp.zeros((height - RATE, breadth, filters), F32)
    summed = (
        centre[RATE : RATE + height]
        + jnp.concatenate([from_n, zero], 0)
        + jnp.concatenate([zero, from_s], 0)
    ).reshape(cells, filters)

    moments = total(jnp.stack([jnp.sum(summed, 0), jnp.sum(summed * summed, 0)]).reshape(-1, 128))
    moments = moments.reshape(2, filters)
    average = moments[0] / total_cells
    variance = moments[1] / total_cells - average * average
    inverse = lax.rsqrt(variance + epsilon)
    normed = (summed - average) * inverse
    preact = norm_gain * normed + norm_bias

    pre_low = preact.astype(BF).reshape(height, breadth, filters)
    pre_n = ring(pre_low[height - RATE :], "lat", 1, False)
    pre_s = ring(pre_low[:RATE], "lat", -1, False)
    pre_col = jnp.concatenate([pre_n, pre_low, pre_s], 0)
    pre_w = ring(pre_col[:, breadth - RATE :], "lon", 1, True)
    pre_e = ring(pre_col[:, :RATE], "lon", -1, True)

    hidden, logits, one_hot, partition, grad_logits, d_preact = head(preact, labels.reshape(-1), head_weight)
    loss_terms = jnp.sum(jnp.log(partition)[:, 0] - jnp.sum(logits * one_hot, 1))
    head_term = jnp.dot(grad_logits.T, hidden, precision=lax.Precision.HIGHEST)
    payload = jnp.concatenate(
        [
            jnp.sum(d_preact, 0)[None],
            jnp.sum(d_preact * normed, 0)[None],
            head_term,
            jnp.broadcast_to(loss_terms, (1, filters)),
        ],
        0,
    )
    totals = total(payload.reshape(-1, 128)).reshape(classes + 3, filters) / total_cells
    grad_bias, grad_gain, grad_head = totals[0], totals[1], totals[2 : 2 + classes]
    mean_loss = totals[2 + classes, 0]

    scale = norm_gain * inverse
    d_own = (scale * (d_preact - grad_bias - normed * grad_gain)).astype(BF)
    d_own = d_own.reshape(height, breadth, filters)

    def halo(pre, lab):
        shape = pre.shape
        wide = pre.reshape(-1, filters).astype(F32)
        d_pre = head(wide, lab.reshape(-1), head_weight)[-1]
        norm = (wide - norm_bias) / norm_gain
        return (scale * (d_pre - grad_bias - norm * grad_gain)).astype(BF).reshape(shape)

    has_n, has_s = lat > 0, lat < lats - 1
    side = RATE
    d_n = jnp.where(has_n, halo(pre_n, lab_n[:, side : side + breadth]), 0)
    d_s = jnp.where(has_s, halo(pre_s, lab_s[:, side : side + breadth]), 0)
    row = jnp.arange(ext_rows)[:, None, None]
    inside = ((row >= RATE) | has_n) & ((row < height + RATE) | has_s)
    lab_cols = jnp.concatenate([lab_n, lab_row, lab_s], 0)
    d_w = jnp.where(inside, halo(pre_w, lab_cols[:, :side]), 0)
    d_e = jnp.where(inside, halo(pre_e, lab_cols[:, side + breadth :]), 0)
    d_pad = jnp.concatenate([d_w, jnp.concatenate([d_n, d_own, d_s], 0), d_e], 1)
    d_pair = core_swap(d_pad)

    def columns(pad):
        parts = [pad[:, c * RATE : c * RATE + breadth].reshape(-1, filters) for c in range(3)]
        return jnp.stack(parts, 0)

    d_cols = columns(d_pad)
    d_cols_pair = columns(d_pair)

    def windows(cols):
        return jnp.stack(
            [
                cols[2 - c, (2 - r) * step_rows : (2 - r) * step_rows + cells]
                for r in range(3)
                for c in range(3)
            ],
            0,
        )

    shifted = jnp.concatenate([windows(d_cols), windows(d_cols_pair)], 1)
    pair_in = jnp.concatenate([mine, theirs], 0)
    partial = jnp.einsum("tqf,qc->tfc", shifted, pair_in, preferred_element_type=F32).astype(BF)
    own_f = filters // lons
    blocks = partial.reshape(9, lons, own_f, lats, half)
    blocks = jnp.transpose(blocks, (3, 1, 0, 2, 4)).reshape(lats * lons, 9, own_f, half)
    got = lax.all_to_all(blocks, ("lat", "lon"), 0, 0)
    got = got.reshape(lats * lons // 2, 2, 9, own_f, half)
    weight_block = jnp.sum(got.astype(F32), 0) / total_cells
    grad_weight = jnp.transpose(weight_block, (0, 3, 1, 2)).reshape(2 * half, 3, 3, own_f)

    grad_features = grad_input(d_cols, weight, cells, step_rows).reshape(height, breadth, channels)
    return (mean_loss, grad_features, grad_weight, grad_gain, grad_bias, grad_head)


def solution(mesh):
    return jax.shard_map(
        shards,
        mesh=mesh,
        in_specs=(P("lat", "lon", None), P(), P(), P(), P(), P("lat", "lon")),
        out_specs=(P(), P("lat", "lon", None), P("lat", None, None, "lon"), P(), P(), P()),
        check_vma=False,
    )
```

time: 574 us -> 243 us (0.42); the launches traced: 566 us -> 242 us
  waiting for transfers between devices: 259 us -> 68 us
  blocking collectives: 137 us -> 0 us
  matrix products: 88.1 us -> 20.6 us
  starting transfers between devices: 19.7 us -> 61.3 us
  local copies, waits for them, and re-layouts: 19.1 us -> 54.9 us
  Pallas kernels: 0 us -> 23.2 us
  between operations: 16.9 us -> 1.46 us
  other arithmetic: 26.4 us -> 13 us
    psum x2 -> x0, blocking collectives: 137 us -> none  [the longest x1 74.2 us: shards(): lax.psum((jnp.sum(summed, 0), jnp.sum(summed * summed, 0)), ('lat', 'lon'))]
    reduce_scatter x2 -> x0, waiting for transfers between devices: 124 us -> none  [the longest x1 72.8 us: shards(): lax.psum_scatter(jnp.einsum('tqf,qc->ftc', shifted_all, flat_input, prefe...]
    ppermute x8 -> x14, waiting for transfers between devices: 134 us -> 20.6 us  [the longest x12 18.1 us: ring(): return lax.ppermute(x, axis, pairs)]
    dot_general x22 -> x12, matrix products: 88.1 us -> 20.6 us  [the longest x1 9.23 us: shards(): jnp.einsum('tqf,qc->tfc', shifted, pair_in, preferred_element_type=F32)]
    all_to_all x0 -> x3, waiting for transfers between devices: none -> 47.4 us  [the longest x1 47.4 us: shards(): got = lax.all_to_all(blocks, ('lat', 'lon'), 0, 0)]
    all_to_all x0 -> x3, starting transfers between devices: none -> 28 us  [the longest x2 19.3 us: total(): return jnp.sum(lax.all_to_all(spread, ('lat', 'lon'), 0, 0), 0)]
    pallas_call x0 -> x3, Pallas kernels: none -> 23.2 us  [the longest x2 12.5 us: taps_forward(): pl.pallas_call(body, grid=(len(cols), 3), in_specs=[pl.BlockSpec((cells,...]
    dynamic_slice x0 -> x1, local copies, waits for them, and re-layouts: none -> 20 us  [shards(): lax.dynamic_index_in_dim(by_half, core, 2, False)]
  transfers between devices with their start and end apart: 10 -> 17, of which waited for: 8 -> 7; matrix products, arithmetic and copies ran while one was open for 11% -> 26% of each run, Pallas kernels for 0% -> 6%
where the time goes in v1:
time: 243 us; the launch traced here: 242 us
  waiting for transfers between devices  68 us (28%)
  starting transfers between devices  61.3 us (25%)
  local copies, waits for them, and re-layouts  54.9 us (23%)
  Pallas kernels  23.2 us (10%)
  matrix products  20.6 us (8%)
  other arithmetic  13 us (5%)
    all_to_all x1, waiting for transfers between devices, shards(): got = lax.all_to_all(blocks, ('lat', 'lon'), 0, 0)  47.4 us
    ppermute x12, starting transfers between devices, ring(): return lax.ppermute(x, axis, pairs)  26.2 us
    dynamic_slice x1, local copies, waits for them, and re-layouts, shards(): lax.dynamic_index_in_dim(by_half, core, 2, False)  20 us
    all_to_all x2, starting transfers between devices, total(): return jnp.sum(lax.all_to_all(spread, ('lat', 'lon'), 0, 0), 0)  19.3 us
    ppermute x12, waiting for transfers between devices, ring(): return lax.ppermute(x, axis, pairs)  18.1 us
    unnamed x84, local copies, waits for them, and re-layouts  13.2 us
    pallas_call x2, Pallas kernels, taps_forward(): pl.pallas_call(body, grid=(len(cols), 3), in_specs=[pl.BlockSpec((cells,...  12.5 us
    pallas_call x1, Pallas kernels, grad_input(): pl.pallas_call(body, grid=(channels // block,), in_specs=[pl.BlockSpec(dc...  10.7 us
  transfers between devices with their start and end apart: 17, of which 7 were waited for; matrix products, arithmetic and copies ran while one was open for 26% of the time, Pallas kernels for 6%

profile of v1, /device:TPU:1, one launch (start us, length us, event | category | flops | bytes accessed | tf_op | source)
XLA Modules:
  0.0 242.4 jit_solution(13365010965558048405)
XLA Ops:
  0.7 1.9 copy-done.2
  2.5 8.0 %shard_map.110 = f32[2,1344,256]{2,1,0:T(8,128)S(1)} custom-call(bf16[768,2048]{1,0:T(8,128)(2,1)S(1)} %bitcast.103, bf16[9,2048,256]{2,1,0:T(8,128)(2,1)} %bitcast.107), custom_call_target="tpu_custom_call" | custom-call | tf_op jit(solution)/shard_map/pallas_call | solution.py:51
  13.3 2.7 %collective-permute-start = (f32[56,12,256]{2,0,1:T(8,128)}, f32[56,12,256]{2,0,1:T(8,128)}, u32[]{:S(2)}, u32[]{:S(2)}) collective-permute-start(f32[56,12,256]{2,0,1:T(8,128)} %bitcast.102), channel_id=1, source_target_pairs={{0,1},{1,2},{2,3},{3,4},{4,5},{5,6},{6,7},{7,8},{8,9},{9,10},{10,1... | collective-permute-start | bytes 2064392 | tf_op jit(solution)/shard_map/ppermute | solution.py:19
  21.1 4.6 %shard_map.109 = f32[1,1344,256]{2,1,0:T(8,128)S(1)} custom-call(bf16[768,2048]{1,0:T(8,128)(2,1)S(1)} %bitcast.104, bf16[9,2048,256]{2,1,0:T(8,128)(2,1)} %bitcast.108), custom_call_target="tpu_custom_call" | custom-call | tf_op jit(solution)/shard_map/pallas_call | solution.py:51
  26.8 3.8 %reshape_reshape.3 = bf16[768,8,2,128]{3,2,1,0:T(2,128)(2,1)} reshape(bf16[32,24,2048]{2,1,0:T(8,128)(2,1)S(1)} %copy-done.3) | data formatting | bytes 6291456 | tf_op jit(solution)/shard_map/reshape;reshape | solution.py:120
  30.6 1.9 fusion.12
  36.0 5.0 %collective-permute-start.2 = (f32[12,24,256]{2,0,1:T(8,128)S(1)}, f32[12,24,256]{2,0,1:T(8,128)S(1)}, u32[]{:S(2)}, u32[]{:S(2)}) collective-permute-start(f32[12,24,256]{2,0,1:T(8,128)S(1)} %get-tuple-element.26), channel_id=1, source_target_pairs={{0,16},{16,32},{32,48},{48,64},{64,80},{80,96},{96,112},{1,17},{17... | collective-permute-start | bytes 884744 | tf_op jit(solution)/shard_map/ppermute | solution.py:19
  42.3 20.0 %dynamic-slice_reduce_fusion.1 = (bf16[768,8,128]{2,1,0:T(8,128)(2,1)}, bf16[768,8,128]{2,1,0:T(8,128)(2,1)S(1)}) fusion(bf16[768,8,2,128]{3,2,1,0:T(2,128)(2,1)S(1)} %copy-done.6, s32[]{:T(128)S(6)} %select_n.73, s32[]{:T(128)S(6)} %select_n.74), kind=kLoop, calls=%fused_computation.9 | loop fusion | bytes 6291464 | tf_op jit(solution)/shard_map/jit(dynamic_index_in_dim)/dynamic_slice | solution.py:121
  63.8 2.8 %collective-permute-start.13 = (bf16[768,1024]{1,0:T(8,128)(2,1)}, bf16[768,1024]{1,0:T(8,128)(2,1)}, u32[]{:S(2)}, u32[]{:S(2)}) collective-permute-start(bf16[768,1024]{1,0:T(8,128)(2,1)} %bitcast.99), channel_id=1, source_target_pairs={{0,1},{1,0},{2,3},{3,2},{4,5},{5,4},{6,7},{7,6},{8,9},{9,8},{10,11... | collective-permute-start | bytes 4718600 | tf_op jit(solution)/shard_map/ppermute | solution.py:24
  68.4 8.8 %all-to-all-start = ((f32[128,4,128]{2,1,0:T(4,128)}), f32[128,4,128]{2,1,0:T(4,128)S(1)}, u32[]{:S(2)}, u32[]{:S(2)}) async-start(f32[128,4,128]{2,1,0:T(4,128)} %broadcast_in_dim.40), calls=%async_computation | async-start | bytes 524288 | tf_op jit(solution)/shard_map/all_to_all | solution.py:30
  77.3 4.8 %collective-permute-start.9 = (s32[12,48]{0,1:T(8,128)S(1)}, s32[12,48]{0,1:T(8,128)S(1)}, u32[]{:S(2)}, u32[]{:S(2)}) collective-permute-start(s32[12,48]{0,1:T(8,128)S(1)} %get-tuple-element.37), channel_id=1, source_target_pairs={{0,16},{16,32},{32,48},{48,64},{64,80},{80,96},{96,112},{1,17},{17... | collective-permute-start | bytes 6920 | tf_op jit(solution)/shard_map/ppermute | solution.py:19
  84.1 3.0 %copy.161 = bf16[96,8,8,128]{3,1,2,0:T(8,128)(2,1)} copy(bf16[96,8,8,128]{3,2,1,0:T(8,128)(2,1)} %bitcast.124) | data formatting | bytes 3145728
  97.5 10.5 %all-to-all-start.1 = ((f32[128,12,128]{2,1,0:T(8,128)}), f32[128,12,128]{2,1,0:T(8,128)S(1)}, u32[]{:S(2)}, u32[]{:S(2)}) async-start(f32[128,12,128]{2,1,0:T(8,128)} %broadcast_in_dim.49), calls=%async_computation.1 | async-start | bytes 2097152 | tf_op jit(solution)/shard_map/all_to_all | solution.py:30
  108.0 4.8 %collective-permute-start.4 = (bf16[12,24,256]{2,1,0:T(8,128)(2,1)S(1)}, bf16[12,24,256]{2,1,0:T(8,128)(2,1)S(1)}, u32[]{:S(2)}, u32[]{:S(2)}) collective-permute-start(bf16[12,24,256]{2,1,0:T(8,128)(2,1)S(1)} %bitcast.147), channel_id=1, source_target_pairs={{0,16},{16,32},{32,48},{48,64},{64,80},{80,96},{96,112},{1,17},{17... | collective-permute-start | bytes 442376 | tf_op jit(solution)/shard_map/ppermute | solution.py:19
  114.3 11.4 %collective-permute-done.4 = bf16[12,24,256]{2,1,0:T(8,128)(2,1)S(1)} collective-permute-done((bf16[12,24,256]{2,1,0:T(8,128)(2,1)S(1)}, bf16[12,24,256]{2,1,0:T(8,128)(2,1)S(1)}, u32[]{:S(2)}, u32[]{:S(2)}) %collective-permute-start.4) | collective-permute-done | bytes 147488 | tf_op jit(solution)/shard_map/ppermute | solution.py:19
  131.8 4.8 %collective-permute-done.11 = bf16[56,12,256]{2,0,1:T(8,128)(2,1)S(1)} collective-permute-done((bf16[56,12,256]{2,0,1:T(8,128)(2,1)S(1)}, bf16[56,12,256]{2,0,1:T(8,128)(2,1)S(1)}, u32[]{:S(2)}, u32[]{:S(2)}) %collective-permute-start.11) | collective-permute-done | bytes 344096 | tf_op jit(solution)/shard_map/ppermute | solution.py:19
  148.0 4.3 %collective-permute-start.12 = (bf16[56,48,256]{2,1,0:T(8,128)(2,1)S(1)}, bf16[56,48,256]{2,1,0:T(8,128)(2,1)S(1)}, u32[]{:S(2)}, u32[]{:S(2)}) collective-permute-start(bf16[56,48,256]{2,1,0:T(8,128)(2,1)S(1)} %pad_maximum_fusion.1), channel_id=1, source_target_pairs={{0,1},{1,0},{2,3},{3,2},{4,5},{5,4},{6,7},{7,6},{8,9},{9,8},{10,11... | collective-permute-start | bytes 4128776 | tf_op jit(solution)/shard_map/ppermute | solution.py:24
  152.5 2.5 %collective-permute-done.12 = bf16[56,48,256]{2,1,0:T(8,128)(2,1)S(1)} collective-permute-done((bf16[56,48,256]{2,1,0:T(8,128)(2,1)S(1)}, bf16[56,48,256]{2,1,0:T(8,128)(2,1)S(1)}, u32[]{:S(2)}, u32[]{:S(2)}) %collective-permute-start.12) | collective-permute-done | bytes 1376288 | tf_op jit(solution)/shard_map/ppermute | solution.py:24
  156.8 9.2 %fusion.6 = bf16[9,256,1024]{2,1,0:T(8,128)(2,1)S(1)} fusion(bf16[768,1024]{1,0:T(8,128)(2,1)} %collective-permute-done.13, bf16[768,1024]{1,0:T(8,128)(2,1)S(1)} %bitcast.139, bf16[9,768,256]{2,1,0:T(8,128)(2,1)S(1)} %get-tuple-element.55, bf16[9,768,256]{2,1,0:T(8,128)(2,1)S(1)} %get-tuple-element.56), kind=kOutput, calls=%fused_computation.10 | convolution fusion | flops 7270563840 | bytes 14942208 | tf_op jit(solution)/shard_map/tqf,qc->tfc/dot_general | solution.py:218
  167.3 3.0 %copy.133 = bf16[9,16,16,8,128]{4,2,0,1,3:T(8,128)(2,1)} copy(bf16[9,16,16,8,128]{4,3,2,1,0:T(8,128)(2,1)S(1)} %bitcast.111) | data formatting | bytes 9437184 | tf_op jit(solution)/shard_map/reshape | solution.py:220
  170.3 8.7 %all-to-all-start.2 = ((bf16[128,9,16,128]{3,2,1,0:T(8,128)(2,1)}), bf16[128,9,16,128]{3,2,1,0:T(8,128)(2,1)}, u32[]{:S(2)}, u32[]{:S(2)}) async-start(bf16[128,9,16,128]{3,2,1,0:T(8,128)(2,1)} %bitcast.110), calls=%async_computation.2 | async-start | bytes 9437184 | tf_op jit(solution)/shard_map/all_to_all | solution.py:222
  179.3 10.7 %shard_map.111 = bf16[768,2048]{1,0:T(8,128)(2,1)} custom-call(bf16[3,1344,256]{2,1,0:T(8,128)(2,1)S(1)} %pad_maximum_fusion.d_ref, bf16[9,2048,256]{2,1,0:T(8,128)(2,1)} %bitcast.109), custom_call_target="tpu_custom_call" | custom-call | tf_op jit(solution)/shard_map/pallas_call | solution.py:79
  191.1 47.4 %all-to-all-done.2 = bf16[128,9,16,128]{3,2,1,0:T(8,128)(2,1)} async-done(((bf16[128,9,16,128]{3,2,1,0:T(8,128)(2,1)}), bf16[128,9,16,128]{3,2,1,0:T(8,128)(2,1)}, u32[]{:S(2)}, u32[]{:S(2)}) %all-to-all-start.2) | async-done | bytes 4718624 | tf_op jit(solution)/shard_map/all_to_all | solution.py:222
  238.5 3.0 %convert_reduce_fusion = f32[2,9,16,128]{3,2,1,0:T(8,128)S(1)} fusion(bf16[64,2,9,16,128]{4,3,2,1,0:T(8,128)(2,1)} %bitcast.40), kind=kLoop, calls=%fused_computation | loop fusion | flops 4681728 | bytes 4866048 | tf_op jit(solution)/shard_map/reduce_sum | solution.py:224
  (177 shorter events, 53.5 us)
Async XLA Ops:
  0.6 91.7 %copy-start = (f32[3,256]{1,0:T(4,128)S(1)}, f32[3,256]{1,0:T(4,128)}, u32[]{:S(2)}) copy-start(f32[3,256]{1,0:T(4,128)} %param.10) | copy-start | bytes 9220
  13.3 17.4 %collective-permute-start = (f32[56,12,256]{2,0,1:T(8,128)}, f32[56,12,256]{2,0,1:T(8,128)}, u32[]{:S(2)}, u32[]{:S(2)}) collective-permute-start(f32[56,12,256]{2,0,1:T(8,128)} %bitcast.102), channel_id=1, source_target_pairs={{0,1},{1,2},{2,3},{3,4},{4,5},{5,6},{6,7},{7,8},{8,9},{9,10},{10,1... | collective-permute-start | bytes 2064392 | tf_op jit(solution)/shard_map/ppermute | solution.py:19
  17.2 16.4 %collective-permute-start.1 = (f32[56,12,256]{2,0,1:T(8,128)}, f32[56,12,256]{2,0,1:T(8,128)}, u32[]{:S(2)}, u32[]{:S(2)}) collective-permute-start(f32[56,12,256]{2,0,1:T(8,128)} %bitcast.101), channel_id=1, source_target_pairs={{0,15},{1,0},{2,1},{3,2},{4,3},{5,4},{6,5},{7,6},{8,7},{9,8},{10,9... | collective-permute-start | bytes 2064392 | tf_op jit(solution)/shard_map/ppermute | solution.py:19
  17.8 48.9 %collective-permute-start.7 = (s32[32,12]{0,1:T(8,128)}, s32[32,12]{0,1:T(8,128)}, u32[]{:S(2)}, u32[]{:S(2)}) collective-permute-start(s32[32,12]{0,1:T(8,128)} %get-tuple-element.39), channel_id=1, source_target_pairs={{0,1},{1,2},{2,3},{3,4},{4,5},{5,6},{6,7},{7,8},{8,9},{9,10},{10,1... | collective-permute-start | bytes 4616 | tf_op jit(solution)/shard_map/ppermute | solution.py:19
  19.6 7.2 %copy-start.3 = (bf16[32,24,2048]{2,1,0:T(8,128)(2,1)S(1)}, bf16[32,24,2048]{2,1,0:T(8,128)(2,1)}, u32[]{:S(2)}) copy-start(bf16[32,24,2048]{2,1,0:T(8,128)(2,1)} %param.6) | copy-start | bytes 9437188
  19.6 47.1 %collective-permute-start.8 = (s32[32,12]{0,1:T(8,128)}, s32[32,12]{0,1:T(8,128)}, u32[]{:S(2)}, u32[]{:S(2)}) collective-permute-start(s32[32,12]{0,1:T(8,128)} %get-tuple-element.40), channel_id=1, source_target_pairs={{0,15},{1,0},{2,1},{3,2},{4,3},{5,4},{6,5},{7,6},{8,7},{9,8},{10,9... | collective-permute-start | bytes 4616 | tf_op jit(solution)/shard_map/ppermute | solution.py:19
  36.0 31.4 %collective-permute-start.2 = (f32[12,24,256]{2,0,1:T(8,128)S(1)}, f32[12,24,256]{2,0,1:T(8,128)S(1)}, u32[]{:S(2)}, u32[]{:S(2)}) collective-permute-start(f32[12,24,256]{2,0,1:T(8,128)S(1)} %get-tuple-element.26), channel_id=1, source_target_pairs={{0,16},{16,32},{32,48},{48,64},{64,80},{80,96},{96,112},{1,17},{17... | collective-permute-start | bytes 884744 | tf_op jit(solution)/shard_map/ppermute | solution.py:19
  41.0 26.4 %collective-permute-start.3 = (f32[12,24,256]{2,0,1:T(8,128)S(1)}, f32[12,24,256]{2,0,1:T(8,128)S(1)}, u32[]{:S(2)}, u32[]{:S(2)}) collective-permute-start(f32[12,24,256]{2,0,1:T(8,128)S(1)} %get-tuple-element.27), channel_id=1, source_target_pairs={{16,0},{32,16},{48,32},{64,48},{80,64},{96,80},{112,96},{17,1},{33... | collective-permute-start | bytes 884744 | tf_op jit(solution)/shard_map/ppermute | solution.py:19
  63.8 91.9 %collective-permute-start.13 = (bf16[768,1024]{1,0:T(8,128)(2,1)}, bf16[768,1024]{1,0:T(8,128)(2,1)}, u32[]{:S(2)}, u32[]{:S(2)}) collective-permute-start(bf16[768,1024]{1,0:T(8,128)(2,1)} %bitcast.99), channel_id=1, source_target_pairs={{0,1},{1,0},{2,3},{3,2},{4,5},{5,4},{6,7},{7,6},{8,9},{9,8},{10,11... | collective-permute-start | bytes 4718600 | tf_op jit(solution)/shard_map/ppermute | solution.py:24
  67.6 24.5 %copy-start.16 = (f32[256]{0:T(256)S(1)}, f32[256]{0:T(256)}, u32[]{:S(2)}) copy-start(f32[256]{0:T(256)} %param.8) | copy-start | bytes 3076
  67.7 24.5 %copy-start.18 = (f32[256]{0:T(256)S(1)}, f32[256]{0:T(256)}, u32[]{:S(2)}) copy-start(f32[256]{0:T(256)} %param.9) | copy-start | bytes 3076
  68.4 23.6 %all-to-all-start = ((f32[128,4,128]{2,1,0:T(4,128)}), f32[128,4,128]{2,1,0:T(4,128)S(1)}, u32[]{:S(2)}, u32[]{:S(2)}) async-start(f32[128,4,128]{2,1,0:T(4,128)} %broadcast_in_dim.40), calls=%async_computation | async-start | bytes 524288 | tf_op jit(solution)/shard_map/all_to_all | solution.py:30
  77.3 9.9 %collective-permute-start.9 = (s32[12,48]{0,1:T(8,128)S(1)}, s32[12,48]{0,1:T(8,128)S(1)}, u32[]{:S(2)}, u32[]{:S(2)}) collective-permute-start(s32[12,48]{0,1:T(8,128)S(1)} %get-tuple-element.37), channel_id=1, source_target_pairs={{0,16},{16,32},{32,48},{48,64},{64,80},{80,96},{96,112},{1,17},{17... | collective-permute-start | bytes 6920 | tf_op jit(solution)/shard_map/ppermute | solution.py:19
  82.1 6.4 %collective-permute-start.10 = (s32[12,48]{0,1:T(8,128)S(1)}, s32[12,48]{0,1:T(8,128)S(1)}, u32[]{:S(2)}, u32[]{:S(2)}) collective-permute-start(s32[12,48]{0,1:T(8,128)S(1)} %get-tuple-element.38), channel_id=1, source_target_pairs={{16,0},{32,16},{48,32},{64,48},{80,64},{96,80},{112,96},{17,1},{33... | collective-permute-start | bytes 6920 | tf_op jit(solution)/shard_map/ppermute | solution.py:19
  97.5 45.3 %all-to-all-start.1 = ((f32[128,12,128]{2,1,0:T(8,128)}), f32[128,12,128]{2,1,0:T(8,128)S(1)}, u32[]{:S(2)}, u32[]{:S(2)}) async-start(f32[128,12,128]{2,1,0:T(8,128)} %broadcast_in_dim.49), calls=%async_computation.1 | async-start | bytes 2097152 | tf_op jit(solution)/shard_map/all_to_all | solution.py:30
  108.0 17.6 %collective-permute-start.4 = (bf16[12,24,256]{2,1,0:T(8,128)(2,1)S(1)}, bf16[12,24,256]{2,1,0:T(8,128)(2,1)S(1)}, u32[]{:S(2)}, u32[]{:S(2)}) collective-permute-start(bf16[12,24,256]{2,1,0:T(8,128)(2,1)S(1)} %bitcast.147), channel_id=1, source_target_pairs={{0,16},{16,32},{32,48},{48,64},{64,80},{80,96},{96,112},{1,17},{17... | collective-permute-start | bytes 442376 | tf_op jit(solution)/shard_map/ppermute | solution.py:19
  112.8 13.2 %collective-permute-start.5 = (bf16[12,24,256]{2,1,0:T(8,128)(2,1)S(1)}, bf16[12,24,256]{2,1,0:T(8,128)(2,1)S(1)}, u32[]{:S(2)}, u32[]{:S(2)}) collective-permute-start(bf16[12,24,256]{2,1,0:T(8,128)(2,1)S(1)} %bitcast.146), channel_id=1, source_target_pairs={{16,0},{32,16},{48,32},{64,48},{80,64},{96,80},{112,96},{17,1},{33... | collective-permute-start | bytes 442376 | tf_op jit(solution)/shard_map/ppermute | solution.py:19
  125.6 11.0 %copy-start.13 = (bf16[12,24,256]{2,1,0:T(8,128)(2,1)}, bf16[12,24,256]{2,1,0:T(8,128)(2,1)S(1)}, u32[]{:S(2)}) copy-start(bf16[12,24,256]{2,1,0:T(8,128)(2,1)S(1)} %collective-permute-done.4) | copy-start | bytes 442372
  126.0 10.5 %copy-start.11 = (bf16[12,24,256]{2,1,0:T(8,128)(2,1)}, bf16[12,24,256]{2,1,0:T(8,128)(2,1)S(1)}, u32[]{:S(2)}) copy-start(bf16[12,24,256]{2,1,0:T(8,128)(2,1)S(1)} %collective-permute-done.5) | copy-start | bytes 442372
  127.2 9.4 %collective-permute-start.11 = (bf16[56,12,256]{2,0,1:T(8,128)(2,1)S(1)}, bf16[56,12,256]{2,0,1:T(8,128)(2,1)S(1)}, u32[]{:S(2)}, u32[]{:S(2)}) collective-permute-start(bf16[56,12,256]{2,0,1:T(8,128)(2,1)S(1)} %get-tuple-element.32), channel_id=1, source_target_pairs={{0,15},{1,0},{2,1},{3,2},{4,3},{5,4},{6,5},{7,6},{8,7},{9,8},{10,9... | collective-permute-start | bytes 1032200 | tf_op jit(solution)/shard_map/ppermute | solution.py:19
  128.0 9.7 %collective-permute-start.6 = (bf16[56,12,256]{2,0,1:T(8,128)(2,1)}, bf16[56,12,256]{2,0,1:T(8,128)(2,1)}, u32[]{:S(2)}, u32[]{:S(2)}) collective-permute-start(bf16[56,12,256]{2,0,1:T(8,128)(2,1)} %get-tuple-element.31), channel_id=1, source_target_pairs={{0,1},{1,2},{2,3},{3,4},{4,5},{5,6},{6,7},{7,8},{8,9},{9,10},{10,1... | collective-permute-start | bytes 1032200 | tf_op jit(solution)/shard_map/ppermute | solution.py:19
  148.0 7.0 %collective-permute-start.12 = (bf16[56,48,256]{2,1,0:T(8,128)(2,1)S(1)}, bf16[56,48,256]{2,1,0:T(8,128)(2,1)S(1)}, u32[]{:S(2)}, u32[]{:S(2)}) collective-permute-start(bf16[56,48,256]{2,1,0:T(8,128)(2,1)S(1)} %pad_maximum_fusion.1), channel_id=1, source_target_pairs={{0,1},{1,0},{2,3},{3,2},{4,5},{5,4},{6,7},{7,6},{8,9},{9,8},{10,11... | collective-permute-start | bytes 4128776 | tf_op jit(solution)/shard_map/ppermute | solution.py:24
  170.3 68.2 %all-to-all-start.2 = ((bf16[128,9,16,128]{3,2,1,0:T(8,128)(2,1)}), bf16[128,9,16,128]{3,2,1,0:T(8,128)(2,1)}, u32[]{:S(2)}, u32[]{:S(2)}) async-start(bf16[128,9,16,128]{3,2,1,0:T(8,128)(2,1)} %bitcast.110), calls=%async_computation.2 | async-start | bytes 9437184 | tf_op jit(solution)/shard_map/all_to_all | solution.py:222
  179.2 63.1 %copy-start.1 = (f32[3,256]{1,0:T(4,128)S(1)}, f32[3,256]{1,0:T(4,128)}, u32[]{:S(2)}) copy-start(f32[3,256]{1,0:T(4,128)} %param.10) | copy-start | bytes 9220
  (24 other events, 61.3 us)

commit v2 on v1

--- a/solution.py
+++ b/solution.py
@@ -30,35 +30,93 @@
     return jnp.sum(lax.all_to_all(spread, ("lat", "lon"), 0, 0), 0)
 
 
-def taps_forward(flat, weight, cols, height, breadth):
+def outer_rows(flat, weight, edge):
     cells, channels = flat.shape
     filters = weight.shape[2]
-    step_rows = RATE * breadth
-    ext = cells + 2 * step_rows
+
+    def body(x_ref, w_ref, o_ref):
+        at = pl.ds(pl.multiple_of(pl.program_id(0) * (cells - edge), 16), edge)
+        o_ref[0, 0] = jnp.dot(x_ref[at, :], w_ref[0], preferred_element_type=F32)
+
+    return pl.pallas_call(
+        body,
+        grid=(2, 3),
+        in_specs=[
+            pl.BlockSpec((cells, channels), lambda e, c: (0, 0)),
+            pl.BlockSpec((1, channels, filters), lambda e, c: ((1 - e) * 6 + c, 0, 0)),
+        ],
+        out_specs=pl.BlockSpec((1, 1, edge, filters), lambda e, c: (e, c, 0, 0)),
+        out_shape=jax.ShapeDtypeStruct((2, 3, edge, filters), F32),
+        compiler_params=pltpu.CompilerParams(vmem_limit_bytes=48 * 1024 * 1024),
+    )(flat, weight)
+
+
+def inner_rows(flat, weight, edge, cols):
+    cells, channels = flat.shape
+    filters = weight.shape[2]
     first, stride = cols[0], (cols[1] - cols[0]) if len(cols) > 1 else 1
 
     def body(x_ref, w_ref, o_ref):
-        r = pl.program_id(1)
-
-        @pl.when(r == 0)
-        def _():
-            o_ref[...] = jnp.zeros_like(o_ref)
-
-        part = jnp.dot(x_ref[...], w_ref[0], preferred_element_type=F32)
-        at = pl.ds(pl.multiple_of((2 - r) * step_rows, step_rows), cells)
-        o_ref[0, at, :] += part
+        k = pl.program_id(1)
+
+        @pl.when(k == 0)
+        def _():
+            o_ref[0] = jnp.dot(x_ref[...], w_ref[0], preferred_element_type=F32)
+
+        @pl.when(k == 1)
+        def _():
+            o_ref[0, edge:, :] += jnp.dot(x_ref[: cells - edge, :], w_ref[0], preferred_element_type=F32)
+
+        @pl.when(k == 2)
+        def _():
+            o_ref[0, : cells - edge, :] += jnp.dot(x_ref[edge:, :], w_ref[0], preferred_element_type=F32)
+
+    def tap(c, k):
+        return ((k * k * 3 - k * 5 + 2) // 2 * 3 + first + c * stride, 0, 0)
 
     return pl.pallas_call(
         body,
         grid=(len(cols), 3),
         in_specs=[
-            pl.BlockSpec((cells, channels), lambda c, r: (0, 0)),
-            pl.BlockSpec((1, channels, filters), lambda c, r: (r * 3 + first + c * stride, 0, 0)),
-        ],
-        out_specs=pl.BlockSpec((1, ext, filters), lambda c, r: (c, 0, 0)),
-        out_shape=jax.ShapeDtypeStruct((len(cols), ext, filters), F32),
+            pl.BlockSpec((cells, channels), lambda c, k: (0, 0)),
+            pl.BlockSpec((1, channels, filters), tap),
+        ],
+        out_specs=pl.BlockSpec((1, cells, filters), lambda c, k: (c, 0, 0)),
+        out_shape=jax.ShapeDtypeStruct((len(cols), cells, filters), F32),
         compiler_params=pltpu.CompilerParams(vmem_limit_bytes=48 * 1024 * 1024),
     )(flat, weight)
+
+
+def split_halves(flat, which, half):
+    cells, channels = flat.shape
+    count = channels // (2 * half)
+
+    def body(which_ref, x_ref, mine_ref, other_ref):
+        low, high = x_ref[:, :half], x_ref[:, half:]
+        first = which_ref[0] == 0
+
+        @pl.when(first)
+        def _():
+            mine_ref[...] = low
+            other_ref[...] = high
+
+        @pl.when(jnp.logical_not(first))
+        def _():
+            mine_ref[...] = high
+            other_ref[...] = low
+
+    shape = jax.ShapeDtypeStruct((cells, count * half), BF)
+    block = pl.BlockSpec((cells, half), lambda i, w: (0, i))
+    return pl.pallas_call(
+        body,
+        grid_spec=pltpu.PrefetchScalarGridSpec(
+            num_scalar_prefetch=1,
+            grid=(count,),
+            in_specs=[pl.BlockSpec((cells, 2 * half), lambda i, w: (0, i))],
+            out_specs=[block, block],
+        ),
+        out_shape=[shape, shape],
+    )(which.reshape(1).astype(jnp.int32), flat)
 
 
 def grad_input(dcols, weight, cells, step_rows):
@@ -107,39 +165,35 @@
     filters = atrous_weight.shape[3]
     classes = head_weight.shape[0]
     lats, lons = lax.axis_size("lat"), lax.axis_size("lon")
-    lat = lax.axis_index("lat")
     core = lax.axis_index("lon") % 2
     cells = height * breadth
     total_cells = cells * lats * lons
     step_rows = RATE * breadth
-    ext_rows = height + 2 * RATE
     weight = atrous_weight.reshape(9, channels, filters)
     flat = features.reshape(cells, channels)
 
+    rest = breadth - RATE
+    outer = outer_rows(flat, weight, step_rows).reshape(2, 3, RATE, breadth, filters)
+    outer_w = ring(outer[:, 0, :, RATE:], "lon", 1, True)
+    outer_e = ring(outer[:, 2, :, :rest], "lon", -1, True)
+    sides = inner_rows(flat, weight, step_rows, (0, 2)).reshape(2, height, breadth, filters)
+    inner_w = ring(sides[0, :, RATE:], "lon", 1, True)
+    inner_e = ring(sides[1, :, :rest], "lon", -1, True)
+    strips = outer[:, 1] + jnp.concatenate(
+        [outer[:, 2, :, rest:] + outer_w, outer[:, 0, :, :RATE] + outer_e], 2
+    )
+    from_s = ring(strips[0], "lat", -1, False)
+    from_n = ring(strips[1], "lat", 1, False)
+    centre = inner_rows(flat, weight, step_rows, (1,)).reshape(height, breadth, filters)
+    centre = centre + jnp.concatenate([sides[1, :, rest:] + inner_w, sides[0, :, :RATE] + inner_e], 1)
+
     half = channels // (2 * lats)
-    by_half = flat.reshape(cells, lats, 2, half)
-    mine = lax.dynamic_index_in_dim(by_half, core, 2, False).reshape(cells, lats * half)
-    other = lax.dynamic_index_in_dim(by_half, 1 - core, 2, False).reshape(cells, lats * half)
+    mine, other = split_halves(flat, core, half)
     theirs = core_swap(other)
 
-    lab_w = ring(labels[:, breadth - RATE :], "lon", 1, True)
-    lab_e = ring(labels[:, :RATE], "lon", -1, True)
-    lab_row = jnp.concatenate([lab_w, labels, lab_e], 1)
-    lab_n = ring(lab_row[height - RATE :], "lat", 1, False)
-    lab_s = ring(lab_row[:RATE], "lat", -1, False)
-
-    sides = taps_forward(flat, weight, (0, 2), height, breadth).reshape(2, ext_rows, breadth, filters)
-    from_w = ring(sides[0, :, RATE:], "lon", 1, True)
-    from_e = ring(sides[1, :, :RATE], "lon", -1, True)
-    centre = taps_forward(flat, weight, (1,), height, breadth).reshape(ext_rows, breadth, filters)
-    centre = centre + jnp.concatenate([sides[1, :, RATE:] + from_w, sides[0, :, :RATE] + from_e], 1)
-    from_n = ring(centre[height + RATE :], "lat", 1, False)
-    from_s = ring(centre[:RATE], "lat", -1, False)
     zero = jnp.zeros((height - RATE, breadth, filters), F32)
     summed = (
-        centre[RATE : RATE + height]
-        + jnp.concatenate([from_n, zero], 0)
-        + jnp.concatenate([zero, from_s], 0)
+        centre + jnp.concatenate([from_n, zero], 0) + jnp.concatenate([zero, from_s], 0)
     ).reshape(cells, filters)
 
     moments = total(jnp.stack([jnp.sum(summed, 0), jnp.sum(summed * summed, 0)]).reshape(-1, 128))
@@ -149,13 +203,6 @@
     inverse = lax.rsqrt(variance + epsilon)
     normed = (summed - average) * inverse
     preact = norm_gain * normed + norm_bias
-
-    pre_low = preact.astype(BF).reshape(height, breadth, filters)
-    pre_n = ring(pre_low[height - RATE :], "lat", 1, False)
-    pre_s = ring(pre_low[:RATE], "lat", -1, False)
-    pre_col = jnp.concatenate([pre_n, pre_low, pre_s], 0)
-    pre_w = ring(pre_col[:, breadth - RATE :], "lon", 1, True)
-    pre_e = ring(pre_col[:, :RATE], "lon", -1, True)
 
     hidden, logits, one_hot, partition, grad_logits, d_preact = head(preact, labels.reshape(-1), head_weight)
     loss_terms = jnp.sum(jnp.log(partition)[:, 0] - jnp.sum(logits * one_hot, 1))
@@ -169,7 +216,7 @@
         ],
         0,
     )
-    totals = total(payload.reshape(-1, 128)).reshape(classes + 3, filters) / total_cells
+    totals = total(payload.reshape(-1, 4, 128)).reshape(classes + 3, filters) / total_cells
     grad_bias, grad_gain, grad_head = totals[0], totals[1], totals[2 : 2 + classes]
     mean_loss = totals[2 + classes, 0]
 
@@ -177,23 +224,12 @@
     d_own = (scale * (d_preact - grad_bias - normed * grad_gain)).astype(BF)
     d_own = d_own.reshape(height, breadth, filters)
 
-    def halo(pre, lab):
-        shape = pre.shape
-        wide = pre.reshape(-1, filters).astype(F32)
-        d_pre = head(wide, lab.reshape(-1), head_weight)[-1]
-        norm = (wide - norm_bias) / norm_gain
-        return (scale * (d_pre - grad_bias - norm * grad_gain)).astype(BF).reshape(shape)
-
-    has_n, has_s = lat > 0, lat < lats - 1
-    side = RATE
-    d_n = jnp.where(has_n, halo(pre_n, lab_n[:, side : side + breadth]), 0)
-    d_s = jnp.where(has_s, halo(pre_s, lab_s[:, side : side + breadth]), 0)
-    row = jnp.arange(ext_rows)[:, None, None]
-    inside = ((row >= RATE) | has_n) & ((row < height + RATE) | has_s)
-    lab_cols = jnp.concatenate([lab_n, lab_row, lab_s], 0)
-    d_w = jnp.where(inside, halo(pre_w, lab_cols[:, :side]), 0)
-    d_e = jnp.where(inside, halo(pre_e, lab_cols[:, side + breadth :]), 0)
-    d_pad = jnp.concatenate([d_w, jnp.concatenate([d_n, d_own, d_s], 0), d_e], 1)
+    d_n = ring(d_own[height - RATE :], "lat", 1, False)
+    d_s = ring(d_own[:RATE], "lat", -1, False)
+    d_col = jnp.concatenate([d_n, d_own, d_s], 0)
+    d_w = ring(d_col[:, breadth - RATE :], "lon", 1, True)
+    d_e = ring(d_col[:, :RATE], "lon", -1, True)
+    d_pad = jnp.concatenate([d_w, d_col, d_e], 1)
     d_pair = core_swap(d_pad)
 
     def columns(pad):

time: 243 us -> 211 us (0.87)
  local copies, waits for them, and re-layouts: 54.9 us -> 12.2 us
  blocking collectives: 0 us -> 20.4 us
  starting transfers between devices: 61.3 us -> 46.9 us
  Pallas kernels: 23.2 us -> 34.5 us
  matrix products: 20.6 us -> 9.68 us
  waiting for transfers between devices: 68 us -> 77.6 us
  other arithmetic: 13 us -> 7.64 us
    all_to_all x0 -> x1, blocking collectives: none -> 20.4 us  [total(): return jnp.sum(lax.all_to_all(spread, ('lat', 'lon'), 0, 0), 0)]
    dynamic_slice x1 -> x0, local copies, waits for them, and re-layouts: 20 us -> none  [shards(): lax.dynamic_index_in_dim(by_half, core, 2, False)]
    pallas_call x2 -> x4, Pallas kernels: 12.5 us -> 23.8 us  [the longest x2 11.5 us: inner_rows(): pl.pallas_call(body, grid=(len(cols), 3), in_specs=[pl.BlockSpec((cells,...]
    all_to_all x2 -> x1, waiting for transfers between devices: 0.01 us -> 11.3 us  [total(): return jnp.sum(lax.all_to_all(spread, ('lat', 'lon'), 0, 0), 0)]
    unnamed x84 -> x40, local copies, waits for them, and re-layouts: 13.2 us -> 4.76 us
    ppermute x12 -> x10, starting transfers between devices: 26.2 us -> 18.9 us  [ring(): return lax.ppermute(x, axis, pairs)]
    dot_general x5 -> x1, matrix products: 6.42 us -> 0.47 us  [head(): logits = jnp.dot(hidden, head_weight.T, precision=lax.Precision.HIGHEST)]
    another operation x1 -> x0, local copies, waits for them, and re-layouts: 3.84 us -> none  [shards(): by_half = flat.reshape(cells, lats, 2, half)]
  transfers between devices with their start and end apart: 17 -> 14, of which waited for: 7 -> 7; matrix products, arithmetic and copies ran while one was open for 26% -> 2% of each run, Pallas kernels for 6% -> 14%
where the time goes in v2:
time: 211 us; the launch traced here: 210 us
  waiting for transfers between devices  77.6 us (37%)
  starting transfers between devices  46.9 us (22%)
  Pallas kernels  34.5 us (16%)
  blocking collectives  20.4 us (10%)
  local copies, waits for them, and re-layouts  12.2 us (6%)
  matrix products  9.68 us (5%)
  other arithmetic  7.64 us (4%)
    all_to_all x1, waiting for transfers between devices, shards(): got = lax.all_to_all(blocks, ('lat', 'lon'), 0, 0)  47.4 us
    all_to_all x1, blocking collectives, total(): return jnp.sum(lax.all_to_all(spread, ('lat', 'lon'), 0, 0), 0)  20.4 us
    ppermute x10, starting transfers between devices, ring(): return lax.ppermute(x, axis, pairs)  18.9 us
    ppermute x10, waiting for transfers between devices, ring(): return lax.ppermute(x, axis, pairs)  16.4 us
    all_to_all x1, starting transfers between devices, total(): return jnp.sum(lax.all_to_all(spread, ('lat', 'lon'), 0, 0), 0)  16 us
    pallas_call x2, Pallas kernels, inner_rows(): pl.pallas_call(body, grid=(len(cols), 3), in_specs=[pl.BlockSpec((cells,...  11.5 us
    all_to_all x1, waiting for transfers between devices, total(): return jnp.sum(lax.all_to_all(spread, ('lat', 'lon'), 0, 0), 0)  11.3 us
    pallas_call x1, Pallas kernels, grad_input(): pl.pallas_call(body, grid=(channels // block,), in_specs=[pl.BlockSpec(dc...  10.7 us
  transfers between devices with their start and end apart: 14, of which 7 were waited for; matrix products, arithmetic and copies ran while one was open for 2% of the time, Pallas kernels for 14%

profile of v2, /device:TPU:1, one launch (start us, length us, event | category | flops | bytes accessed | tf_op | source)
XLA Modules:
  0.0 210.0 jit_solution(10069445139099307146)
XLA Ops:
  0.7 1.9 copy-done.2
  2.5 5.8 %shard_map.111 = f32[2,3,288,256]{3,2,1,0:T(8,128)S(1)} custom-call(bf16[768,2048]{1,0:T(8,128)(2,1)S(1)} %bitcast.103, bf16[9,2048,256]{2,1,0:T(8,128)(2,1)} %bitcast.112), custom_call_target="tpu_custom_call" | custom-call | tf_op jit(solution)/shard_map/pallas_call | solution.py:41
  8.5 2.8 %collective-permute-start.2 = (f32[2,12,12,256]{3,2,1,0:T(8,128)S(1)}, f32[2,12,12,256]{3,2,1,0:T(8,128)S(1)}, u32[]{:S(2)}, u32[]{:S(2)}) collective-permute-start(f32[2,12,12,256]{3,2,1,0:T(8,128)S(1)} %get-tuple-element.21), channel_id=1, source_target_pairs={{0,1},{1,2},{2,3},{3,4},{4,5},{5,6},{6,7},{7,8},{8,9},{9,10},{10,1... | collective-permute-start | bytes 884744 | tf_op jit(solution)/shard_map/ppermute | solution.py:19
  11.2 7.3 %shard_map.110 = f32[2,768,256]{2,1,0:T(8,128)S(1)} custom-call(bf16[768,2048]{1,0:T(8,128)(2,1)S(1)} %bitcast.104, bf16[9,2048,256]{2,1,0:T(8,128)(2,1)} %bitcast.113), custom_call_target="tpu_custom_call" | custom-call | tf_op jit(solution)/shard_map/pallas_call | solution.py:77
  18.6 1.8 collective-permute-start
  22.5 4.8 %collective-permute-start.4 = (f32[12,24,256]{2,1,0:T(8,128)S(1)}, f32[12,24,256]{2,1,0:T(8,128)S(1)}, u32[]{:S(2)}, u32[]{:S(2)}) collective-permute-start(f32[12,24,256]{2,1,0:T(8,128)S(1)} %get-tuple-element.34), channel_id=1, source_target_pairs={{0,16},{16,32},{32,48},{48,64},{64,80},{80,96},{96,112},{1,17},{17... | collective-permute-start | bytes 884744 | tf_op jit(solution)/shard_map/ppermute | solution.py:19
  28.6 4.2 %shard_map.109 = f32[1,768,256]{2,1,0:T(8,128)S(1)} custom-call(bf16[768,2048]{1,0:T(8,128)(2,1)S(1)} %bitcast.105, bf16[9,2048,256]{2,1,0:T(8,128)(2,1)} %bitcast.114), custom_call_target="tpu_custom_call" | custom-call | tf_op jit(solution)/shard_map/pallas_call | solution.py:77
  32.8 8.2 %collective-permute-done.1 = f32[32,12,256]{2,1,0:T(8,128)S(1)} collective-permute-done((f32[32,12,256]{2,1,0:T(8,128)S(1)}, f32[32,12,256]{2,1,0:T(8,128)S(1)}, u32[]{:S(2)}, u32[]{:S(2)}) %collective-permute-start.1) | collective-permute-done | bytes 393248 | tf_op jit(solution)/shard_map/ppermute | solution.py:19
  42.2 16.0 %all-to-all-start = ((f32[128,4,128]{2,1,0:T(4,128)}), f32[128,4,128]{2,1,0:T(4,128)S(1)}, u32[]{:S(2)}, u32[]{:S(2)}) async-start(f32[128,4,128]{2,1,0:T(4,128)} %broadcast_in_dim.17), calls=%async_computation | async-start | bytes 524288 | tf_op jit(solution)/shard_map/all_to_all | solution.py:30
  58.4 11.3 %all-to-all-done = f32[128,4,128]{2,1,0:T(4,128)S(1)} async-done(((f32[128,4,128]{2,1,0:T(4,128)}), f32[128,4,128]{2,1,0:T(4,128)S(1)}, u32[]{:S(2)}, u32[]{:S(2)}) %all-to-all-start) | async-done | bytes 262176 | tf_op jit(solution)/shard_map/all_to_all | solution.py:30
  73.2 20.4 %all_to_all.15 = f32[128,3,4,128]{3,2,1,0:T(4,128)S(1)} all-to-all(f32[128,3,4,128]{3,2,1,0:T(4,128)S(1)} %broadcast_in_dim.39), channel_id=1, replica_groups=mesh['lat'=8,'lon'=16] {'lat','lon'}, dimensions={0} | all-to-all | bytes 1572864 | tf_op jit(solution)/shard_map/all_to_all | solution.py:30
  94.0 2.3 %collective-permute-start.6 = (bf16[12,24,256]{2,1,0:T(8,128)(2,1)S(1)}, bf16[12,24,256]{2,1,0:T(8,128)(2,1)S(1)}, u32[]{:S(2)}, u32[]{:S(2)}) collective-permute-start(bf16[12,24,256]{2,1,0:T(8,128)(2,1)S(1)} %bitcast.145), channel_id=1, source_target_pairs={{0,16},{16,32},{32,48},{48,64},{64,80},{80,96},{96,112},{1,17},{17... | collective-permute-start | bytes 442376 | tf_op jit(solution)/shard_map/ppermute | solution.py:19
  98.3 5.3 %collective-permute-done.7 = bf16[12,24,256]{2,1,0:T(8,128)(2,1)S(1)} collective-permute-done((bf16[12,24,256]{2,1,0:T(8,128)(2,1)S(1)}, bf16[12,24,256]{2,1,0:T(8,128)(2,1)S(1)}, u32[]{:S(2)}, u32[]{:S(2)}) %collective-permute-start.7) | collective-permute-done | bytes 147488 | tf_op jit(solution)/shard_map/ppermute | solution.py:19
  103.9 3.0 %collective-permute-start.8 = (bf16[56,12,256]{2,1,0:T(8,128)(2,1)S(1)}, bf16[56,12,256]{2,1,0:T(8,128)(2,1)S(1)}, u32[]{:S(2)}, u32[]{:S(2)}) collective-permute-start(bf16[56,12,256]{2,1,0:T(8,128)(2,1)S(1)} %get-tuple-element.32), channel_id=1, source_target_pairs={{0,1},{1,2},{2,3},{3,4},{4,5},{5,6},{6,7},{7,8},{8,9},{9,10},{10,1... | collective-permute-start | bytes 1032200 | tf_op jit(solution)/shard_map/ppermute | solution.py:19
  106.9 6.4 %shard_map.113 = (bf16[768,1024]{1,0:T(8,128)(2,1)}, bf16[768,1024]{1,0:T(8,128)(2,1)}) custom-call(s32[1]{0:T(128)} %bitcast.36.which_ref, bf16[768,2048]{1,0:T(8,128)(2,1)} %bitcast.102), custom_call_target="tpu_custom_call" | custom-call | tf_op jit(solution)/shard_map/pallas_call | solution.py:110
  113.4 4.0 %collective-permute-start.11 = (bf16[768,1024]{1,0:T(8,128)(2,1)}, bf16[768,1024]{1,0:T(8,128)(2,1)S(1)}, u32[]{:S(2)}, u32[]{:S(2)}) collective-permute-start(bf16[768,1024]{1,0:T(8,128)(2,1)} %get-tuple-element.9), channel_id=1, source_target_pairs={{0,1},{1,0},{2,3},{3,2},{4,5},{5,4},{6,7},{7,6},{8,9},{9,8},{10,11... | collective-permute-start | bytes 4718600 | tf_op jit(solution)/shard_map/ppermute | solution.py:24
  117.4 2.1 %collective-permute-done.9 = bf16[56,12,256]{2,1,0:T(8,128)(2,1)S(1)} collective-permute-done((bf16[56,12,256]{2,1,0:T(8,128)(2,1)S(1)}, bf16[56,12,256]{2,1,0:T(8,128)(2,1)S(1)}, u32[]{:S(2)}, u32[]{:S(2)}) %collective-permute-start.9) | collective-permute-done | bytes 344096 | tf_op jit(solution)/shard_map/ppermute | solution.py:19
  123.5 2.5 %collective-permute-done.10 = bf16[56,48,256]{2,1,0:T(8,128)(2,1)S(1)} collective-permute-done((bf16[56,48,256]{2,1,0:T(8,128)(2,1)S(1)}, bf16[56,48,256]{2,1,0:T(8,128)(2,1)S(1)}, u32[]{:S(2)}, u32[]{:S(2)}) %collective-permute-start.10) | collective-permute-done | bytes 1376288 | tf_op jit(solution)/shard_map/ppermute | solution.py:24
  127.8 8.0 %fusion.6 = bf16[9,256,1024]{2,1,0:T(8,128)(2,1)S(1)} fusion(bf16[768,1024]{1,0:T(8,128)(2,1)S(1)} %collective-permute-done.11, bf16[768,1024]{1,0:T(8,128)(2,1)S(1)} %copy-done.10, bf16[9,768,256]{2,1,0:T(8,128)(2,1)S(1)} %get-tuple-element.42, bf16[9,768,256]{2,1,0:T(8,128)(2,1)S(1)} %get-tuple-element.43), kind=kOutput, calls=%fused_computation.8 | convolution fusion | flops 7270563840 | bytes 14942208 | tf_op jit(solution)/shard_map/tqf,qc->tfc/dot_general | solution.py:254
  137.1 3.0 %copy.55 = bf16[9,16,16,8,128]{4,2,0,1,3:T(8,128)(2,1)} copy(bf16[9,16,16,8,128]{4,3,2,1,0:T(8,128)(2,1)S(1)} %bitcast.117) | data formatting | bytes 9437184 | tf_op jit(solution)/shard_map/reshape | solution.py:256
  140.0 6.5 %all-to-all-start.2 = ((bf16[128,9,16,128]{3,2,1,0:T(8,128)(2,1)}), bf16[128,9,16,128]{3,2,1,0:T(8,128)(2,1)}, u32[]{:S(2)}, u32[]{:S(2)}) async-start(bf16[128,9,16,128]{3,2,1,0:T(8,128)(2,1)} %bitcast.116), calls=%async_computation.2 | async-start | bytes 9437184 | tf_op jit(solution)/shard_map/all_to_all | solution.py:258
  147.9 10.7 %shard_map.112 = bf16[768,2048]{1,0:T(8,128)(2,1)} custom-call(bf16[3,1344,256]{2,1,0:T(8,128)(2,1)S(1)} %pad_maximum_fusion.d_ref, bf16[9,2048,256]{2,1,0:T(8,128)(2,1)} %bitcast.115), custom_call_target="tpu_custom_call" | custom-call | tf_op jit(solution)/shard_map/pallas_call | solution.py:137
  158.6 47.4 %all-to-all-done.2 = bf16[128,9,16,128]{3,2,1,0:T(8,128)(2,1)} async-done(((bf16[128,9,16,128]{3,2,1,0:T(8,128)(2,1)}), bf16[128,9,16,128]{3,2,1,0:T(8,128)(2,1)}, u32[]{:S(2)}, u32[]{:S(2)}) %all-to-all-start.2) | async-done | bytes 4718624 | tf_op jit(solution)/shard_map/all_to_all | solution.py:258
  206.0 3.0 %convert_reduce_fusion = f32[2,9,16,128]{3,2,1,0:T(8,128)S(1)} fusion(bf16[64,2,9,16,128]{4,3,2,1,0:T(8,128)(2,1)} %bitcast.43), kind=kLoop, calls=%fused_computation | loop fusion | flops 4681728 | bytes 4866048 | tf_op jit(solution)/shard_map/reduce_sum | solution.py:260
  (94 shorter events, 20.2 us)
Async XLA Ops:
  0.6 69.3 %copy-start = (f32[3,256]{1,0:T(4,128)S(1)}, f32[3,256]{1,0:T(4,128)}, u32[]{:S(2)}) copy-start(f32[3,256]{1,0:T(4,128)} %param.10) | copy-start | bytes 9220
  0.6 1.9 copy-start.2
  8.5 13.7 %collective-permute-start.2 = (f32[2,12,12,256]{3,2,1,0:T(8,128)S(1)}, f32[2,12,12,256]{3,2,1,0:T(8,128)S(1)}, u32[]{:S(2)}, u32[]{:S(2)}) collective-permute-start(f32[2,12,12,256]{3,2,1,0:T(8,128)S(1)} %get-tuple-element.21), channel_id=1, source_target_pairs={{0,1},{1,2},{2,3},{3,4},{4,5},{5,6},{6,7},{7,8},{8,9},{9,10},{10,1... | collective-permute-start | bytes 884744 | tf_op jit(solution)/shard_map/ppermute | solution.py:19
  11.2 10.9 %collective-permute-start.3 = (f32[2,12,12,256]{3,2,1,0:T(8,128)S(1)}, f32[2,12,12,256]{3,2,1,0:T(8,128)S(1)}, u32[]{:S(2)}, u32[]{:S(2)}) collective-permute-start(f32[2,12,12,256]{3,2,1,0:T(8,128)S(1)} %get-tuple-element.22), channel_id=1, source_target_pairs={{0,15},{1,0},{2,1},{3,2},{4,3},{5,4},{6,5},{7,6},{8,7},{9,8},{10,9... | collective-permute-start | bytes 884744 | tf_op jit(solution)/shard_map/ppermute | solution.py:19
  18.6 14.2 %collective-permute-start = (f32[32,12,256]{2,1,0:T(8,128)S(1)}, f32[32,12,256]{2,1,0:T(8,128)S(1)}, u32[]{:S(2)}, u32[]{:S(2)}) collective-permute-start(f32[32,12,256]{2,1,0:T(8,128)S(1)} %get-tuple-element.25), channel_id=1, source_target_pairs={{0,1},{1,2},{2,3},{3,4},{4,5},{5,6},{6,7},{7,8},{8,9},{9,10},{10,1... | collective-permute-start | bytes 1179656 | tf_op jit(solution)/shard_map/ppermute | solution.py:19
  20.4 20.5 %collective-permute-start.1 = (f32[32,12,256]{2,1,0:T(8,128)S(1)}, f32[32,12,256]{2,1,0:T(8,128)S(1)}, u32[]{:S(2)}, u32[]{:S(2)}) collective-permute-start(f32[32,12,256]{2,1,0:T(8,128)S(1)} %get-tuple-element.26), channel_id=1, source_target_pairs={{0,15},{1,0},{2,1},{3,2},{4,3},{5,4},{6,5},{7,6},{8,7},{9,8},{10,9... | collective-permute-start | bytes 1179656 | tf_op jit(solution)/shard_map/ppermute | solution.py:19
  22.5 18.7 %collective-permute-start.4 = (f32[12,24,256]{2,1,0:T(8,128)S(1)}, f32[12,24,256]{2,1,0:T(8,128)S(1)}, u32[]{:S(2)}, u32[]{:S(2)}) collective-permute-start(f32[12,24,256]{2,1,0:T(8,128)S(1)} %get-tuple-element.34), channel_id=1, source_target_pairs={{0,16},{16,32},{32,48},{48,64},{64,80},{80,96},{96,112},{1,17},{17... | collective-permute-start | bytes 884744 | tf_op jit(solution)/shard_map/ppermute | solution.py:19
  27.3 13.9 %collective-permute-start.5 = (f32[12,24,256]{2,1,0:T(8,128)S(1)}, f32[12,24,256]{2,1,0:T(8,128)S(1)}, u32[]{:S(2)}, u32[]{:S(2)}) collective-permute-start(f32[12,24,256]{2,1,0:T(8,128)S(1)} %get-tuple-element.35), channel_id=1, source_target_pairs={{16,0},{32,16},{48,32},{64,48},{80,64},{96,80},{112,96},{17,1},{33... | collective-permute-start | bytes 884744 | tf_op jit(solution)/shard_map/ppermute | solution.py:19
  32.8 25.4 %copy-start.6 = (s32[32,24]{0,1:T(8,128)S(1)}, s32[32,24]{0,1:T(8,128)}, u32[]{:S(2)}) copy-start(s32[32,24]{0,1:T(8,128)} %param.11) | copy-start | bytes 9220
  32.8 37.0 %copy-start.5 = (f32[256]{0:T(256)S(1)}, f32[256]{0:T(256)}, u32[]{:S(2)}) copy-start(f32[256]{0:T(256)} %param.8) | copy-start | bytes 3076
  41.2 28.7 %copy-start.7 = (f32[256]{0:T(256)S(1)}, f32[256]{0:T(256)}, u32[]{:S(2)}) copy-start(f32[256]{0:T(256)} %param.9) | copy-start | bytes 3076
  42.2 27.4 %all-to-all-start = ((f32[128,4,128]{2,1,0:T(4,128)}), f32[128,4,128]{2,1,0:T(4,128)S(1)}, u32[]{:S(2)}, u32[]{:S(2)}) async-start(f32[128,4,128]{2,1,0:T(4,128)} %broadcast_in_dim.17), calls=%async_computation | async-start | bytes 524288 | tf_op jit(solution)/shard_map/all_to_all | solution.py:30
  93.8 19.6 %copy-start.8 = (f32[1,256]{1,0:T(1,128)}, f32[1,256]{1,0:T(1,128)S(1)}, u32[]{:S(2)}) copy-start(f32[1,256]{1,0:T(1,128)S(1)} %get-tuple-element.38) | copy-start | bytes 3076
  93.8 19.6 %copy-start.9 = (f32[1,256]{1,0:T(1,128)}, f32[1,256]{1,0:T(1,128)S(1)}, u32[]{:S(2)}) copy-start(f32[1,256]{1,0:T(1,128)S(1)} %get-tuple-element.39) | copy-start | bytes 3076
  94.0 4.3 %collective-permute-start.6 = (bf16[12,24,256]{2,1,0:T(8,128)(2,1)S(1)}, bf16[12,24,256]{2,1,0:T(8,128)(2,1)S(1)}, u32[]{:S(2)}, u32[]{:S(2)}) collective-permute-start(bf16[12,24,256]{2,1,0:T(8,128)(2,1)S(1)} %bitcast.145), channel_id=1, source_target_pairs={{0,16},{16,32},{32,48},{48,64},{64,80},{80,96},{96,112},{1,17},{17... | collective-permute-start | bytes 442376 | tf_op jit(solution)/shard_map/ppermute | solution.py:19
  96.3 7.4 %collective-permute-start.7 = (bf16[12,24,256]{2,1,0:T(8,128)(2,1)S(1)}, bf16[12,24,256]{2,1,0:T(8,128)(2,1)S(1)}, u32[]{:S(2)}, u32[]{:S(2)}) collective-permute-start(bf16[12,24,256]{2,1,0:T(8,128)(2,1)S(1)} %bitcast.144), channel_id=1, source_target_pairs={{16,0},{32,16},{48,32},{64,48},{80,64},{96,80},{112,96},{17,1},{33... | collective-permute-start | bytes 442376 | tf_op jit(solution)/shard_map/ppermute | solution.py:19
  103.7 13.7 %copy-start.3 = (bf16[12,24,256]{2,1,0:T(8,128)(2,1)}, bf16[12,24,256]{2,1,0:T(8,128)(2,1)S(1)}, u32[]{:S(2)}) copy-start(bf16[12,24,256]{2,1,0:T(8,128)(2,1)S(1)} %collective-permute-done.7) | copy-start | bytes 442372
  103.9 13.4 %collective-permute-start.8 = (bf16[56,12,256]{2,1,0:T(8,128)(2,1)S(1)}, bf16[56,12,256]{2,1,0:T(8,128)(2,1)S(1)}, u32[]{:S(2)}, u32[]{:S(2)}) collective-permute-start(bf16[56,12,256]{2,1,0:T(8,128)(2,1)S(1)} %get-tuple-element.32), channel_id=1, source_target_pairs={{0,1},{1,2},{2,3},{3,4},{4,5},{5,6},{6,7},{7,8},{8,9},{9,10},{10,1... | collective-permute-start | bytes 1032200 | tf_op jit(solution)/shard_map/ppermute | solution.py:19
  106.9 12.6 %collective-permute-start.9 = (bf16[56,12,256]{2,1,0:T(8,128)(2,1)S(1)}, bf16[56,12,256]{2,1,0:T(8,128)(2,1)S(1)}, u32[]{:S(2)}, u32[]{:S(2)}) collective-permute-start(bf16[56,12,256]{2,1,0:T(8,128)(2,1)S(1)} %get-tuple-element.33), channel_id=1, source_target_pairs={{0,15},{1,0},{2,1},{3,2},{4,3},{5,4},{6,5},{7,6},{8,7},{9,8},{10,9... | collective-permute-start | bytes 1032200 | tf_op jit(solution)/shard_map/ppermute | solution.py:19
  113.4 13.4 %collective-permute-start.11 = (bf16[768,1024]{1,0:T(8,128)(2,1)}, bf16[768,1024]{1,0:T(8,128)(2,1)S(1)}, u32[]{:S(2)}, u32[]{:S(2)}) collective-permute-start(bf16[768,1024]{1,0:T(8,128)(2,1)} %get-tuple-element.9), channel_id=1, source_target_pairs={{0,1},{1,0},{2,3},{3,2},{4,5},{5,4},{6,7},{7,6},{8,9},{9,8},{10,11... | collective-permute-start | bytes 4718600 | tf_op jit(solution)/shard_map/ppermute | solution.py:24
  119.5 1.7 copy-start.4
  121.9 4.2 %collective-permute-start.10 = (bf16[56,48,256]{2,1,0:T(8,128)(2,1)S(1)}, bf16[56,48,256]{2,1,0:T(8,128)(2,1)S(1)}, u32[]{:S(2)}, u32[]{:S(2)}) collective-permute-start(bf16[56,48,256]{2,1,0:T(8,128)(2,1)S(1)} %pad_maximum_fusion.1), channel_id=1, source_target_pairs={{0,1},{1,0},{2,3},{3,2},{4,5},{5,4},{6,7},{7,6},{8,9},{9,8},{10,11... | collective-permute-start | bytes 4128776 | tf_op jit(solution)/shard_map/ppermute | solution.py:24
  140.0 66.0 %all-to-all-start.2 = ((bf16[128,9,16,128]{3,2,1,0:T(8,128)(2,1)}), bf16[128,9,16,128]{3,2,1,0:T(8,128)(2,1)}, u32[]{:S(2)}, u32[]{:S(2)}) async-start(bf16[128,9,16,128]{3,2,1,0:T(8,128)(2,1)} %bitcast.116), calls=%async_computation.2 | async-start | bytes 9437184 | tf_op jit(solution)/shard_map/all_to_all | solution.py:258
  147.9 62.1 %copy-start.1 = (f32[3,256]{1,0:T(4,128)S(1)}, f32[3,256]{1,0:T(4,128)}, u32[]{:S(2)}) copy-start(f32[3,256]{1,0:T(4,128)} %param.10) | copy-start | bytes 9220
  (1 other events, 1.4 us)

commit v3 on v2

--- a/solution.py
+++ b/solution.py
@@ -19,9 +19,18 @@
     return lax.ppermute(x, axis, pairs)
 
 
-def core_swap(x):
+def swap(x, mask):
     count = lax.axis_size("lon")
-    return lax.ppermute(x, "lon", [(i, i ^ 1) for i in range(count)])
+    return lax.ppermute(x, "lon", [(i, i ^ mask) for i in range(count)])
+
+
+def to_groups(x, gap):
+    count = lax.axis_size("lon")
+    pairs = []
+    for first in range(0, count, 4):
+        pairs.append((first + 3, (first + 3 + gap) % count))
+        pairs.append((first, (first - gap) % count))
+    return lax.ppermute(x, "lon", pairs)
 
 
 def total(x):
@@ -87,36 +96,113 @@
     )(flat, weight)
 
 
-def split_halves(flat, which, half):
+def split_quarters(flat, where, quarter):
     cells, channels = flat.shape
-    count = channels // (2 * half)
-
-    def body(which_ref, x_ref, mine_ref, other_ref):
-        low, high = x_ref[:, :half], x_ref[:, half:]
-        first = which_ref[0] == 0
-
-        @pl.when(first)
-        def _():
-            mine_ref[...] = low
-            other_ref[...] = high
-
-        @pl.when(jnp.logical_not(first))
-        def _():
-            mine_ref[...] = high
-            other_ref[...] = low
-
-    shape = jax.ShapeDtypeStruct((cells, count * half), BF)
-    block = pl.BlockSpec((cells, half), lambda i, w: (0, i))
+    blocks = channels // (4 * quarter)
+
+    def body(where_ref, x_ref, *o_refs):
+        parts = []
+        for t in range(4):
+            left = x_ref[:, t * quarter : (t + 1) * quarter]
+            right = x_ref[:, (4 + t) * quarter : (5 + t) * quarter]
+            parts.append(jnp.concatenate([left, right], 1).T)
+        for here in range(4):
+
+            @pl.when(where_ref[0] == here)
+            def _():
+                for t in range(4):
+                    o_refs[here ^ t][...] = parts[t]
+
     return pl.pallas_call(
         body,
         grid_spec=pltpu.PrefetchScalarGridSpec(
             num_scalar_prefetch=1,
-            grid=(count,),
-            in_specs=[pl.BlockSpec((cells, 2 * half), lambda i, w: (0, i))],
-            out_specs=[block, block],
+            grid=(blocks // 2,),
+            in_specs=[pl.BlockSpec((cells, 8 * quarter), lambda i, w: (0, i))],
+            out_specs=[pl.BlockSpec((2 * quarter, cells), lambda i, w: (i, 0))] * 4,
         ),
-        out_shape=[shape, shape],
-    )(which.reshape(1).astype(jnp.int32), flat)
+        out_shape=[jax.ShapeDtypeStruct((blocks * quarter, cells), BF)] * 4,
+        compiler_params=pltpu.CompilerParams(vmem_limit_bytes=48 * 1024 * 1024),
+    )(where.reshape(1).astype(jnp.int32), flat)
+
+
+def group_windows(place, mine, pair, breadth):
+    rows, _, filters = mine[0].shape
+    step, lead = 8, 16
+    wide = lead + 4 * breadth + lead
+
+    def body(place_ref, *refs):
+        parts, o_ref, buf = refs[:8], refs[8], refs[9]
+        here = place_ref[0]
+        order = (0, 4, 1, 5)
+        for k in range(4):
+            first = pl.multiple_of(lead + breadth * (here ^ k), 8)
+            d = parts[order[k]][...]
+            o_ref[1, k] = d.reshape(step * breadth, filters)
+            buf[:, pl.ds(first, breadth), :] = d.astype(F32)
+        ends = (here == 0) | (here == 3)
+        west = here < 2
+        near, far = [jnp.where(ends, parts[n][...], parts[4 + n][...]).astype(F32) for n in (2, 3)]
+        buf[:, lead - RATE : lead, :] = jnp.where(west, near, far)
+        buf[:, lead + 4 * breadth : lead + 4 * breadth + RATE, :] = jnp.where(west, far, near)
+        for t in range(4):
+            for c in (0, 2):
+                first = lead + t * breadth + (c - 1) * RATE
+                win = buf[:, first : first + breadth, :]
+                o_ref[c, here ^ t] = win.reshape(step * breadth, filters).astype(BF)
+
+    arrays = tuple(mine) + tuple(pair)
+    return pl.pallas_call(
+        body,
+        grid_spec=pltpu.PrefetchScalarGridSpec(
+            num_scalar_prefetch=1,
+            grid=(rows // step,),
+            in_specs=[
+                pl.BlockSpec((step, x.shape[1], filters), lambda i, place: (i, 0, 0)) for x in arrays
+            ],
+            out_specs=pl.BlockSpec((3, 4, step * breadth, filters), lambda i, place: (0, 0, i, 0)),
+            scratch_shapes=[pltpu.VMEM((step, wide, filters), F32)],
+        ),
+        out_shape=jax.ShapeDtypeStruct((3, 4, rows * breadth, filters), BF),
+        compiler_params=pltpu.CompilerParams(vmem_limit_bytes=48 * 1024 * 1024),
+    )(place.reshape(1).astype(jnp.int32), *arrays)
+
+
+def grad_kernel(d_all, group_in, lats, lons, step_rows):
+    filters = d_all.shape[3]
+    width, cells = group_in[0].shape
+    quarter = width // lats
+    half_f = filters // lons // 2
+
+    def body(d_ref, *refs):
+        x_refs, o_ref = refs[:4], refs[4]
+        for r in range(3):
+            at = (2 - r) * step_rows
+            acc = None
+            for k in range(4):
+                part = jnp.dot(x_refs[k][...], d_ref[0, k, at : at + cells, :], preferred_element_type=F32)
+                acc = part if acc is None else acc + part
+            out = acc.T
+            for pair in range(lats // 2):
+                both = out[:, pair * 2 * quarter : (pair + 1) * 2 * quarter]
+                both = both.reshape(lons, 2, half_f, 2 * quarter)
+                low, high = both[:, 0], both[:, 1]
+                even = jnp.concatenate([low[..., :quarter], high[..., :quarter]], 2)
+                odd = jnp.concatenate([low[..., quarter:], high[..., quarter:]], 2)
+                o_ref[2 * pair, :, r, 0] = even.astype(BF)
+                o_ref[2 * pair + 1, :, r, 0] = odd.astype(BF)
+
+    return pl.pallas_call(
+        body,
+        grid=(3,),
+        in_specs=[
+            pl.BlockSpec((1,) + d_all.shape[1:], lambda c: (2 - c, 0, 0, 0)),
+        ]
+        + [pl.BlockSpec((width, cells), lambda c: (0, 0))] * 4,
+        out_specs=pl.BlockSpec((lats, lons, 3, 1, half_f, 2 * quarter), lambda c: (0, 0, 0, c, 0, 0)),
+        out_shape=jax.ShapeDtypeStruct((lats, lons, 3, 3, half_f, 2 * quarter), BF),
+        compiler_params=pltpu.CompilerParams(vmem_limit_bytes=56 * 1024 * 1024),
+    )(d_all, *group_in)
 
 
 def grad_input(dcols, weight, cells, step_rows):
@@ -165,7 +251,8 @@
     filters = atrous_weight.shape[3]
     classes = head_weight.shape[0]
     lats, lons = lax.axis_size("lat"), lax.axis_size("lon")
-    core = lax.axis_index("lon") % 2
+    lat = lax.axis_index("lat")
+    place = lax.axis_index("lon") % 4
     cells = height * breadth
     total_cells = cells * lats * lons
     step_rows = RATE * breadth
@@ -174,9 +261,10 @@
 
     rest = breadth - RATE
     outer = outer_rows(flat, weight, step_rows).reshape(2, 3, RATE, breadth, filters)
+    outer, late_weight = lax.optimization_barrier((outer, weight))
     outer_w = ring(outer[:, 0, :, RATE:], "lon", 1, True)
     outer_e = ring(outer[:, 2, :, :rest], "lon", -1, True)
-    sides = inner_rows(flat, weight, step_rows, (0, 2)).reshape(2, height, breadth, filters)
+    sides = inner_rows(flat, late_weight, step_rows, (0, 2)).reshape(2, height, breadth, filters)
     inner_w = ring(sides[0, :, RATE:], "lon", 1, True)
     inner_e = ring(sides[1, :, :rest], "lon", -1, True)
     strips = outer[:, 1] + jnp.concatenate(
@@ -184,12 +272,13 @@
     )
     from_s = ring(strips[0], "lat", -1, False)
     from_n = ring(strips[1], "lat", 1, False)
-    centre = inner_rows(flat, weight, step_rows, (1,)).reshape(height, breadth, filters)
+    quarter = channels // (4 * lats)
+    quarters = split_quarters(flat, place, quarter)
+    inner_w, inner_e, quarters = lax.optimization_barrier((inner_w, inner_e, quarters))
+    group_in = [quarters[0]] + [swap(quarters[k], k) for k in range(1, 4)]
+
+    centre = inner_rows(flat, late_weight, step_rows, (1,)).reshape(height, breadth, filters)
     centre = centre + jnp.concatenate([sides[1, :, rest:] + inner_w, sides[0, :, :RATE] + inner_e], 1)
-
-    half = channels // (2 * lats)
-    mine, other = split_halves(flat, core, half)
-    theirs = core_swap(other)
 
     zero = jnp.zeros((height - RATE, breadth, filters), F32)
     summed = (
@@ -197,12 +286,23 @@
     ).reshape(cells, filters)
 
     moments = total(jnp.stack([jnp.sum(summed, 0), jnp.sum(summed * summed, 0)]).reshape(-1, 128))
+    moments, group_in[2] = lax.optimization_barrier((moments, group_in[2]))
     moments = moments.reshape(2, filters)
     average = moments[0] / total_cells
     variance = moments[1] / total_cells - average * average
     inverse = lax.rsqrt(variance + epsilon)
     normed = (summed - average) * inverse
     preact = norm_gain * normed + norm_bias
+
+    pre_low = preact.astype(BF).reshape(height, breadth, filters)
+    lab_low = labels.T.astype(BF)
+
+    def with_labels(rows):
+        lab = jnp.pad(lab_low[:, rows], ((0, 0), (0, filters - RATE)))
+        return jnp.concatenate([pre_low[rows], lab[None]], 0)
+
+    pre_n = ring(with_labels(slice(height - RATE, height)), "lat", 1, False)
+    pre_s = ring(with_labels(slice(0, RATE)), "lat", -1, False)
 
     hidden, logits, one_hot, partition, grad_logits, d_preact = head(preact, labels.reshape(-1), head_weight)
     loss_terms = jnp.sum(jnp.log(partition)[:, 0] - jnp.sum(logits * one_hot, 1))
@@ -216,51 +316,41 @@
         ],
         0,
     )
-    totals = total(payload.reshape(-1, 4, 128)).reshape(classes + 3, filters) / total_cells
+    totals = total(payload.reshape(-1, 4, 128))
+    totals, group_in[3] = lax.optimization_barrier((totals, group_in[3]))
+    totals = totals.reshape(classes + 3, filters) / total_cells
     grad_bias, grad_gain, grad_head = totals[0], totals[1], totals[2 : 2 + classes]
     mean_loss = totals[2 + classes, 0]
 
     scale = norm_gain * inverse
+    slope = inverse * grad_gain
+    shift = slope * norm_bias - scale * grad_bias
     d_own = (scale * (d_preact - grad_bias - normed * grad_gain)).astype(BF)
-    d_own = d_own.reshape(height, breadth, filters)
-
-    d_n = ring(d_own[height - RATE :], "lat", 1, False)
-    d_s = ring(d_own[:RATE], "lat", -1, False)
-    d_col = jnp.concatenate([d_n, d_own, d_s], 0)
-    d_w = ring(d_col[:, breadth - RATE :], "lon", 1, True)
-    d_e = ring(d_col[:, :RATE], "lon", -1, True)
-    d_pad = jnp.concatenate([d_w, d_col, d_e], 1)
-    d_pair = core_swap(d_pad)
-
-    def columns(pad):
-        parts = [pad[:, c * RATE : c * RATE + breadth].reshape(-1, filters) for c in range(3)]
-        return jnp.stack(parts, 0)
-
-    d_cols = columns(d_pad)
-    d_cols_pair = columns(d_pair)
-
-    def windows(cols):
-        return jnp.stack(
-            [
-                cols[2 - c, (2 - r) * step_rows : (2 - r) * step_rows + cells]
-                for r in range(3)
-                for c in range(3)
-            ],
-            0,
-        )
-
-    shifted = jnp.concatenate([windows(d_cols), windows(d_cols_pair)], 1)
-    pair_in = jnp.concatenate([mine, theirs], 0)
-    partial = jnp.einsum("tqf,qc->tfc", shifted, pair_in, preferred_element_type=F32).astype(BF)
+
+    def halo(pre, exists):
+        lab = pre[RATE, :, :RATE].T.astype(jnp.int32)
+        wide = pre[:RATE].astype(F32).reshape(step_rows, filters)
+        d_pre = head(wide, lab.reshape(step_rows), head_weight)[-1]
+        d = scale * d_pre - slope * wide + shift
+        return jnp.where(exists, d, 0.0).astype(BF)
+
+    d_col = jnp.concatenate([halo(pre_n, lat > 0), d_own, halo(pre_s, lat < lats - 1)], 0)
+    d_col = d_col.reshape(height + 2 * RATE, breadth, filters)
+    strip = jnp.where(place == 0, d_col[:, :RATE], d_col[:, breadth - RATE :])
+    mine = (d_col, swap(d_col, 2), to_groups(strip, 1), to_groups(strip, 4))
+    pair = [swap(x, 1) for x in mine]
+    d_all = group_windows(place, mine, pair, breadth)
+
+    blocks = grad_kernel(d_all, group_in, lats, lons, step_rows)
+    blocks = blocks.reshape(lats * lons, -1, 2 * quarter)
+    got = lax.all_to_all(blocks, ("lat", "lon"), 0, 0)
     own_f = filters // lons
-    blocks = partial.reshape(9, lons, own_f, lats, half)
-    blocks = jnp.transpose(blocks, (3, 1, 0, 2, 4)).reshape(lats * lons, 9, own_f, half)
-    got = lax.all_to_all(blocks, ("lat", "lon"), 0, 0)
-    got = got.reshape(lats * lons // 2, 2, 9, own_f, half)
-    weight_block = jnp.sum(got.astype(F32), 0) / total_cells
-    grad_weight = jnp.transpose(weight_block, (0, 3, 1, 2)).reshape(2 * half, 3, 3, own_f)
-
-    grad_features = grad_input(d_cols, weight, cells, step_rows).reshape(height, breadth, channels)
+    got = got.reshape(lats, lons // 4, 4, -1, 2 * quarter)
+    weight_block = jnp.sum(got.astype(F32), (0, 1)) / total_cells
+    weight_block = weight_block.reshape(4, 9, own_f // 2, 2, quarter)
+    grad_weight = jnp.transpose(weight_block, (0, 4, 1, 3, 2)).reshape(4 * quarter, 3, 3, own_f)
+
+    grad_features = grad_input(d_all[:, 0], weight, cells, step_rows).reshape(height, breadth, channels)
     return (mean_loss, grad_features, grad_weight, grad_gain, grad_bias, grad_head)
 
 

time: 211 us -> 193 us (0.915)
  waiting for transfers between devices: 77.6 us -> 52.6 us
  blocking collectives: 20.4 us -> 0 us
  Pallas kernels: 34.5 us -> 50.7 us
  starting transfers between devices: 46.9 us -> 62.3 us
  matrix products: 9.68 us -> 3.31 us
  local copies, waits for them, and re-layouts: 12.2 us -> 14.8 us
    all_to_all x1, waiting for transfers between devices: 47.4 us -> 19.3 us  [shards(): got = lax.all_to_all(blocks, ('lat', 'lon'), 0, 0)]
    all_to_all x1 -> x0, blocking collectives: 20.4 us -> none  [total(): return jnp.sum(lax.all_to_all(spread, ('lat', 'lon'), 0, 0), 0)]
    pallas_call x1 -> x3, Pallas kernels: 6.44 us -> 22.6 us  [the longest x1 12.5 us: grad_kernel(): pl.pallas_call(body, grid=(3,), in_specs=[pl.BlockSpec((1,) + d_all.shape...]
    ppermute x2 -> x10, starting transfers between devices: 5.37 us -> 19.2 us  [the longest x8 17.8 us: swap(): return lax.ppermute(x, 'lon', [(i, i ^ mask) for i in range(count)])]
    ppermute x10 -> x8, waiting for transfers between devices: 16.4 us -> 2.69 us  [ring(): return lax.ppermute(x, axis, pairs)]
    all_to_all x1 -> x2, waiting for transfers between devices: 11.3 us -> 21.6 us  [total(): return jnp.sum(lax.all_to_all(spread, ('lat', 'lon'), 0, 0), 0)]
    dot_general x1 -> x0, matrix products: 7.98 us -> none  [shards(): jnp.einsum('tqf,qc->tfc', shifted, pair_in, preferred_element_type=F32)]
    ppermute x2 -> x10, waiting for transfers between devices: 2.51 us -> 8.99 us  [the longest x8 8.98 us: swap(): return lax.ppermute(x, 'lon', [(i, i ^ mask) for i in range(count)])]
  transfers between devices with their start and end apart: 14 -> 21, of which waited for: 7 -> 6; matrix products, arithmetic and copies ran while one was open for 2% -> 10% of each run, Pallas kernels for 14% -> 17%
where the time goes in v3:
time: 193 us; the launch traced here: 192 us
  starting transfers between devices  62.3 us (32%)
  waiting for transfers between devices  52.6 us (27%)
  Pallas kernels  50.7 us (26%)
  local copies, waits for them, and re-layouts  14.8 us (8%)
  other arithmetic  7.25 us (4%)
  matrix products  3.31 us (2%)
    all_to_all x2, waiting for transfers between devices, total(): return jnp.sum(lax.all_to_all(spread, ('lat', 'lon'), 0, 0), 0)  21.6 us
    ppermute x8, starting transfers between devices, ring(): return lax.ppermute(x, axis, pairs)  19.5 us
    all_to_all x1, waiting for transfers between devices, shards(): got = lax.all_to_all(blocks, ('lat', 'lon'), 0, 0)  19.3 us
    all_to_all x2, starting transfers between devices, total(): return jnp.sum(lax.all_to_all(spread, ('lat', 'lon'), 0, 0), 0)  18.7 us
    ppermute x8, starting transfers between devices, swap(): return lax.ppermute(x, 'lon', [(i, i ^ mask) for i in range(count)])  17.8 us
    pallas_call x1, Pallas kernels, grad_kernel(): pl.pallas_call(body, grid=(3,), in_specs=[pl.BlockSpec((1,) + d_all.shape...  12.5 us
    pallas_call x2, Pallas kernels, inner_rows(): pl.pallas_call(body, grid=(len(cols), 3), in_specs=[pl.BlockSpec((cells,...  11.5 us
    pallas_call x1, Pallas kernels, grad_input(): pl.pallas_call(body, grid=(channels // block,), in_specs=[pl.BlockSpec(dc...  10.7 us
  transfers between devices with their start and end apart: 21, of which 6 were waited for; matrix products, arithmetic and copies ran while one was open for 10% of the time, Pallas kernels for 17%

profile of v3, /device:TPU:1, one launch (start us, length us, event | category | flops | bytes accessed | tf_op | source)
XLA Modules:
  0.0 192.1 jit_solution(4354210452410824289)
XLA Ops:
  0.7 1.9 copy-done.1
  2.5 5.8 %shard_map.109 = f32[2,3,288,256]{3,2,1,0:T(8,128)S(1)} custom-call(bf16[768,2048]{1,0:T(8,128)(2,1)S(1)} %bitcast.114, bf16[9,2048,256]{2,1,0:T(8,128)(2,1)} %bitcast.127), custom_call_target="tpu_custom_call" | custom-call | tf_op jit(solution)/shard_map/pallas_call | solution.py:50
  8.5 2.8 %collective-permute-start.2 = (f32[2,12,12,256]{3,2,1,0:T(8,128)S(1)}, f32[2,12,12,256]{3,2,1,0:T(8,128)S(1)}, u32[]{:S(2)}, u32[]{:S(2)}) collective-permute-start(f32[2,12,12,256]{3,2,1,0:T(8,128)S(1)} %get-tuple-element.51), channel_id=1, source_target_pairs={{0,1},{1,2},{2,3},{3,4},{4,5},{5,6},{6,7},{7,8},{8,9},{9,10},{10,1... | collective-permute-start | bytes 884744 | tf_op jit(solution)/shard_map/ppermute | solution.py:19
  11.2 7.3 %shard_map.111 = f32[2,768,256]{2,1,0:T(8,128)S(1)} custom-call(bf16[768,2048]{1,0:T(8,128)(2,1)S(1)} %bitcast.115, bf16[9,2048,256]{2,1,0:T(8,128)(2,1)} %bitcast.128), custom_call_target="tpu_custom_call" | custom-call | tf_op jit(solution)/shard_map/pallas_call | solution.py:86
  19.8 3.4 %collective-permute-start.1 = (f32[32,12,256]{2,1,0:T(8,128)}, f32[32,12,256]{2,1,0:T(8,128)}, u32[]{:S(2)}, u32[]{:S(2)}) collective-permute-start(f32[32,12,256]{2,1,0:T(8,128)} %get-tuple-element.55), channel_id=1, source_target_pairs={{0,15},{1,0},{2,1},{3,2},{4,3},{5,4},{6,5},{7,6},{8,7},{9,8},{10,9... | collective-permute-start | bytes 1179656 | tf_op jit(solution)/shard_map/ppermute | solution.py:19
  24.3 4.7 %collective-permute-start.4 = (f32[12,24,256]{2,1,0:T(8,128)}, f32[12,24,256]{2,1,0:T(8,128)S(1)}, u32[]{:S(2)}, u32[]{:S(2)}) collective-permute-start(f32[12,24,256]{2,1,0:T(8,128)} %get-tuple-element.57), channel_id=1, source_target_pairs={{0,16},{16,32},{32,48},{48,64},{64,80},{80,96},{96,112},{1,17},{17... | collective-permute-start | bytes 884744 | tf_op jit(solution)/shard_map/ppermute | solution.py:19
  30.3 4.2 %shard_map.110 = f32[1,768,256]{2,1,0:T(8,128)S(1)} custom-call(bf16[768,2048]{1,0:T(8,128)(2,1)S(1)} %bitcast.116, bf16[9,2048,256]{2,1,0:T(8,128)(2,1)} %bitcast.129), custom_call_target="tpu_custom_call" | custom-call | tf_op jit(solution)/shard_map/pallas_call | solution.py:86
  35.5 5.1 %shard_map.112 = (bf16[512,768]{1,0:T(8,128)(2,1)S(1)}, bf16[512,768]{1,0:T(8,128)(2,1)S(1)}, bf16[512,768]{1,0:T(8,128)(2,1)}, bf16[512,768]{1,0:T(8,128)(2,1)S(1)}) custom-call(s32[1]{0:T(128)} %bitcast.8.where_ref.place_ref, bf16[768,2048]{1,0:T(8,128)(2,1)} %bitcast.113), custom_call_target="tpu_custom_call" | custom-call | tf_op jit(solution)/shard_map/pallas_call | solution.py:116
  40.6 2.4 %collective-permute-start.6 = (bf16[512,768]{1,0:T(8,128)(2,1)}, bf16[512,768]{1,0:T(8,128)(2,1)}, u32[]{:S(2)}, u32[]{:S(2)}) collective-permute-start(bf16[512,768]{1,0:T(8,128)(2,1)} %get-tuple-element.30), channel_id=1, source_target_pairs={{0,2},{1,3},{2,0},{3,1},{4,6},{5,7},{6,4},{7,5},{8,10},{9,11},{10,... | collective-permute-start | bytes 2359304 | tf_op jit(solution)/shard_map/ppermute | solution.py:24
  44.3 2.7 %collective-permute-done.4 = f32[12,24,256]{2,1,0:T(8,128)S(1)} collective-permute-done((f32[12,24,256]{2,1,0:T(8,128)}, f32[12,24,256]{2,1,0:T(8,128)S(1)}, u32[]{:S(2)}, u32[]{:S(2)}) %collective-permute-start.4) | collective-permute-done | bytes 294944 | tf_op jit(solution)/shard_map/ppermute | solution.py:19
  49.0 10.5 %all-to-all-start = ((f32[128,4,128]{2,1,0:T(4,128)}), f32[128,4,128]{2,1,0:T(4,128)S(1)}, u32[]{:S(2)}, u32[]{:S(2)}) async-start(f32[128,4,128]{2,1,0:T(4,128)} %broadcast_in_dim.26), calls=%async_computation | async-start | bytes 524288 | tf_op jit(solution)/shard_map/all_to_all | solution.py:39
  61.5 9.4 %all-to-all-done = f32[128,4,128]{2,1,0:T(4,128)S(1)} async-done(((f32[128,4,128]{2,1,0:T(4,128)}), f32[128,4,128]{2,1,0:T(4,128)S(1)}, u32[]{:S(2)}, u32[]{:S(2)}) %all-to-all-start) | async-done | bytes 262176 | tf_op jit(solution)/shard_map/all_to_all | solution.py:39
  75.0 6.2 %collective-permute-start.8 = (bf16[13,24,256]{2,1,0:T(8,128)(2,1)S(1)}, bf16[13,24,256]{2,1,0:T(8,128)(2,1)}, u32[]{:S(2)}, u32[]{:S(2)}) collective-permute-start(bf16[13,24,256]{2,1,0:T(8,128)(2,1)S(1)} %pad_maximum_fusion.1), channel_id=1, source_target_pairs={{0,16},{16,32},{32,48},{48,64},{64,80},{80,96},{96,112},{1,17},{17... | collective-permute-start | bytes 479240 | tf_op jit(solution)/shard_map/ppermute | solution.py:19
  83.0 8.2 %all-to-all-start.1 = ((f32[128,3,4,128]{3,2,1,0:T(4,128)}), f32[128,3,4,128]{3,2,1,0:T(4,128)}, u32[]{:S(2)}, u32[]{:S(2)}) async-start(f32[128,3,4,128]{3,2,1,0:T(4,128)} %broadcast_in_dim.32), calls=%async_computation.1 | async-start | bytes 1572864 | tf_op jit(solution)/shard_map/all_to_all | solution.py:39
  95.4 12.2 %all-to-all-done.1 = f32[128,3,4,128]{3,2,1,0:T(4,128)} async-done(((f32[128,3,4,128]{3,2,1,0:T(4,128)}), f32[128,3,4,128]{3,2,1,0:T(4,128)}, u32[]{:S(2)}, u32[]{:S(2)}) %all-to-all-start.1) | async-done | bytes 786464 | tf_op jit(solution)/shard_map/all_to_all | solution.py:39
  113.0 6.4 %collective-permute-start.13 = (bf16[56,24,256]{2,1,0:T(8,128)(2,1)S(1)}, bf16[56,24,256]{2,1,0:T(8,128)(2,1)S(1)}, u32[]{:S(2)}, u32[]{:S(2)}) collective-permute-start(bf16[56,24,256]{2,1,0:T(8,128)(2,1)S(1)} %bitcast.124), channel_id=1, source_target_pairs={{0,1},{1,0},{2,3},{3,2},{4,5},{5,4},{6,7},{7,6},{8,9},{9,8},{10,11... | collective-permute-start | bytes 2064392 | tf_op jit(solution)/shard_map/ppermute | solution.py:24
  119.3 7.5 %collective-permute-done.10.refs_1_ = bf16[56,24,256]{2,1,0:T(8,128)(2,1)S(1)} collective-permute-done((bf16[56,24,256]{2,1,0:T(8,128)(2,1)S(1)}, bf16[56,24,256]{2,1,0:T(8,128)(2,1)S(1)}, u32[]{:S(2)}, u32[]{:S(2)}) %collective-permute-start.10) | collective-permute-done | bytes 688160 | tf_op jit(solution)/shard_map/ppermute | solution.py:24
  126.9 2.2 %collective-permute-start.14 = (bf16[56,24,256]{2,1,0:T(8,128)(2,1)S(1)}, bf16[56,24,256]{2,1,0:T(8,128)(2,1)S(1)}, u32[]{:S(2)}, u32[]{:S(2)}) collective-permute-start(bf16[56,24,256]{2,1,0:T(8,128)(2,1)S(1)} %collective-permute-done.10.refs_1_), channel_id=1, source_target_pairs={{0,1},{1,0},{2,3},{3,2},{4,5},{5,4},{6,7},{7,6},{8,9},{9,8},{10,11... | collective-permute-start | bytes 2064392 | tf_op jit(solution)/shard_map/ppermute | solution.py:24
  129.1 3.9 %collective-permute-start.15 = (bf16[56,12,256]{2,1,0:T(8,128)(2,1)S(1)}, bf16[56,12,256]{2,1,0:T(8,128)(2,1)S(1)}, u32[]{:S(2)}, u32[]{:S(2)}) collective-permute-start(bf16[56,12,256]{2,1,0:T(8,128)(2,1)S(1)} %collective-permute-done.11.refs_2_), channel_id=1, source_target_pairs={{0,1},{1,0},{2,3},{3,2},{4,5},{5,4},{6,7},{7,6},{8,9},{9,8},{10,11... | collective-permute-start | bytes 1032200 | tf_op jit(solution)/shard_map/ppermute | solution.py:24
  134.4 5.0 %shard_map.113.d_ref = bf16[3,4,1344,256]{3,2,1,0:T(8,128)(2,1)} custom-call(s32[1]{0:T(128)} %bitcast.8.where_ref.place_ref, bf16[56,24,256]{2,1,0:T(8,128)(2,1)S(1)} %bitcast.125, bf16[56,24,256]{2,1,0:T(8,128)(2,1)S(1)} %collective-permute-done.10.refs_1_, bf16[56,12,256]{2,1,0:T(8,128)(2,1)S(1)} %collective-permute-done.11.refs_2_, ...), custom_call_target="tpu_custom_call" | custom-call | tf_op jit(solution)/shard_map/pallas_call | solution.py:155
  140.3 12.5 %shard_map.115 = bf16[8,16,3,3,8,128]{5,4,3,2,1,0:T(8,128)(2,1)} custom-call(bf16[3,4,1344,256]{3,2,1,0:T(8,128)(2,1)} %shard_map.113.d_ref, bf16[512,768]{1,0:T(8,128)(2,1)} %copy-done.7, bf16[512,768]{1,0:T(8,128)(2,1)} %copy-done.8, bf16[512,768]{1,0:T(8,128)(2,1)} %collective-permute-done.6.refs_2_, bf16[512,768]{1,0:T(8,128)(2,1)} %collective-permute-done.7.refs_3_), custom_call_target="tpu_custom_call" | custom-call | tf_op jit(solution)/shard_map/pallas_call | solution.py:195
  152.9 4.8 %all-to-all-start.2 = ((bf16[128,72,128]{2,1,0:T(8,128)(2,1)}), bf16[128,72,128]{2,1,0:T(8,128)(2,1)S(1)}, u32[]{:S(2)}, u32[]{:S(2)}) async-start(bf16[128,72,128]{2,1,0:T(8,128)(2,1)} %bitcast.132), calls=%async_computation.2 | async-start | bytes 4718592 | tf_op jit(solution)/shard_map/all_to_all | solution.py:346
  160.5 10.7 %shard_map.114 = bf16[768,2048]{1,0:T(8,128)(2,1)} custom-call(bf16[3,1344,256]{2,1,0:T(8,128)(2,1)S(1)} %slice_bitcast_fusion.d_ref, bf16[9,2048,256]{2,1,0:T(8,128)(2,1)} %bitcast.130), custom_call_target="tpu_custom_call" | custom-call | tf_op jit(solution)/shard_map/pallas_call | solution.py:223
  171.3 19.3 %all-to-all-done.2 = bf16[128,72,128]{2,1,0:T(8,128)(2,1)S(1)} async-done(((bf16[128,72,128]{2,1,0:T(8,128)(2,1)}), bf16[128,72,128]{2,1,0:T(8,128)(2,1)S(1)}, u32[]{:S(2)}, u32[]{:S(2)}) %all-to-all-start.2) | async-done | bytes 2359328 | tf_op jit(solution)/shard_map/all_to_all | solution.py:346
  (112 shorter events, 31.9 us)
Async XLA Ops:
  0.6 70.7 %copy-start = (f32[3,256]{1,0:T(4,128)S(1)}, f32[3,256]{1,0:T(4,128)}, u32[]{:S(2)}) copy-start(f32[3,256]{1,0:T(4,128)} %param.10) | copy-start | bytes 9220
  8.5 14.7 %collective-permute-start.2 = (f32[2,12,12,256]{3,2,1,0:T(8,128)S(1)}, f32[2,12,12,256]{3,2,1,0:T(8,128)S(1)}, u32[]{:S(2)}, u32[]{:S(2)}) collective-permute-start(f32[2,12,12,256]{3,2,1,0:T(8,128)S(1)} %get-tuple-element.51), channel_id=1, source_target_pairs={{0,1},{1,2},{2,3},{3,4},{4,5},{5,6},{6,7},{7,8},{8,9},{9,10},{10,1... | collective-permute-start | bytes 884744 | tf_op jit(solution)/shard_map/ppermute | solution.py:19
  11.2 11.9 %collective-permute-start.3 = (f32[2,12,12,256]{3,2,1,0:T(8,128)S(1)}, f32[2,12,12,256]{3,2,1,0:T(8,128)S(1)}, u32[]{:S(2)}, u32[]{:S(2)}) collective-permute-start(f32[2,12,12,256]{3,2,1,0:T(8,128)S(1)} %get-tuple-element.52), channel_id=1, source_target_pairs={{0,15},{1,0},{2,1},{3,2},{4,3},{5,4},{6,5},{7,6},{8,7},{9,8},{10,9... | collective-permute-start | bytes 884744 | tf_op jit(solution)/shard_map/ppermute | solution.py:19
  19.8 20.8 %collective-permute-start.1 = (f32[32,12,256]{2,1,0:T(8,128)}, f32[32,12,256]{2,1,0:T(8,128)}, u32[]{:S(2)}, u32[]{:S(2)}) collective-permute-start(f32[32,12,256]{2,1,0:T(8,128)} %get-tuple-element.55), channel_id=1, source_target_pairs={{0,15},{1,0},{2,1},{3,2},{4,3},{5,4},{6,5},{7,6},{8,7},{9,8},{10,9... | collective-permute-start | bytes 1179656 | tf_op jit(solution)/shard_map/ppermute | solution.py:19
  23.1 17.4 %collective-permute-start = (f32[32,12,256]{2,1,0:T(8,128)}, f32[32,12,256]{2,1,0:T(8,128)}, u32[]{:S(2)}, u32[]{:S(2)}) collective-permute-start(f32[32,12,256]{2,1,0:T(8,128)} %get-tuple-element.56), channel_id=1, source_target_pairs={{0,1},{1,2},{2,3},{3,4},{4,5},{5,6},{6,7},{7,8},{8,9},{9,10},{10,1... | collective-permute-start | bytes 1179656 | tf_op jit(solution)/shard_map/ppermute | solution.py:19
  24.3 22.7 %collective-permute-start.4 = (f32[12,24,256]{2,1,0:T(8,128)}, f32[12,24,256]{2,1,0:T(8,128)S(1)}, u32[]{:S(2)}, u32[]{:S(2)}) collective-permute-start(f32[12,24,256]{2,1,0:T(8,128)} %get-tuple-element.57), channel_id=1, source_target_pairs={{0,16},{16,32},{32,48},{48,64},{64,80},{80,96},{96,112},{1,17},{17... | collective-permute-start | bytes 884744 | tf_op jit(solution)/shard_map/ppermute | solution.py:19
  29.0 18.0 %collective-permute-start.5 = (f32[12,24,256]{2,1,0:T(8,128)}, f32[12,24,256]{2,1,0:T(8,128)}, u32[]{:S(2)}, u32[]{:S(2)}) collective-permute-start(f32[12,24,256]{2,1,0:T(8,128)} %get-tuple-element.58), channel_id=1, source_target_pairs={{16,0},{32,16},{48,32},{64,48},{80,64},{96,80},{112,96},{17,1},{33... | collective-permute-start | bytes 884744 | tf_op jit(solution)/shard_map/ppermute | solution.py:19
  40.6 30.5 %collective-permute-start.6 = (bf16[512,768]{1,0:T(8,128)(2,1)}, bf16[512,768]{1,0:T(8,128)(2,1)}, u32[]{:S(2)}, u32[]{:S(2)}) collective-permute-start(bf16[512,768]{1,0:T(8,128)(2,1)} %get-tuple-element.30), channel_id=1, source_target_pairs={{0,2},{1,3},{2,0},{3,1},{4,6},{5,7},{6,4},{7,5},{8,10},{9,11},{10,... | collective-permute-start | bytes 2359304 | tf_op jit(solution)/shard_map/ppermute | solution.py:24
  47.0 24.1 %copy-start.10 = (f32[256]{0:T(256)S(1)}, f32[256]{0:T(256)}, u32[]{:S(2)}) copy-start(f32[256]{0:T(256)} %param.9) | copy-start | bytes 3076
  47.0 24.1 %copy-start.11 = (f32[256]{0:T(256)S(1)}, f32[256]{0:T(256)}, u32[]{:S(2)}) copy-start(f32[256]{0:T(256)} %param.8) | copy-start | bytes 3076
  49.0 21.9 %all-to-all-start = ((f32[128,4,128]{2,1,0:T(4,128)}), f32[128,4,128]{2,1,0:T(4,128)S(1)}, u32[]{:S(2)}, u32[]{:S(2)}) async-start(f32[128,4,128]{2,1,0:T(4,128)} %broadcast_in_dim.26), calls=%async_computation | async-start | bytes 524288 | tf_op jit(solution)/shard_map/all_to_all | solution.py:39
  59.8 49.1 %collective-permute-start.7 = (bf16[512,768]{1,0:T(8,128)(2,1)S(1)}, bf16[512,768]{1,0:T(8,128)(2,1)}, u32[]{:S(2)}, u32[]{:S(2)}) collective-permute-start(bf16[512,768]{1,0:T(8,128)(2,1)S(1)} %get-tuple-element.32), channel_id=1, source_target_pairs={{0,3},{1,2},{2,1},{3,0},{4,7},{5,6},{6,5},{7,4},{8,11},{9,10},{10,... | collective-permute-start | bytes 2359304 | tf_op jit(solution)/shard_map/ppermute | solution.py:24
  73.7 17.5 %collective-permute-start.9 = (bf16[13,24,256]{2,1,0:T(8,128)(2,1)S(1)}, bf16[13,24,256]{2,1,0:T(8,128)(2,1)}, u32[]{:S(2)}, u32[]{:S(2)}) collective-permute-start(bf16[13,24,256]{2,1,0:T(8,128)(2,1)S(1)} %pad_maximum_fusion.2), channel_id=1, source_target_pairs={{16,0},{32,16},{48,32},{64,48},{80,64},{96,80},{112,96},{17,1},{33... | collective-permute-start | bytes 479240 | tf_op jit(solution)/shard_map/ppermute | solution.py:19
  75.0 17.1 %collective-permute-start.8 = (bf16[13,24,256]{2,1,0:T(8,128)(2,1)S(1)}, bf16[13,24,256]{2,1,0:T(8,128)(2,1)}, u32[]{:S(2)}, u32[]{:S(2)}) collective-permute-start(bf16[13,24,256]{2,1,0:T(8,128)(2,1)S(1)} %pad_maximum_fusion.1), channel_id=1, source_target_pairs={{0,16},{16,32},{32,48},{48,64},{64,80},{80,96},{96,112},{1,17},{17... | collective-permute-start | bytes 479240 | tf_op jit(solution)/shard_map/ppermute | solution.py:19
  83.0 24.6 %all-to-all-start.1 = ((f32[128,3,4,128]{3,2,1,0:T(4,128)}), f32[128,3,4,128]{3,2,1,0:T(4,128)}, u32[]{:S(2)}, u32[]{:S(2)}) async-start(f32[128,3,4,128]{3,2,1,0:T(4,128)} %broadcast_in_dim.32), calls=%async_computation.1 | async-start | bytes 1572864 | tf_op jit(solution)/shard_map/all_to_all | solution.py:39
  110.2 16.6 %collective-permute-start.10 = (bf16[56,24,256]{2,1,0:T(8,128)(2,1)S(1)}, bf16[56,24,256]{2,1,0:T(8,128)(2,1)S(1)}, u32[]{:S(2)}, u32[]{:S(2)}) collective-permute-start(bf16[56,24,256]{2,1,0:T(8,128)(2,1)S(1)} %bitcast.122), channel_id=1, source_target_pairs={{0,2},{1,3},{2,0},{3,1},{4,6},{5,7},{6,4},{7,5},{8,10},{9,11},{10,... | collective-permute-start | bytes 2064392 | tf_op jit(solution)/shard_map/ppermute | solution.py:24
  110.7 28.8 %collective-permute-start.17 = (bf16[512,768]{1,0:T(8,128)(2,1)S(1)}, bf16[512,768]{1,0:T(8,128)(2,1)S(1)}, u32[]{:S(2)}, u32[]{:S(2)}) collective-permute-start(bf16[512,768]{1,0:T(8,128)(2,1)S(1)} %get-tuple-element.35), channel_id=1, source_target_pairs={{0,1},{1,0},{2,3},{3,2},{4,5},{5,4},{6,7},{7,6},{8,9},{9,8},{10,11... | collective-permute-start | bytes 2359304 | tf_op jit(solution)/shard_map/ppermute | solution.py:24
  111.6 17.5 %collective-permute-start.12 = (bf16[56,12,256]{2,1,0:T(8,128)(2,1)S(1)}, bf16[56,12,256]{2,1,0:T(8,128)(2,1)S(1)}, u32[]{:S(2)}, u32[]{:S(2)}) collective-permute-start(bf16[56,12,256]{2,1,0:T(8,128)(2,1)S(1)} %slice_select_fusion), channel_id=1, source_target_pairs={{3,7},{0,12},{7,11},{4,0},{11,15},{8,4},{15,3},{12,8},{19,23},{16,... | collective-permute-start | bytes 1032200 | tf_op jit(solution)/shard_map/ppermute | solution.py:33
  112.3 16.8 %collective-permute-start.11 = (bf16[56,12,256]{2,1,0:T(8,128)(2,1)S(1)}, bf16[56,12,256]{2,1,0:T(8,128)(2,1)S(1)}, u32[]{:S(2)}, u32[]{:S(2)}) collective-permute-start(bf16[56,12,256]{2,1,0:T(8,128)(2,1)S(1)} %slice_select_fusion), channel_id=1, source_target_pairs={{3,4},{0,15},{7,8},{4,3},{11,12},{8,7},{15,0},{12,11},{19,20},{16,... | collective-permute-start | bytes 1032200 | tf_op jit(solution)/shard_map/ppermute | solution.py:33
  113.0 21.4 %collective-permute-start.13 = (bf16[56,24,256]{2,1,0:T(8,128)(2,1)S(1)}, bf16[56,24,256]{2,1,0:T(8,128)(2,1)S(1)}, u32[]{:S(2)}, u32[]{:S(2)}) collective-permute-start(bf16[56,24,256]{2,1,0:T(8,128)(2,1)S(1)} %bitcast.124), channel_id=1, source_target_pairs={{0,1},{1,0},{2,3},{3,2},{4,5},{5,4},{6,7},{7,6},{8,9},{9,8},{10,11... | collective-permute-start | bytes 2064392 | tf_op jit(solution)/shard_map/ppermute | solution.py:24
  126.9 7.6 %collective-permute-start.14 = (bf16[56,24,256]{2,1,0:T(8,128)(2,1)S(1)}, bf16[56,24,256]{2,1,0:T(8,128)(2,1)S(1)}, u32[]{:S(2)}, u32[]{:S(2)}) collective-permute-start(bf16[56,24,256]{2,1,0:T(8,128)(2,1)S(1)} %collective-permute-done.10.refs_1_), channel_id=1, source_target_pairs={{0,1},{1,0},{2,3},{3,2},{4,5},{5,4},{6,7},{7,6},{8,9},{9,8},{10,11... | collective-permute-start | bytes 2064392 | tf_op jit(solution)/shard_map/ppermute | solution.py:24
  129.1 3.9 %collective-permute-start.16 = (bf16[56,12,256]{2,1,0:T(8,128)(2,1)S(1)}, bf16[56,12,256]{2,1,0:T(8,128)(2,1)S(1)}, u32[]{:S(2)}, u32[]{:S(2)}) collective-permute-start(bf16[56,12,256]{2,1,0:T(8,128)(2,1)S(1)} %collective-permute-done.12.refs_3_), channel_id=1, source_target_pairs={{0,1},{1,0},{2,3},{3,2},{4,5},{5,4},{6,7},{7,6},{8,9},{9,8},{10,11... | collective-permute-start | bytes 1032200 | tf_op jit(solution)/shard_map/ppermute | solution.py:24
  129.1 5.4 %collective-permute-start.15 = (bf16[56,12,256]{2,1,0:T(8,128)(2,1)S(1)}, bf16[56,12,256]{2,1,0:T(8,128)(2,1)S(1)}, u32[]{:S(2)}, u32[]{:S(2)}) collective-permute-start(bf16[56,12,256]{2,1,0:T(8,128)(2,1)S(1)} %collective-permute-done.11.refs_2_), channel_id=1, source_target_pairs={{0,1},{1,0},{2,3},{3,2},{4,5},{5,4},{6,7},{7,6},{8,9},{9,8},{10,11... | collective-permute-start | bytes 1032200 | tf_op jit(solution)/shard_map/ppermute | solution.py:24
  152.9 37.7 %all-to-all-start.2 = ((bf16[128,72,128]{2,1,0:T(8,128)(2,1)}), bf16[128,72,128]{2,1,0:T(8,128)(2,1)S(1)}, u32[]{:S(2)}, u32[]{:S(2)}) async-start(bf16[128,72,128]{2,1,0:T(8,128)(2,1)} %bitcast.132), calls=%async_computation.2 | async-start | bytes 4718592 | tf_op jit(solution)/shard_map/all_to_all | solution.py:346
  (11 other events, 46.7 us)

commit v4 on v3

--- a/solution.py
+++ b/solution.py
@@ -35,8 +35,10 @@
 
 def total(x):
     count = lax.axis_size("lat") * lax.axis_size("lon")
-    spread = jnp.broadcast_to(x[None], (count,) + x.shape)
-    return jnp.sum(lax.all_to_all(spread, ("lat", "lon"), 0, 0), 0)
+    groups = [list(range(core, count, 2)) for core in range(2)]
+    x = x + swap(x, 1)
+    spread = jnp.broadcast_to(x[None], (count // 2,) + x.shape)
+    return jnp.sum(lax.all_to_all(spread, ("lat", "lon"), 0, 0, axis_index_groups=groups), 0)
 
 
 def outer_rows(flat, weight, edge):
@@ -325,16 +327,14 @@
     scale = norm_gain * inverse
     slope = inverse * grad_gain
     shift = slope * norm_bias - scale * grad_bias
-    d_own = (scale * (d_preact - grad_bias - normed * grad_gain)).astype(BF)
-
-    def halo(pre, exists):
-        lab = pre[RATE, :, :RATE].T.astype(jnp.int32)
-        wide = pre[:RATE].astype(F32).reshape(step_rows, filters)
-        d_pre = head(wide, lab.reshape(step_rows), head_weight)[-1]
-        d = scale * d_pre - slope * wide + shift
-        return jnp.where(exists, d, 0.0).astype(BF)
-
-    d_col = jnp.concatenate([halo(pre_n, lat > 0), d_own, halo(pre_s, lat < lats - 1)], 0)
+    d_mid = (scale * (d_preact - grad_bias - normed * grad_gain)).astype(BF)
+    wide = jnp.concatenate([pre_n[:RATE], pre_s[:RATE]], 0).astype(F32).reshape(2 * step_rows, filters)
+    lab = jnp.concatenate([pre_n[RATE, :, :RATE], pre_s[RATE, :, :RATE]], 1).T.astype(jnp.int32)
+    d_pre = head(wide, lab.reshape(2 * step_rows), head_weight)[-1]
+    north = jnp.arange(2 * step_rows)[:, None] < step_rows
+    exists = jnp.where(north, lat > 0, lat < lats - 1)
+    d_halo = jnp.where(exists, scale * d_pre - slope * wide + shift, 0.0).astype(BF)
+    d_col = jnp.concatenate([d_halo[:step_rows], d_mid, d_halo[step_rows:]], 0)
     d_col = d_col.reshape(height + 2 * RATE, breadth, filters)
     strip = jnp.where(place == 0, d_col[:, :RATE], d_col[:, breadth - RATE :])
     mine = (d_col, swap(d_col, 2), to_groups(strip, 1), to_groups(strip, 4))

time: 193 us -> 191 us (0.990)
  waiting for transfers between devices: 52.6 us -> 38.6 us
  starting transfers between devices: 62.3 us -> 67.4 us
  local copies, waits for them, and re-layouts: 14.8 us -> 18.5 us
  other arithmetic: 7.25 us -> 9.2 us
    all_to_all x2, waiting for transfers between devices: 21.6 us -> 9.45 us  [total(): lax.all_to_all(spread, ('lat', 'lon'), 0, 0, axis_index_groups=groups)]
    ppermute x8 -> x10, starting transfers between devices: 17.8 us -> 24.5 us  [swap(): return lax.ppermute(x, 'lon', [(i, i ^ mask) for i in range(count)])]
    all_to_all x2, starting transfers between devices: 18.7 us -> 16 us  [total(): lax.all_to_all(spread, ('lat', 'lon'), 0, 0, axis_index_groups=groups)]
    ppermute x8 -> x10, waiting for transfers between devices: 8.98 us -> 7.14 us  [swap(): return lax.ppermute(x, 'lon', [(i, i ^ mask) for i in range(count)])]
    unnamed x29 -> x45, local copies, waits for them, and re-layouts: 3.8 us -> 4.55 us
  transfers between devices with their start and end apart: 21 -> 23, of which waited for: 6 -> 7; matrix products, arithmetic and copies ran while one was open for 10% -> 12% of each run, Pallas kernels for 17% -> 17%
where the time goes in v4:
time: 191 us; the launch traced here: 190 us
  starting transfers between devices  67.4 us (35%)
  Pallas kernels  50.5 us (26%)
  waiting for transfers between devices  38.6 us (20%)
  local copies, waits for them, and re-layouts  18.5 us (10%)
  other arithmetic  9.2 us (5%)
  matrix products  4.78 us (3%)
    ppermute x10, starting transfers between devices, swap(): return lax.ppermute(x, 'lon', [(i, i ^ mask) for i in range(count)])  24.5 us
    ppermute x8, starting transfers between devices, ring(): return lax.ppermute(x, axis, pairs)  19.8 us
    all_to_all x1, waiting for transfers between devices, shards(): got = lax.all_to_all(blocks, ('lat', 'lon'), 0, 0)  19.3 us
    all_to_all x2, starting transfers between devices, total(): lax.all_to_all(spread, ('lat', 'lon'), 0, 0, axis_index_groups=groups)  16 us
    pallas_call x1, Pallas kernels, grad_kernel(): pl.pallas_call(body, grid=(3,), in_specs=[pl.BlockSpec((1,) + d_all.shape...  12.4 us
    pallas_call x2, Pallas kernels, inner_rows(): pl.pallas_call(body, grid=(len(cols), 3), in_specs=[pl.BlockSpec((cells,...  11.4 us
    pallas_call x1, Pallas kernels, grad_input(): pl.pallas_call(body, grid=(channels // block,), in_specs=[pl.BlockSpec(dc...  10.7 us
    all_to_all x2, waiting for transfers between devices, total(): lax.all_to_all(spread, ('lat', 'lon'), 0, 0, axis_index_groups=groups)  9.45 us
  transfers between devices with their start and end apart: 23, of which 7 were waited for; matrix products, arithmetic and copies ran while one was open for 12% of the time, Pallas kernels for 17%

profile of v4, /device:TPU:1, one launch (start us, length us, event | category | flops | bytes accessed | tf_op | source)
XLA Modules:
  0.0 190.1 jit_solution(6526057506221556689)
XLA Ops:
  2.5 5.8 %shard_map.109 = f32[2,3,288,256]{3,2,1,0:T(8,128)S(1)} custom-call(bf16[768,2048]{1,0:T(8,128)(2,1)S(1)} %bitcast.100, bf16[9,2048,256]{2,1,0:T(8,128)(2,1)} %bitcast.113), custom_call_target="tpu_custom_call" | custom-call | tf_op jit(solution)/shard_map/pallas_call | solution.py:52
  8.4 2.8 %collective-permute-start.2 = (f32[2,12,12,256]{3,2,1,0:T(8,128)S(1)}, f32[2,12,12,256]{3,2,1,0:T(8,128)S(1)}, u32[]{:S(2)}, u32[]{:S(2)}) collective-permute-start(f32[2,12,12,256]{3,2,1,0:T(8,128)S(1)} %get-tuple-element.51), channel_id=1, source_target_pairs={{0,1},{1,2},{2,3},{3,4},{4,5},{5,6},{6,7},{7,8},{8,9},{9,10},{10,1... | collective-permute-start | bytes 884744 | tf_op jit(solution)/shard_map/ppermute | solution.py:19
  11.2 7.2 %shard_map.111 = f32[2,768,256]{2,1,0:T(8,128)S(1)} custom-call(bf16[768,2048]{1,0:T(8,128)(2,1)S(1)} %bitcast.101, bf16[9,2048,256]{2,1,0:T(8,128)(2,1)} %bitcast.114), custom_call_target="tpu_custom_call" | custom-call | tf_op jit(solution)/shard_map/pallas_call | solution.py:88
  19.6 3.4 %collective-permute-start.1 = (f32[32,12,256]{2,1,0:T(8,128)}, f32[32,12,256]{2,1,0:T(8,128)}, u32[]{:S(2)}, u32[]{:S(2)}) collective-permute-start(f32[32,12,256]{2,1,0:T(8,128)} %get-tuple-element.55), channel_id=1, source_target_pairs={{0,15},{1,0},{2,1},{3,2},{4,3},{5,4},{6,5},{7,6},{8,7},{9,8},{10,9... | collective-permute-start | bytes 1179656 | tf_op jit(solution)/shard_map/ppermute | solution.py:19
  24.2 4.7 %collective-permute-start.4 = (f32[12,24,256]{2,1,0:T(8,128)}, f32[12,24,256]{2,1,0:T(8,128)S(1)}, u32[]{:S(2)}, u32[]{:S(2)}) collective-permute-start(f32[12,24,256]{2,1,0:T(8,128)} %get-tuple-element.57), channel_id=1, source_target_pairs={{0,16},{16,32},{32,48},{48,64},{64,80},{80,96},{96,112},{1,17},{17... | collective-permute-start | bytes 884744 | tf_op jit(solution)/shard_map/ppermute | solution.py:19
  30.2 4.2 %shard_map.110 = f32[1,768,256]{2,1,0:T(8,128)S(1)} custom-call(bf16[768,2048]{1,0:T(8,128)(2,1)S(1)} %bitcast.102, bf16[9,2048,256]{2,1,0:T(8,128)(2,1)} %bitcast.115), custom_call_target="tpu_custom_call" | custom-call | tf_op jit(solution)/shard_map/pallas_call | solution.py:88
  35.4 5.1 %shard_map.112 = (bf16[512,768]{1,0:T(8,128)(2,1)S(1)}, bf16[512,768]{1,0:T(8,128)(2,1)S(1)}, bf16[512,768]{1,0:T(8,128)(2,1)}, bf16[512,768]{1,0:T(8,128)(2,1)S(1)}) custom-call(s32[1]{0:T(128)} %bitcast.8.where_ref.place_ref, bf16[768,2048]{1,0:T(8,128)(2,1)} %bitcast.99), custom_call_target="tpu_custom_call" | custom-call | tf_op jit(solution)/shard_map/pallas_call | solution.py:118
  40.5 2.3 %collective-permute-start.7 = (bf16[512,768]{1,0:T(8,128)(2,1)}, bf16[512,768]{1,0:T(8,128)(2,1)}, u32[]{:S(2)}, u32[]{:S(2)}) collective-permute-start(bf16[512,768]{1,0:T(8,128)(2,1)} %get-tuple-element.30), channel_id=1, source_target_pairs={{0,2},{1,3},{2,0},{3,1},{4,6},{5,7},{6,4},{7,5},{8,10},{9,11},{10,... | collective-permute-start | bytes 2359304 | tf_op jit(solution)/shard_map/ppermute | solution.py:24
  44.2 2.7 %collective-permute-done.4 = f32[12,24,256]{2,1,0:T(8,128)S(1)} collective-permute-done((f32[12,24,256]{2,1,0:T(8,128)}, f32[12,24,256]{2,1,0:T(8,128)S(1)}, u32[]{:S(2)}, u32[]{:S(2)}) %collective-permute-start.4) | collective-permute-done | bytes 294944 | tf_op jit(solution)/shard_map/ppermute | solution.py:19
  48.2 2.1 %collective-permute-start.6 = (f32[4,128]{1,0:T(4,128)S(1)}, f32[4,128]{1,0:T(4,128)S(1)}, u32[]{:S(2)}, u32[]{:S(2)}) collective-permute-start(f32[4,128]{1,0:T(4,128)S(1)} %reshape.151), channel_id=1, source_target_pairs={{0,1},{1,0},{2,3},{3,2},{4,5},{5,4},{6,7},{7,6},{8,9},{9,8},{10,11... | collective-permute-start | bytes 6152 | tf_op jit(solution)/shard_map/ppermute | solution.py:24
  51.8 9.6 %all-to-all-start = ((f32[64,4,128]{2,1,0:T(4,128)}), f32[64,4,128]{2,1,0:T(4,128)S(1)}, u32[]{:S(2)}, u32[]{:S(2)}) async-start(f32[64,4,128]{2,1,0:T(4,128)} %broadcast_in_dim.32), calls=%async_computation | async-start | bytes 262144 | tf_op jit(solution)/shard_map/all_to_all | solution.py:41
  64.1 6.1 %all-to-all-done = f32[64,4,128]{2,1,0:T(4,128)S(1)} async-done(((f32[64,4,128]{2,1,0:T(4,128)}), f32[64,4,128]{2,1,0:T(4,128)S(1)}, u32[]{:S(2)}, u32[]{:S(2)}) %all-to-all-start) | async-done | bytes 131104 | tf_op jit(solution)/shard_map/all_to_all | solution.py:41
  78.6 6.4 %collective-permute-start.10 = (bf16[13,24,256]{2,1,0:T(8,128)(2,1)}, bf16[13,24,256]{2,1,0:T(8,128)(2,1)}, u32[]{:S(2)}, u32[]{:S(2)}) collective-permute-start(bf16[13,24,256]{2,1,0:T(8,128)(2,1)} %pad_maximum_fusion.2), channel_id=1, source_target_pairs={{0,16},{16,32},{32,48},{48,64},{64,80},{80,96},{96,112},{1,17},{17... | collective-permute-start | bytes 479240 | tf_op jit(solution)/shard_map/ppermute | solution.py:19
  85.8 6.4 %all-to-all-start.1 = ((f32[64,3,4,128]{3,2,1,0:T(4,128)}), f32[64,3,4,128]{3,2,1,0:T(4,128)S(1)}, u32[]{:S(2)}, u32[]{:S(2)}) async-start(f32[64,3,4,128]{3,2,1,0:T(4,128)} %broadcast_in_dim.36), calls=%async_computation.1 | async-start | bytes 786432 | tf_op jit(solution)/shard_map/all_to_all | solution.py:41
  100.0 3.4 %all-to-all-done.1 = f32[64,3,4,128]{3,2,1,0:T(4,128)S(1)} async-done(((f32[64,3,4,128]{3,2,1,0:T(4,128)}), f32[64,3,4,128]{3,2,1,0:T(4,128)S(1)}, u32[]{:S(2)}, u32[]{:S(2)}) %all-to-all-start.1) | async-done | bytes 393248 | tf_op jit(solution)/shard_map/all_to_all | solution.py:41
  111.0 6.7 %collective-permute-start.15 = (bf16[56,24,256]{2,1,0:T(8,128)(2,1)S(1)}, bf16[56,24,256]{2,1,0:T(8,128)(2,1)S(1)}, u32[]{:S(2)}, u32[]{:S(2)}) collective-permute-start(bf16[56,24,256]{2,1,0:T(8,128)(2,1)S(1)} %bitcast.110), channel_id=1, source_target_pairs={{0,1},{1,0},{2,3},{3,2},{4,5},{5,4},{6,7},{7,6},{8,9},{9,8},{10,11... | collective-permute-start | bytes 2064392 | tf_op jit(solution)/shard_map/ppermute | solution.py:24
  117.7 4.9 %collective-permute-done.12.refs_1_ = bf16[56,24,256]{2,1,0:T(8,128)(2,1)S(1)} collective-permute-done((bf16[56,24,256]{2,1,0:T(8,128)(2,1)S(1)}, bf16[56,24,256]{2,1,0:T(8,128)(2,1)S(1)}, u32[]{:S(2)}, u32[]{:S(2)}) %collective-permute-start.12) | collective-permute-done | bytes 688160 | tf_op jit(solution)/shard_map/ppermute | solution.py:24
  122.6 4.9 %collective-permute-start.16 = (bf16[56,24,256]{2,1,0:T(8,128)(2,1)S(1)}, bf16[56,24,256]{2,1,0:T(8,128)(2,1)S(1)}, u32[]{:S(2)}, u32[]{:S(2)}) collective-permute-start(bf16[56,24,256]{2,1,0:T(8,128)(2,1)S(1)} %collective-permute-done.12.refs_1_), channel_id=1, source_target_pairs={{0,1},{1,0},{2,3},{3,2},{4,5},{5,4},{6,7},{7,6},{8,9},{9,8},{10,11... | collective-permute-start | bytes 2064392 | tf_op jit(solution)/shard_map/ppermute | solution.py:24
  127.5 2.6 %collective-permute-start.17 = (bf16[56,12,256]{2,1,0:T(8,128)(2,1)S(1)}, bf16[56,12,256]{2,1,0:T(8,128)(2,1)S(1)}, u32[]{:S(2)}, u32[]{:S(2)}) collective-permute-start(bf16[56,12,256]{2,1,0:T(8,128)(2,1)S(1)} %collective-permute-done.13.refs_2_), channel_id=1, source_target_pairs={{0,1},{1,0},{2,3},{3,2},{4,5},{5,4},{6,7},{7,6},{8,9},{9,8},{10,11... | collective-permute-start | bytes 1032200 | tf_op jit(solution)/shard_map/ppermute | solution.py:24
  131.6 5.0 %shard_map.113.d_ref = bf16[3,4,1344,256]{3,2,1,0:T(8,128)(2,1)} custom-call(s32[1]{0:T(128)} %bitcast.8.where_ref.place_ref, bf16[56,24,256]{2,1,0:T(8,128)(2,1)S(1)} %bitcast.111, bf16[56,24,256]{2,1,0:T(8,128)(2,1)S(1)} %collective-permute-done.12.refs_1_, bf16[56,12,256]{2,1,0:T(8,128)(2,1)S(1)} %collective-permute-done.13.refs_2_, ...), custom_call_target="tpu_custom_call" | custom-call | tf_op jit(solution)/shard_map/pallas_call | solution.py:157
  137.5 12.4 %shard_map.115 = bf16[8,16,3,3,8,128]{5,4,3,2,1,0:T(8,128)(2,1)} custom-call(bf16[3,4,1344,256]{3,2,1,0:T(8,128)(2,1)} %shard_map.113.d_ref, bf16[512,768]{1,0:T(8,128)(2,1)} %copy-done.7, bf16[512,768]{1,0:T(8,128)(2,1)} %copy-done.10, bf16[512,768]{1,0:T(8,128)(2,1)} %collective-permute-done.7.refs_2_, bf16[512,768]{1,0:T(8,128)(2,1)} %collective-permute-done.9.refs_3_), custom_call_target="tpu_custom_call" | custom-call | tf_op jit(solution)/shard_map/pallas_call | solution.py:197
  149.9 5.7 %all-to-all-start.2 = ((bf16[128,72,128]{2,1,0:T(8,128)(2,1)}), bf16[128,72,128]{2,1,0:T(8,128)(2,1)S(1)}, u32[]{:S(2)}, u32[]{:S(2)}) async-start(bf16[128,72,128]{2,1,0:T(8,128)(2,1)} %bitcast.118), calls=%async_computation.2 | async-start | bytes 4718592 | tf_op jit(solution)/shard_map/all_to_all | solution.py:346
  158.5 10.7 %shard_map.114 = bf16[768,2048]{1,0:T(8,128)(2,1)} custom-call(bf16[3,1344,256]{2,1,0:T(8,128)(2,1)S(1)} %slice_bitcast_fusion.d_ref, bf16[9,2048,256]{2,1,0:T(8,128)(2,1)} %bitcast.116), custom_call_target="tpu_custom_call" | custom-call | tf_op jit(solution)/shard_map/pallas_call | solution.py:225
  169.2 19.3 %all-to-all-done.2 = bf16[128,72,128]{2,1,0:T(8,128)(2,1)S(1)} async-done(((bf16[128,72,128]{2,1,0:T(8,128)(2,1)}), bf16[128,72,128]{2,1,0:T(8,128)(2,1)S(1)}, u32[]{:S(2)}, u32[]{:S(2)}) %all-to-all-start.2) | async-done | bytes 2359328 | tf_op jit(solution)/shard_map/all_to_all | solution.py:346
  (134 shorter events, 44.5 us)
Async XLA Ops:
  0.6 70.3 %copy-start = (f32[3,256]{1,0:T(4,128)S(1)}, f32[3,256]{1,0:T(4,128)}, u32[]{:S(2)}) copy-start(f32[3,256]{1,0:T(4,128)} %param.10) | copy-start | bytes 9220
  8.4 14.6 %collective-permute-start.2 = (f32[2,12,12,256]{3,2,1,0:T(8,128)S(1)}, f32[2,12,12,256]{3,2,1,0:T(8,128)S(1)}, u32[]{:S(2)}, u32[]{:S(2)}) collective-permute-start(f32[2,12,12,256]{3,2,1,0:T(8,128)S(1)} %get-tuple-element.51), channel_id=1, source_target_pairs={{0,1},{1,2},{2,3},{3,4},{4,5},{5,6},{6,7},{7,8},{8,9},{9,10},{10,1... | collective-permute-start | bytes 884744 | tf_op jit(solution)/shard_map/ppermute | solution.py:19
  11.2 11.9 %collective-permute-start.3 = (f32[2,12,12,256]{3,2,1,0:T(8,128)S(1)}, f32[2,12,12,256]{3,2,1,0:T(8,128)S(1)}, u32[]{:S(2)}, u32[]{:S(2)}) collective-permute-start(f32[2,12,12,256]{3,2,1,0:T(8,128)S(1)} %get-tuple-element.52), channel_id=1, source_target_pairs={{0,15},{1,0},{2,1},{3,2},{4,3},{5,4},{6,5},{7,6},{8,7},{9,8},{10,9... | collective-permute-start | bytes 884744 | tf_op jit(solution)/shard_map/ppermute | solution.py:19
  19.6 20.8 %collective-permute-start.1 = (f32[32,12,256]{2,1,0:T(8,128)}, f32[32,12,256]{2,1,0:T(8,128)}, u32[]{:S(2)}, u32[]{:S(2)}) collective-permute-start(f32[32,12,256]{2,1,0:T(8,128)} %get-tuple-element.55), channel_id=1, source_target_pairs={{0,15},{1,0},{2,1},{3,2},{4,3},{5,4},{6,5},{7,6},{8,7},{9,8},{10,9... | collective-permute-start | bytes 1179656 | tf_op jit(solution)/shard_map/ppermute | solution.py:19
  23.0 17.4 %collective-permute-start = (f32[32,12,256]{2,1,0:T(8,128)}, f32[32,12,256]{2,1,0:T(8,128)}, u32[]{:S(2)}, u32[]{:S(2)}) collective-permute-start(f32[32,12,256]{2,1,0:T(8,128)} %get-tuple-element.56), channel_id=1, source_target_pairs={{0,1},{1,2},{2,3},{3,4},{4,5},{5,6},{6,7},{7,8},{8,9},{9,10},{10,1... | collective-permute-start | bytes 1179656 | tf_op jit(solution)/shard_map/ppermute | solution.py:19
  24.2 22.7 %collective-permute-start.4 = (f32[12,24,256]{2,1,0:T(8,128)}, f32[12,24,256]{2,1,0:T(8,128)S(1)}, u32[]{:S(2)}, u32[]{:S(2)}) collective-permute-start(f32[12,24,256]{2,1,0:T(8,128)} %get-tuple-element.57), channel_id=1, source_target_pairs={{0,16},{16,32},{32,48},{48,64},{64,80},{80,96},{96,112},{1,17},{17... | collective-permute-start | bytes 884744 | tf_op jit(solution)/shard_map/ppermute | solution.py:19
  28.9 18.0 %collective-permute-start.5 = (f32[12,24,256]{2,1,0:T(8,128)}, f32[12,24,256]{2,1,0:T(8,128)}, u32[]{:S(2)}, u32[]{:S(2)}) collective-permute-start(f32[12,24,256]{2,1,0:T(8,128)} %get-tuple-element.58), channel_id=1, source_target_pairs={{16,0},{32,16},{48,32},{64,48},{80,64},{96,80},{112,96},{17,1},{33... | collective-permute-start | bytes 884744 | tf_op jit(solution)/shard_map/ppermute | solution.py:19
  40.5 29.7 %collective-permute-start.7 = (bf16[512,768]{1,0:T(8,128)(2,1)}, bf16[512,768]{1,0:T(8,128)(2,1)}, u32[]{:S(2)}, u32[]{:S(2)}) collective-permute-start(bf16[512,768]{1,0:T(8,128)(2,1)} %get-tuple-element.30), channel_id=1, source_target_pairs={{0,2},{1,3},{2,0},{3,1},{4,6},{5,7},{6,4},{7,5},{8,10},{9,11},{10,... | collective-permute-start | bytes 2359304 | tf_op jit(solution)/shard_map/ppermute | solution.py:24
  48.2 2.9 %collective-permute-start.6 = (f32[4,128]{1,0:T(4,128)S(1)}, f32[4,128]{1,0:T(4,128)S(1)}, u32[]{:S(2)}, u32[]{:S(2)}) collective-permute-start(f32[4,128]{1,0:T(4,128)S(1)} %reshape.151), channel_id=1, source_target_pairs={{0,1},{1,0},{2,3},{3,2},{4,5},{5,4},{6,7},{7,6},{8,9},{9,8},{10,11... | collective-permute-start | bytes 6152 | tf_op jit(solution)/shard_map/ppermute | solution.py:24
  51.8 18.3 %all-to-all-start = ((f32[64,4,128]{2,1,0:T(4,128)}), f32[64,4,128]{2,1,0:T(4,128)S(1)}, u32[]{:S(2)}, u32[]{:S(2)}) async-start(f32[64,4,128]{2,1,0:T(4,128)} %broadcast_in_dim.32), calls=%async_computation | async-start | bytes 262144 | tf_op jit(solution)/shard_map/all_to_all | solution.py:41
  62.2 41.9 %collective-permute-start.9 = (bf16[512,768]{1,0:T(8,128)(2,1)S(1)}, bf16[512,768]{1,0:T(8,128)(2,1)}, u32[]{:S(2)}, u32[]{:S(2)}) collective-permute-start(bf16[512,768]{1,0:T(8,128)(2,1)S(1)} %get-tuple-element.32), channel_id=1, source_target_pairs={{0,3},{1,2},{2,1},{3,0},{4,7},{5,6},{6,5},{7,4},{8,11},{9,10},{10,... | collective-permute-start | bytes 2359304 | tf_op jit(solution)/shard_map/ppermute | solution.py:24
  74.0 18.2 %collective-permute-start.11 = (bf16[13,24,256]{2,1,0:T(8,128)(2,1)}, bf16[13,24,256]{2,1,0:T(8,128)(2,1)}, u32[]{:S(2)}, u32[]{:S(2)}) collective-permute-start(bf16[13,24,256]{2,1,0:T(8,128)(2,1)} %pad_maximum_fusion.3), channel_id=1, source_target_pairs={{16,0},{32,16},{48,32},{64,48},{80,64},{96,80},{112,96},{17,1},{33... | collective-permute-start | bytes 479240 | tf_op jit(solution)/shard_map/ppermute | solution.py:19
  76.1 8.9 %collective-permute-start.8 = (f32[3,4,128]{2,1,0:T(4,128)S(1)}, f32[3,4,128]{2,1,0:T(4,128)S(1)}, u32[]{:S(2)}, u32[]{:S(2)}) collective-permute-start(f32[3,4,128]{2,1,0:T(4,128)S(1)} %reshape.152), channel_id=1, source_target_pairs={{0,1},{1,0},{2,3},{3,2},{4,5},{5,4},{6,7},{7,6},{8,9},{9,8},{10,11... | collective-permute-start | bytes 18440 | tf_op jit(solution)/shard_map/ppermute | solution.py:24
  78.6 14.4 %collective-permute-start.10 = (bf16[13,24,256]{2,1,0:T(8,128)(2,1)}, bf16[13,24,256]{2,1,0:T(8,128)(2,1)}, u32[]{:S(2)}, u32[]{:S(2)}) collective-permute-start(bf16[13,24,256]{2,1,0:T(8,128)(2,1)} %pad_maximum_fusion.2), channel_id=1, source_target_pairs={{0,16},{16,32},{32,48},{48,64},{64,80},{80,96},{96,112},{1,17},{17... | collective-permute-start | bytes 479240 | tf_op jit(solution)/shard_map/ppermute | solution.py:19
  85.8 17.5 %all-to-all-start.1 = ((f32[64,3,4,128]{3,2,1,0:T(4,128)}), f32[64,3,4,128]{3,2,1,0:T(4,128)S(1)}, u32[]{:S(2)}, u32[]{:S(2)}) async-start(f32[64,3,4,128]{3,2,1,0:T(4,128)} %broadcast_in_dim.36), calls=%async_computation.1 | async-start | bytes 786432 | tf_op jit(solution)/shard_map/all_to_all | solution.py:41
  107.3 15.3 %collective-permute-start.12 = (bf16[56,24,256]{2,1,0:T(8,128)(2,1)S(1)}, bf16[56,24,256]{2,1,0:T(8,128)(2,1)S(1)}, u32[]{:S(2)}, u32[]{:S(2)}) collective-permute-start(bf16[56,24,256]{2,1,0:T(8,128)(2,1)S(1)} %bitcast.108), channel_id=1, source_target_pairs={{0,2},{1,3},{2,0},{3,1},{4,6},{5,7},{6,4},{7,5},{8,10},{9,11},{10,... | collective-permute-start | bytes 2064392 | tf_op jit(solution)/shard_map/ppermute | solution.py:24
  107.4 29.2 %collective-permute-start.19 = (bf16[512,768]{1,0:T(8,128)(2,1)S(1)}, bf16[512,768]{1,0:T(8,128)(2,1)S(1)}, u32[]{:S(2)}, u32[]{:S(2)}) collective-permute-start(bf16[512,768]{1,0:T(8,128)(2,1)S(1)} %get-tuple-element.35), channel_id=1, source_target_pairs={{0,1},{1,0},{2,3},{3,2},{4,5},{5,4},{6,7},{7,6},{8,9},{9,8},{10,11... | collective-permute-start | bytes 2359304 | tf_op jit(solution)/shard_map/ppermute | solution.py:24
  109.6 17.9 %collective-permute-start.14 = (bf16[56,12,256]{2,1,0:T(8,128)(2,1)S(1)}, bf16[56,12,256]{2,1,0:T(8,128)(2,1)S(1)}, u32[]{:S(2)}, u32[]{:S(2)}) collective-permute-start(bf16[56,12,256]{2,1,0:T(8,128)(2,1)S(1)} %slice_select_fusion), channel_id=1, source_target_pairs={{3,7},{0,12},{7,11},{4,0},{11,15},{8,4},{15,3},{12,8},{19,23},{16,... | collective-permute-start | bytes 1032200 | tf_op jit(solution)/shard_map/ppermute | solution.py:33
  110.3 17.2 %collective-permute-start.13 = (bf16[56,12,256]{2,1,0:T(8,128)(2,1)S(1)}, bf16[56,12,256]{2,1,0:T(8,128)(2,1)S(1)}, u32[]{:S(2)}, u32[]{:S(2)}) collective-permute-start(bf16[56,12,256]{2,1,0:T(8,128)(2,1)S(1)} %slice_select_fusion), channel_id=1, source_target_pairs={{3,4},{0,15},{7,8},{4,3},{11,12},{8,7},{15,0},{12,11},{19,20},{16,... | collective-permute-start | bytes 1032200 | tf_op jit(solution)/shard_map/ppermute | solution.py:33
  111.0 20.5 %collective-permute-start.15 = (bf16[56,24,256]{2,1,0:T(8,128)(2,1)S(1)}, bf16[56,24,256]{2,1,0:T(8,128)(2,1)S(1)}, u32[]{:S(2)}, u32[]{:S(2)}) collective-permute-start(bf16[56,24,256]{2,1,0:T(8,128)(2,1)S(1)} %bitcast.110), channel_id=1, source_target_pairs={{0,1},{1,0},{2,3},{3,2},{4,5},{5,4},{6,7},{7,6},{8,9},{9,8},{10,11... | collective-permute-start | bytes 2064392 | tf_op jit(solution)/shard_map/ppermute | solution.py:24
  122.6 9.0 %collective-permute-start.16 = (bf16[56,24,256]{2,1,0:T(8,128)(2,1)S(1)}, bf16[56,24,256]{2,1,0:T(8,128)(2,1)S(1)}, u32[]{:S(2)}, u32[]{:S(2)}) collective-permute-start(bf16[56,24,256]{2,1,0:T(8,128)(2,1)S(1)} %collective-permute-done.12.refs_1_), channel_id=1, source_target_pairs={{0,1},{1,0},{2,3},{3,2},{4,5},{5,4},{6,7},{7,6},{8,9},{9,8},{10,11... | collective-permute-start | bytes 2064392 | tf_op jit(solution)/shard_map/ppermute | solution.py:24
  127.5 2.6 %collective-permute-start.18 = (bf16[56,12,256]{2,1,0:T(8,128)(2,1)S(1)}, bf16[56,12,256]{2,1,0:T(8,128)(2,1)S(1)}, u32[]{:S(2)}, u32[]{:S(2)}) collective-permute-start(bf16[56,12,256]{2,1,0:T(8,128)(2,1)S(1)} %collective-permute-done.14.refs_3_), channel_id=1, source_target_pairs={{0,1},{1,0},{2,3},{3,2},{4,5},{5,4},{6,7},{7,6},{8,9},{9,8},{10,11... | collective-permute-start | bytes 1032200 | tf_op jit(solution)/shard_map/ppermute | solution.py:24
  127.5 4.0 %collective-permute-start.17 = (bf16[56,12,256]{2,1,0:T(8,128)(2,1)S(1)}, bf16[56,12,256]{2,1,0:T(8,128)(2,1)S(1)}, u32[]{:S(2)}, u32[]{:S(2)}) collective-permute-start(bf16[56,12,256]{2,1,0:T(8,128)(2,1)S(1)} %collective-permute-done.13.refs_2_), channel_id=1, source_target_pairs={{0,1},{1,0},{2,3},{3,2},{4,5},{5,4},{6,7},{7,6},{8,9},{9,8},{10,11... | collective-permute-start | bytes 1032200 | tf_op jit(solution)/shard_map/ppermute | solution.py:24
  149.9 38.6 %all-to-all-start.2 = ((bf16[128,72,128]{2,1,0:T(8,128)(2,1)}), bf16[128,72,128]{2,1,0:T(8,128)(2,1)S(1)}, u32[]{:S(2)}, u32[]{:S(2)}) async-start(bf16[128,72,128]{2,1,0:T(8,128)(2,1)} %bitcast.118), calls=%async_computation.2 | async-start | bytes 4718592 | tf_op jit(solution)/shard_map/all_to_all | solution.py:346
  (21 other events, 133.4 us)

commit v5 on v4

--- a/solution.py
+++ b/solution.py
@@ -1,3 +1,5 @@
+import math
+
 import jax
 import jax.numpy as jnp
 from jax import lax
@@ -33,6 +35,11 @@
     return lax.ppermute(x, "lon", pairs)
 
 
+def cost(flops, *arrays):
+    size = sum(math.prod(x.shape) * x.dtype.itemsize for x in arrays)
+    return pl.CostEstimate(flops=flops, transcendentals=0, bytes_accessed=size)
+
+
 def total(x):
     count = lax.axis_size("lat") * lax.axis_size("lon")
     groups = [list(range(core, count, 2)) for core in range(2)]
@@ -58,6 +65,7 @@
         ],
         out_specs=pl.BlockSpec((1, 1, edge, filters), lambda e, c: (e, c, 0, 0)),
         out_shape=jax.ShapeDtypeStruct((2, 3, edge, filters), F32),
+        cost_estimate=cost(12 * edge * channels * filters, flat, weight),
         compiler_params=pltpu.CompilerParams(vmem_limit_bytes=48 * 1024 * 1024),
     )(flat, weight)
 
@@ -94,6 +102,7 @@
         ],
         out_specs=pl.BlockSpec((1, cells, filters), lambda c, k: (c, 0, 0)),
         out_shape=jax.ShapeDtypeStruct((len(cols), cells, filters), F32),
+        cost_estimate=cost(6 * len(cols) * cells * channels * filters, flat),
         compiler_params=pltpu.CompilerParams(vmem_limit_bytes=48 * 1024 * 1024),
     )(flat, weight)
 
@@ -124,6 +133,7 @@
             out_specs=[pl.BlockSpec((2 * quarter, cells), lambda i, w: (i, 0))] * 4,
         ),
         out_shape=[jax.ShapeDtypeStruct((blocks * quarter, cells), BF)] * 4,
+        cost_estimate=cost(0, flat, flat),
         compiler_params=pltpu.CompilerParams(vmem_limit_bytes=48 * 1024 * 1024),
     )(where.reshape(1).astype(jnp.int32), flat)
 
@@ -166,6 +176,7 @@
             scratch_shapes=[pltpu.VMEM((step, wide, filters), F32)],
         ),
         out_shape=jax.ShapeDtypeStruct((3, 4, rows * breadth, filters), BF),
+        cost_estimate=cost(0, *arrays, *arrays),
         compiler_params=pltpu.CompilerParams(vmem_limit_bytes=48 * 1024 * 1024),
     )(place.reshape(1).astype(jnp.int32), *arrays)
 
@@ -203,6 +214,7 @@
         + [pl.BlockSpec((width, cells), lambda c: (0, 0))] * 4,
         out_specs=pl.BlockSpec((lats, lons, 3, 1, half_f, 2 * quarter), lambda c: (0, 0, 0, c, 0, 0)),
         out_shape=jax.ShapeDtypeStruct((lats, lons, 3, 3, half_f, 2 * quarter), BF),
+        cost_estimate=cost(72 * cells * width * filters, d_all, *group_in),
         compiler_params=pltpu.CompilerParams(vmem_limit_bytes=56 * 1024 * 1024),
     )(d_all, *group_in)
 
@@ -231,6 +243,7 @@
         ],
         out_specs=pl.BlockSpec((cells, block), lambda n: (0, n)),
         out_shape=jax.ShapeDtypeStruct((cells, channels), BF),
+        cost_estimate=cost(18 * cells * channels * filters, weight),
         compiler_params=pltpu.CompilerParams(vmem_limit_bytes=48 * 1024 * 1024),
     )(dcols, weight)
 

time: 191 us -> 185 us (0.969)
  waiting for transfers between devices: 38.6 us -> 49.3 us
  local copies, waits for them, and re-layouts: 18.5 us -> 11.6 us
  other arithmetic: 9.2 us -> 4.71 us
  starting transfers between devices: 67.4 us -> 64.1 us
    all_to_all x2, waiting for transfers between devices: 9.45 us -> 17.2 us  [total(): lax.all_to_all(spread, ('lat', 'lon'), 0, 0, axis_index_groups=groups)]
    ppermute x8, waiting for transfers between devices: 2.71 us -> 5.7 us  [ring(): return lax.ppermute(x, axis, pairs)]
    ppermute x10, starting transfers between devices: 24.5 us -> 22.3 us  [swap(): return lax.ppermute(x, 'lon', [(i, i ^ mask) for i in range(count)])]
    eq x3, local copies, waits for them, and re-layouts: 2.17 us -> 0.24 us  [head(): labels[:, None] == jnp.arange(classes, dtype=jnp.int32)[None, :]]
    unnamed x45 -> x21, local copies, waits for them, and re-layouts: 4.55 us -> 2.89 us
  transfers between devices with their start and end apart: 23 -> 23, of which waited for: 7 -> 7; matrix products, arithmetic and copies ran while one was open for 12% -> 7% of each run, Pallas kernels for 17% -> 17%
where the time goes in v5:
time: 185 us; the launch traced here: 184 us
  starting transfers between devices  64.1 us (35%)
  Pallas kernels  50.5 us (27%)
  waiting for transfers between devices  49.3 us (27%)
  local copies, waits for them, and re-layouts  11.6 us (6%)
  other arithmetic  4.71 us (3%)
  matrix products  2.91 us (2%)
    ppermute x10, starting transfers between devices, swap(): return lax.ppermute(x, 'lon', [(i, i ^ mask) for i in range(count)])  22.3 us
    all_to_all x1, waiting for transfers between devices, shards(): got = lax.all_to_all(blocks, ('lat', 'lon'), 0, 0)  19.3 us
    ppermute x8, starting transfers between devices, ring(): return lax.ppermute(x, axis, pairs)  19 us
    all_to_all x2, waiting for transfers between devices, total(): lax.all_to_all(spread, ('lat', 'lon'), 0, 0, axis_index_groups=groups)  17.2 us
    all_to_all x2, starting transfers between devices, total(): lax.all_to_all(spread, ('lat', 'lon'), 0, 0, axis_index_groups=groups)  16.6 us
    pallas_call x1, Pallas kernels, grad_kernel(): pl.pallas_call(body, grid=(3,), in_specs=[pl.BlockSpec((1,) + d_all.shape...  12.5 us
    pallas_call x2, Pallas kernels, inner_rows(): pl.pallas_call(body, grid=(len(cols), 3), in_specs=[pl.BlockSpec((cells,...  11.5 us
    pallas_call x1, Pallas kernels, grad_input(): pl.pallas_call(body, grid=(channels // block,), in_specs=[pl.BlockSpec(dc...  10.7 us
  transfers between devices with their start and end apart: 23, of which 7 were waited for; matrix products, arithmetic and copies ran while one was open for 7% of the time, Pallas kernels for 17%

profile of v5, /device:TPU:1, one launch (start us, length us, event | category | flops | bytes accessed | tf_op | source)
XLA Modules:
  0.0 184.3 jit_solution(5407367947053120360)
XLA Ops:
  2.5 5.8 %shard_map.109 = f32[2,3,288,256]{3,2,1,0:T(8,128)S(1)} custom-call(bf16[768,2048]{1,0:T(8,128)(2,1)S(1)} %bitcast.100, bf16[9,2048,256]{2,1,0:T(8,128)(2,1)} %bitcast.113), custom_call_target="tpu_custom_call" | custom-call | flops 1811939328 | bytes 12582912 | tf_op jit(solution)/shard_map/pallas_call | solution.py:59
  8.5 2.8 %collective-permute-start.2 = (f32[2,12,12,256]{3,2,1,0:T(8,128)S(1)}, f32[2,12,12,256]{3,2,1,0:T(8,128)S(1)}, u32[]{:S(2)}, u32[]{:S(2)}) collective-permute-start(f32[2,12,12,256]{3,2,1,0:T(8,128)S(1)} %get-tuple-element.51), channel_id=1, source_target_pairs={{0,1},{1,2},{2,3},{3,4},{4,5},{5,6},{6,7},{7,8},{8,9},{9,10},{10,1... | collective-permute-start | bytes 884744 | tf_op jit(solution)/shard_map/ppermute | solution.py:21
  11.2 7.3 %shard_map.111 = f32[2,768,256]{2,1,0:T(8,128)S(1)} custom-call(bf16[768,2048]{1,0:T(8,128)(2,1)S(1)} %bitcast.101, bf16[9,2048,256]{2,1,0:T(8,128)(2,1)} %bitcast.114), custom_call_target="tpu_custom_call" | custom-call | flops 4831838208 | bytes 3145728 | tf_op jit(solution)/shard_map/pallas_call | solution.py:96
  19.7 3.4 %collective-permute-start.1 = (f32[32,12,256]{2,1,0:T(8,128)}, f32[32,12,256]{2,1,0:T(8,128)}, u32[]{:S(2)}, u32[]{:S(2)}) collective-permute-start(f32[32,12,256]{2,1,0:T(8,128)} %get-tuple-element.55), channel_id=1, source_target_pairs={{0,15},{1,0},{2,1},{3,2},{4,3},{5,4},{6,5},{7,6},{8,7},{9,8},{10,9... | collective-permute-start | bytes 1179656 | tf_op jit(solution)/shard_map/ppermute | solution.py:21
  23.1 4.2 %shard_map.110 = f32[1,768,256]{2,1,0:T(8,128)S(1)} custom-call(bf16[768,2048]{1,0:T(8,128)(2,1)S(1)} %bitcast.102, bf16[9,2048,256]{2,1,0:T(8,128)(2,1)} %bitcast.115), custom_call_target="tpu_custom_call" | custom-call | flops 2415919104 | bytes 3145728 | tf_op jit(solution)/shard_map/pallas_call | solution.py:96
  28.4 4.5 %collective-permute-start.4 = (f32[12,24,256]{2,1,0:T(8,128)}, f32[12,24,256]{2,1,0:T(8,128)S(1)}, u32[]{:S(2)}, u32[]{:S(2)}) collective-permute-start(f32[12,24,256]{2,1,0:T(8,128)} %get-tuple-element.57), channel_id=1, source_target_pairs={{0,16},{16,32},{32,48},{48,64},{64,80},{80,96},{96,112},{1,17},{17... | collective-permute-start | bytes 884744 | tf_op jit(solution)/shard_map/ppermute | solution.py:21
  34.3 5.0 %shard_map.112 = (bf16[512,768]{1,0:T(8,128)(2,1)S(1)}, bf16[512,768]{1,0:T(8,128)(2,1)S(1)}, bf16[512,768]{1,0:T(8,128)(2,1)}, bf16[512,768]{1,0:T(8,128)(2,1)S(1)}) custom-call(s32[1]{0:T(128)} %bitcast.8.where_ref.place_ref, bf16[768,2048]{1,0:T(8,128)(2,1)} %bitcast.99), custom_call_target="tpu_custom_call" | custom-call | bytes 6291456 | tf_op jit(solution)/shard_map/pallas_call | solution.py:127
  41.2 5.7 %collective-permute-done.4 = f32[12,24,256]{2,1,0:T(8,128)S(1)} collective-permute-done((f32[12,24,256]{2,1,0:T(8,128)}, f32[12,24,256]{2,1,0:T(8,128)S(1)}, u32[]{:S(2)}, u32[]{:S(2)}) %collective-permute-start.4) | collective-permute-done | bytes 294944 | tf_op jit(solution)/shard_map/ppermute | solution.py:21
  48.2 2.1 %collective-permute-start.6 = (f32[4,128]{1,0:T(4,128)S(1)}, f32[4,128]{1,0:T(4,128)S(1)}, u32[]{:S(2)}, u32[]{:S(2)}) collective-permute-start(f32[4,128]{1,0:T(4,128)S(1)} %reshape.151), channel_id=1, source_target_pairs={{0,1},{1,0},{2,3},{3,2},{4,5},{5,4},{6,7},{7,6},{8,9},{9,8},{10,11... | collective-permute-start | bytes 6152 | tf_op jit(solution)/shard_map/ppermute | solution.py:26
  51.8 9.9 %all-to-all-start = ((f32[64,4,128]{2,1,0:T(4,128)}), f32[64,4,128]{2,1,0:T(4,128)S(1)}, u32[]{:S(2)}, u32[]{:S(2)}) async-start(f32[64,4,128]{2,1,0:T(4,128)} %broadcast_in_dim.32), calls=%async_computation | async-start | bytes 262144 | tf_op jit(solution)/shard_map/all_to_all | solution.py:48
  63.6 6.8 %all-to-all-done = f32[64,4,128]{2,1,0:T(4,128)S(1)} async-done(((f32[64,4,128]{2,1,0:T(4,128)}), f32[64,4,128]{2,1,0:T(4,128)S(1)}, u32[]{:S(2)}, u32[]{:S(2)}) %all-to-all-start) | async-done | bytes 131104 | tf_op jit(solution)/shard_map/all_to_all | solution.py:48
  76.9 5.8 %collective-permute-start.10 = (bf16[13,24,256]{2,1,0:T(8,128)(2,1)S(1)}, bf16[13,24,256]{2,1,0:T(8,128)(2,1)S(1)}, u32[]{:S(2)}, u32[]{:S(2)}) collective-permute-start(bf16[13,24,256]{2,1,0:T(8,128)(2,1)S(1)} %pad_maximum_fusion.2), channel_id=1, source_target_pairs={{0,16},{16,32},{32,48},{48,64},{64,80},{80,96},{96,112},{1,17},{17... | collective-permute-start | bytes 479240 | tf_op jit(solution)/shard_map/ppermute | solution.py:21
  83.5 6.8 %all-to-all-start.1 = ((f32[64,3,4,128]{3,2,1,0:T(4,128)}), f32[64,3,4,128]{3,2,1,0:T(4,128)S(1)}, u32[]{:S(2)}, u32[]{:S(2)}) async-start(f32[64,3,4,128]{3,2,1,0:T(4,128)} %broadcast_in_dim.36), calls=%async_computation.1 | async-start | bytes 786432 | tf_op jit(solution)/shard_map/all_to_all | solution.py:48
  91.0 10.4 %all-to-all-done.1 = f32[64,3,4,128]{3,2,1,0:T(4,128)S(1)} async-done(((f32[64,3,4,128]{3,2,1,0:T(4,128)}), f32[64,3,4,128]{3,2,1,0:T(4,128)S(1)}, u32[]{:S(2)}, u32[]{:S(2)}) %all-to-all-start.1) | async-done | bytes 393248 | tf_op jit(solution)/shard_map/all_to_all | solution.py:48
  102.7 2.1 %collective-permute-start.19 = (bf16[512,768]{1,0:T(8,128)(2,1)S(1)}, bf16[512,768]{1,0:T(8,128)(2,1)S(1)}, u32[]{:S(2)}, u32[]{:S(2)}) collective-permute-start(bf16[512,768]{1,0:T(8,128)(2,1)S(1)} %get-tuple-element.35), channel_id=1, source_target_pairs={{0,1},{1,0},{2,3},{3,2},{4,5},{5,4},{6,7},{7,6},{8,9},{9,8},{10,11... | collective-permute-start | bytes 2359304 | tf_op jit(solution)/shard_map/ppermute | solution.py:26
  106.3 6.7 %collective-permute-start.15 = (bf16[56,24,256]{2,1,0:T(8,128)(2,1)S(1)}, bf16[56,24,256]{2,1,0:T(8,128)(2,1)S(1)}, u32[]{:S(2)}, u32[]{:S(2)}) collective-permute-start(bf16[56,24,256]{2,1,0:T(8,128)(2,1)S(1)} %bitcast.108), channel_id=1, source_target_pairs={{0,1},{1,0},{2,3},{3,2},{4,5},{5,4},{6,7},{7,6},{8,9},{9,8},{10,11... | collective-permute-start | bytes 2064392 | tf_op jit(solution)/shard_map/ppermute | solution.py:26
  113.0 4.8 %collective-permute-done.12.refs_1_ = bf16[56,24,256]{2,1,0:T(8,128)(2,1)S(1)} collective-permute-done((bf16[56,24,256]{2,1,0:T(8,128)(2,1)S(1)}, bf16[56,24,256]{2,1,0:T(8,128)(2,1)S(1)}, u32[]{:S(2)}, u32[]{:S(2)}) %collective-permute-start.12) | collective-permute-done | bytes 688160 | tf_op jit(solution)/shard_map/ppermute | solution.py:26
  117.8 5.0 %collective-permute-start.16 = (bf16[56,24,256]{2,1,0:T(8,128)(2,1)S(1)}, bf16[56,24,256]{2,1,0:T(8,128)(2,1)S(1)}, u32[]{:S(2)}, u32[]{:S(2)}) collective-permute-start(bf16[56,24,256]{2,1,0:T(8,128)(2,1)S(1)} %collective-permute-done.12.refs_1_), channel_id=1, source_target_pairs={{0,1},{1,0},{2,3},{3,2},{4,5},{5,4},{6,7},{7,6},{8,9},{9,8},{10,11... | collective-permute-start | bytes 2064392 | tf_op jit(solution)/shard_map/ppermute | solution.py:26
  122.8 2.5 %collective-permute-start.17 = (bf16[56,12,256]{2,1,0:T(8,128)(2,1)S(1)}, bf16[56,12,256]{2,1,0:T(8,128)(2,1)S(1)}, u32[]{:S(2)}, u32[]{:S(2)}) collective-permute-start(bf16[56,12,256]{2,1,0:T(8,128)(2,1)S(1)} %collective-permute-done.13.refs_2_), channel_id=1, source_target_pairs={{0,1},{1,0},{2,3},{3,2},{4,5},{5,4},{6,7},{7,6},{8,9},{9,8},{10,11... | collective-permute-start | bytes 1032200 | tf_op jit(solution)/shard_map/ppermute | solution.py:26
  126.7 5.0 %shard_map.113.d_ref = bf16[3,4,1344,256]{3,2,1,0:T(8,128)(2,1)} custom-call(s32[1]{0:T(128)} %bitcast.8.where_ref.place_ref, bf16[56,24,256]{2,1,0:T(8,128)(2,1)S(1)} %bitcast.109, bf16[56,24,256]{2,1,0:T(8,128)(2,1)S(1)} %collective-permute-done.12.refs_1_, bf16[56,12,256]{2,1,0:T(8,128)(2,1)S(1)} %collective-permute-done.13.refs_2_, ...), custom_call_target="tpu_custom_call" | custom-call | bytes 8257536 | tf_op jit(solution)/shard_map/pallas_call | solution.py:167
  132.6 12.5 %shard_map.115 = bf16[8,16,3,3,8,128]{5,4,3,2,1,0:T(8,128)(2,1)} custom-call(bf16[3,4,1344,256]{3,2,1,0:T(8,128)(2,1)} %shard_map.113.d_ref, bf16[512,768]{1,0:T(8,128)(2,1)} %copy-done.2, bf16[512,768]{1,0:T(8,128)(2,1)} %copy-done.9, bf16[512,768]{1,0:T(8,128)(2,1)} %collective-permute-done.7.refs_2_, bf16[512,768]{1,0:T(8,128)(2,1)} %collective-permute-done.9.refs_3_), custom_call_target="tpu_custom_call" | custom-call | flops 7247757312 | bytes 11403264 | tf_op jit(solution)/shard_map/pallas_call | solution.py:208
  145.1 4.8 %all-to-all-start.2 = ((bf16[128,72,128]{2,1,0:T(8,128)(2,1)}), bf16[128,72,128]{2,1,0:T(8,128)(2,1)S(1)}, u32[]{:S(2)}, u32[]{:S(2)}) async-start(bf16[128,72,128]{2,1,0:T(8,128)(2,1)} %bitcast.118), calls=%async_computation.2 | async-start | bytes 4718592 | tf_op jit(solution)/shard_map/all_to_all | solution.py:359
  152.7 10.7 %shard_map.114 = bf16[768,2048]{1,0:T(8,128)(2,1)} custom-call(bf16[3,1344,256]{2,1,0:T(8,128)(2,1)S(1)} %slice_bitcast_fusion.d_ref, bf16[9,2048,256]{2,1,0:T(8,128)(2,1)} %bitcast.116), custom_call_target="tpu_custom_call" | custom-call | flops 7247757312 | bytes 9437184 | tf_op jit(solution)/shard_map/pallas_call | solution.py:237
  163.4 19.3 %all-to-all-done.2 = bf16[128,72,128]{2,1,0:T(8,128)(2,1)S(1)} async-done(((bf16[128,72,128]{2,1,0:T(8,128)(2,1)}), bf16[128,72,128]{2,1,0:T(8,128)(2,1)S(1)}, u32[]{:S(2)}, u32[]{:S(2)}) %all-to-all-start.2) | async-done | bytes 2359328 | tf_op jit(solution)/shard_map/all_to_all | solution.py:359
  (110 shorter events, 29.4 us)
Async XLA Ops:
  0.6 70.1 %copy-start = (f32[3,256]{1,0:T(4,128)S(1)}, f32[3,256]{1,0:T(4,128)}, u32[]{:S(2)}) copy-start(f32[3,256]{1,0:T(4,128)} %param.10) | copy-start | bytes 9220
  8.5 18.8 %collective-permute-start.2 = (f32[2,12,12,256]{3,2,1,0:T(8,128)S(1)}, f32[2,12,12,256]{3,2,1,0:T(8,128)S(1)}, u32[]{:S(2)}, u32[]{:S(2)}) collective-permute-start(f32[2,12,12,256]{3,2,1,0:T(8,128)S(1)} %get-tuple-element.51), channel_id=1, source_target_pairs={{0,1},{1,2},{2,3},{3,4},{4,5},{5,6},{6,7},{7,8},{8,9},{9,10},{10,1... | collective-permute-start | bytes 884744 | tf_op jit(solution)/shard_map/ppermute | solution.py:21
  11.2 16.1 %collective-permute-start.3 = (f32[2,12,12,256]{3,2,1,0:T(8,128)S(1)}, f32[2,12,12,256]{3,2,1,0:T(8,128)S(1)}, u32[]{:S(2)}, u32[]{:S(2)}) collective-permute-start(f32[2,12,12,256]{3,2,1,0:T(8,128)S(1)} %get-tuple-element.52), channel_id=1, source_target_pairs={{0,15},{1,0},{2,1},{3,2},{4,3},{5,4},{6,5},{7,6},{8,7},{9,8},{10,9... | collective-permute-start | bytes 884744 | tf_op jit(solution)/shard_map/ppermute | solution.py:21
  19.7 19.6 %collective-permute-start.1 = (f32[32,12,256]{2,1,0:T(8,128)}, f32[32,12,256]{2,1,0:T(8,128)}, u32[]{:S(2)}, u32[]{:S(2)}) collective-permute-start(f32[32,12,256]{2,1,0:T(8,128)} %get-tuple-element.55), channel_id=1, source_target_pairs={{0,15},{1,0},{2,1},{3,2},{4,3},{5,4},{6,5},{7,6},{8,7},{9,8},{10,9... | collective-permute-start | bytes 1179656 | tf_op jit(solution)/shard_map/ppermute | solution.py:21
  23.1 16.3 %collective-permute-start = (f32[32,12,256]{2,1,0:T(8,128)}, f32[32,12,256]{2,1,0:T(8,128)}, u32[]{:S(2)}, u32[]{:S(2)}) collective-permute-start(f32[32,12,256]{2,1,0:T(8,128)} %get-tuple-element.56), channel_id=1, source_target_pairs={{0,1},{1,2},{2,3},{3,4},{4,5},{5,6},{6,7},{7,8},{8,9},{9,10},{10,1... | collective-permute-start | bytes 1179656 | tf_op jit(solution)/shard_map/ppermute | solution.py:21
  28.4 18.5 %collective-permute-start.4 = (f32[12,24,256]{2,1,0:T(8,128)}, f32[12,24,256]{2,1,0:T(8,128)S(1)}, u32[]{:S(2)}, u32[]{:S(2)}) collective-permute-start(f32[12,24,256]{2,1,0:T(8,128)} %get-tuple-element.57), channel_id=1, source_target_pairs={{0,16},{16,32},{32,48},{48,64},{64,80},{80,96},{96,112},{1,17},{17... | collective-permute-start | bytes 884744 | tf_op jit(solution)/shard_map/ppermute | solution.py:21
  33.0 14.0 %collective-permute-start.5 = (f32[12,24,256]{2,1,0:T(8,128)}, f32[12,24,256]{2,1,0:T(8,128)}, u32[]{:S(2)}, u32[]{:S(2)}) collective-permute-start(f32[12,24,256]{2,1,0:T(8,128)} %get-tuple-element.58), channel_id=1, source_target_pairs={{16,0},{32,16},{48,32},{64,48},{80,64},{96,80},{112,96},{17,1},{33... | collective-permute-start | bytes 884744 | tf_op jit(solution)/shard_map/ppermute | solution.py:21
  39.3 31.2 %collective-permute-start.7 = (bf16[512,768]{1,0:T(8,128)(2,1)}, bf16[512,768]{1,0:T(8,128)(2,1)}, u32[]{:S(2)}, u32[]{:S(2)}) collective-permute-start(bf16[512,768]{1,0:T(8,128)(2,1)} %get-tuple-element.30), channel_id=1, source_target_pairs={{0,2},{1,3},{2,0},{3,1},{4,6},{5,7},{6,4},{7,5},{8,10},{9,11},{10,... | collective-permute-start | bytes 2359304 | tf_op jit(solution)/shard_map/ppermute | solution.py:26
  48.2 3.0 %collective-permute-start.6 = (f32[4,128]{1,0:T(4,128)S(1)}, f32[4,128]{1,0:T(4,128)S(1)}, u32[]{:S(2)}, u32[]{:S(2)}) collective-permute-start(f32[4,128]{1,0:T(4,128)S(1)} %reshape.151), channel_id=1, source_target_pairs={{0,1},{1,0},{2,3},{3,2},{4,5},{5,4},{6,7},{7,6},{8,9},{9,8},{10,11... | collective-permute-start | bytes 6152 | tf_op jit(solution)/shard_map/ppermute | solution.py:26
  51.8 18.6 %all-to-all-start = ((f32[64,4,128]{2,1,0:T(4,128)}), f32[64,4,128]{2,1,0:T(4,128)S(1)}, u32[]{:S(2)}, u32[]{:S(2)}) async-start(f32[64,4,128]{2,1,0:T(4,128)} %broadcast_in_dim.32), calls=%async_computation | async-start | bytes 262144 | tf_op jit(solution)/shard_map/all_to_all | solution.py:48
  61.9 39.5 %collective-permute-start.9 = (bf16[512,768]{1,0:T(8,128)(2,1)}, bf16[512,768]{1,0:T(8,128)(2,1)}, u32[]{:S(2)}, u32[]{:S(2)}) collective-permute-start(bf16[512,768]{1,0:T(8,128)(2,1)} %copy-done.3), channel_id=1, source_target_pairs={{0,3},{1,2},{2,1},{3,0},{4,7},{5,6},{6,5},{7,4},{8,11},{9,10},{10,... | collective-permute-start | bytes 2359304 | tf_op jit(solution)/shard_map/ppermute | solution.py:26
  73.1 17.1 %collective-permute-start.11 = (bf16[13,24,256]{2,1,0:T(8,128)(2,1)S(1)}, bf16[13,24,256]{2,1,0:T(8,128)(2,1)S(1)}, u32[]{:S(2)}, u32[]{:S(2)}) collective-permute-start(bf16[13,24,256]{2,1,0:T(8,128)(2,1)S(1)} %pad_maximum_fusion.3), channel_id=1, source_target_pairs={{16,0},{32,16},{48,32},{64,48},{80,64},{96,80},{112,96},{17,1},{33... | collective-permute-start | bytes 479240 | tf_op jit(solution)/shard_map/ppermute | solution.py:21
  75.2 7.4 %collective-permute-start.8 = (f32[3,4,128]{2,1,0:T(4,128)S(1)}, f32[3,4,128]{2,1,0:T(4,128)S(1)}, u32[]{:S(2)}, u32[]{:S(2)}) collective-permute-start(f32[3,4,128]{2,1,0:T(4,128)S(1)} %reshape.152), channel_id=1, source_target_pairs={{0,1},{1,0},{2,3},{3,2},{4,5},{5,4},{6,7},{7,6},{8,9},{9,8},{10,11... | collective-permute-start | bytes 18440 | tf_op jit(solution)/shard_map/ppermute | solution.py:26
  76.9 13.4 %collective-permute-start.10 = (bf16[13,24,256]{2,1,0:T(8,128)(2,1)S(1)}, bf16[13,24,256]{2,1,0:T(8,128)(2,1)S(1)}, u32[]{:S(2)}, u32[]{:S(2)}) collective-permute-start(bf16[13,24,256]{2,1,0:T(8,128)(2,1)S(1)} %pad_maximum_fusion.2), channel_id=1, source_target_pairs={{0,16},{16,32},{32,48},{48,64},{64,80},{80,96},{96,112},{1,17},{17... | collective-permute-start | bytes 479240 | tf_op jit(solution)/shard_map/ppermute | solution.py:21
  83.5 17.9 %all-to-all-start.1 = ((f32[64,3,4,128]{3,2,1,0:T(4,128)}), f32[64,3,4,128]{3,2,1,0:T(4,128)S(1)}, u32[]{:S(2)}, u32[]{:S(2)}) async-start(f32[64,3,4,128]{3,2,1,0:T(4,128)} %broadcast_in_dim.36), calls=%async_computation.1 | async-start | bytes 786432 | tf_op jit(solution)/shard_map/all_to_all | solution.py:48
  102.6 15.3 %collective-permute-start.12 = (bf16[56,24,256]{2,1,0:T(8,128)(2,1)S(1)}, bf16[56,24,256]{2,1,0:T(8,128)(2,1)S(1)}, u32[]{:S(2)}, u32[]{:S(2)}) collective-permute-start(bf16[56,24,256]{2,1,0:T(8,128)(2,1)S(1)} %bitcast.106), channel_id=1, source_target_pairs={{0,2},{1,3},{2,0},{3,1},{4,6},{5,7},{6,4},{7,5},{8,10},{9,11},{10,... | collective-permute-start | bytes 2064392 | tf_op jit(solution)/shard_map/ppermute | solution.py:26
  102.7 29.1 %collective-permute-start.19 = (bf16[512,768]{1,0:T(8,128)(2,1)S(1)}, bf16[512,768]{1,0:T(8,128)(2,1)S(1)}, u32[]{:S(2)}, u32[]{:S(2)}) collective-permute-start(bf16[512,768]{1,0:T(8,128)(2,1)S(1)} %get-tuple-element.35), channel_id=1, source_target_pairs={{0,1},{1,0},{2,3},{3,2},{4,5},{5,4},{6,7},{7,6},{8,9},{9,8},{10,11... | collective-permute-start | bytes 2359304 | tf_op jit(solution)/shard_map/ppermute | solution.py:26
  104.9 17.9 %collective-permute-start.14 = (bf16[56,12,256]{2,1,0:T(8,128)(2,1)S(1)}, bf16[56,12,256]{2,1,0:T(8,128)(2,1)S(1)}, u32[]{:S(2)}, u32[]{:S(2)}) collective-permute-start(bf16[56,12,256]{2,1,0:T(8,128)(2,1)S(1)} %slice_select_fusion), channel_id=1, source_target_pairs={{3,7},{0,12},{7,11},{4,0},{11,15},{8,4},{15,3},{12,8},{19,23},{16,... | collective-permute-start | bytes 1032200 | tf_op jit(solution)/shard_map/ppermute | solution.py:35
  105.6 17.2 %collective-permute-start.13 = (bf16[56,12,256]{2,1,0:T(8,128)(2,1)S(1)}, bf16[56,12,256]{2,1,0:T(8,128)(2,1)S(1)}, u32[]{:S(2)}, u32[]{:S(2)}) collective-permute-start(bf16[56,12,256]{2,1,0:T(8,128)(2,1)S(1)} %slice_select_fusion), channel_id=1, source_target_pairs={{3,4},{0,15},{7,8},{4,3},{11,12},{8,7},{15,0},{12,11},{19,20},{16,... | collective-permute-start | bytes 1032200 | tf_op jit(solution)/shard_map/ppermute | solution.py:35
  106.3 20.5 %collective-permute-start.15 = (bf16[56,24,256]{2,1,0:T(8,128)(2,1)S(1)}, bf16[56,24,256]{2,1,0:T(8,128)(2,1)S(1)}, u32[]{:S(2)}, u32[]{:S(2)}) collective-permute-start(bf16[56,24,256]{2,1,0:T(8,128)(2,1)S(1)} %bitcast.108), channel_id=1, source_target_pairs={{0,1},{1,0},{2,3},{3,2},{4,5},{5,4},{6,7},{7,6},{8,9},{9,8},{10,11... | collective-permute-start | bytes 2064392 | tf_op jit(solution)/shard_map/ppermute | solution.py:26
  117.8 8.9 %collective-permute-start.16 = (bf16[56,24,256]{2,1,0:T(8,128)(2,1)S(1)}, bf16[56,24,256]{2,1,0:T(8,128)(2,1)S(1)}, u32[]{:S(2)}, u32[]{:S(2)}) collective-permute-start(bf16[56,24,256]{2,1,0:T(8,128)(2,1)S(1)} %collective-permute-done.12.refs_1_), channel_id=1, source_target_pairs={{0,1},{1,0},{2,3},{3,2},{4,5},{5,4},{6,7},{7,6},{8,9},{9,8},{10,11... | collective-permute-start | bytes 2064392 | tf_op jit(solution)/shard_map/ppermute | solution.py:26
  122.8 2.5 %collective-permute-start.18 = (bf16[56,12,256]{2,1,0:T(8,128)(2,1)S(1)}, bf16[56,12,256]{2,1,0:T(8,128)(2,1)S(1)}, u32[]{:S(2)}, u32[]{:S(2)}) collective-permute-start(bf16[56,12,256]{2,1,0:T(8,128)(2,1)S(1)} %collective-permute-done.14.refs_3_), channel_id=1, source_target_pairs={{0,1},{1,0},{2,3},{3,2},{4,5},{5,4},{6,7},{7,6},{8,9},{9,8},{10,11... | collective-permute-start | bytes 1032200 | tf_op jit(solution)/shard_map/ppermute | solution.py:26
  122.8 4.0 %collective-permute-start.17 = (bf16[56,12,256]{2,1,0:T(8,128)(2,1)S(1)}, bf16[56,12,256]{2,1,0:T(8,128)(2,1)S(1)}, u32[]{:S(2)}, u32[]{:S(2)}) collective-permute-start(bf16[56,12,256]{2,1,0:T(8,128)(2,1)S(1)} %collective-permute-done.13.refs_2_), channel_id=1, source_target_pairs={{0,1},{1,0},{2,3},{3,2},{4,5},{5,4},{6,7},{7,6},{8,9},{9,8},{10,11... | collective-permute-start | bytes 1032200 | tf_op jit(solution)/shard_map/ppermute | solution.py:26
  145.1 37.6 %all-to-all-start.2 = ((bf16[128,72,128]{2,1,0:T(8,128)(2,1)}), bf16[128,72,128]{2,1,0:T(8,128)(2,1)S(1)}, u32[]{:S(2)}, u32[]{:S(2)}) async-start(bf16[128,72,128]{2,1,0:T(8,128)(2,1)} %bitcast.118), calls=%async_computation.2 | async-start | bytes 4718592 | tf_op jit(solution)/shard_map/all_to_all | solution.py:359
  (9 other events, 74.2 us)

commit v6 on v5

--- a/solution.py
+++ b/solution.py
@@ -66,7 +66,7 @@
         out_specs=pl.BlockSpec((1, 1, edge, filters), lambda e, c: (e, c, 0, 0)),
         out_shape=jax.ShapeDtypeStruct((2, 3, edge, filters), F32),
         cost_estimate=cost(12 * edge * channels * filters, flat, weight),
-        compiler_params=pltpu.CompilerParams(vmem_limit_bytes=48 * 1024 * 1024),
+        compiler_params=pltpu.CompilerParams(vmem_limit_bytes=20 * 1024 * 1024),
     )(flat, weight)
 
 
@@ -103,7 +103,7 @@
         out_specs=pl.BlockSpec((1, cells, filters), lambda c, k: (c, 0, 0)),
         out_shape=jax.ShapeDtypeStruct((len(cols), cells, filters), F32),
         cost_estimate=cost(6 * len(cols) * cells * channels * filters, flat),
-        compiler_params=pltpu.CompilerParams(vmem_limit_bytes=48 * 1024 * 1024),
+        compiler_params=pltpu.CompilerParams(vmem_limit_bytes=24 * 1024 * 1024),
     )(flat, weight)
 
 
@@ -134,7 +134,7 @@
         ),
         out_shape=[jax.ShapeDtypeStruct((blocks * quarter, cells), BF)] * 4,
         cost_estimate=cost(0, flat, flat),
-        compiler_params=pltpu.CompilerParams(vmem_limit_bytes=48 * 1024 * 1024),
+        compiler_params=pltpu.CompilerParams(vmem_limit_bytes=20 * 1024 * 1024),
     )(where.reshape(1).astype(jnp.int32), flat)
 
 
@@ -177,7 +177,7 @@
         ),
         out_shape=jax.ShapeDtypeStruct((3, 4, rows * breadth, filters), BF),
         cost_estimate=cost(0, *arrays, *arrays),
-        compiler_params=pltpu.CompilerParams(vmem_limit_bytes=48 * 1024 * 1024),
+        compiler_params=pltpu.CompilerParams(vmem_limit_bytes=16 * 1024 * 1024),
     )(place.reshape(1).astype(jnp.int32), *arrays)
 
 
@@ -215,7 +215,7 @@
         out_specs=pl.BlockSpec((lats, lons, 3, 1, half_f, 2 * quarter), lambda c: (0, 0, 0, c, 0, 0)),
         out_shape=jax.ShapeDtypeStruct((lats, lons, 3, 3, half_f, 2 * quarter), BF),
         cost_estimate=cost(72 * cells * width * filters, d_all, *group_in),
-        compiler_params=pltpu.CompilerParams(vmem_limit_bytes=56 * 1024 * 1024),
+        compiler_params=pltpu.CompilerParams(vmem_limit_bytes=32 * 1024 * 1024),
     )(d_all, *group_in)
 
 
@@ -244,7 +244,7 @@
         out_specs=pl.BlockSpec((cells, block), lambda n: (0, n)),
         out_shape=jax.ShapeDtypeStruct((cells, channels), BF),
         cost_estimate=cost(18 * cells * channels * filters, weight),
-        compiler_params=pltpu.CompilerParams(vmem_limit_bytes=48 * 1024 * 1024),
+        compiler_params=pltpu.CompilerParams(vmem_limit_bytes=32 * 1024 * 1024),
     )(dcols, weight)
 
 

time: 185 us -> 181 us (0.978)
  Pallas kernels: 50.5 us -> 35.3 us
  local copies, waits for them, and re-layouts: 11.6 us -> 20.6 us
  other arithmetic: 4.71 us -> 8.34 us
  waiting for transfers between devices: 49.3 us -> 46.1 us
    unnamed x21 -> x47, local copies, waits for them, and re-layouts: 2.89 us -> 10.2 us
    pallas_call x2, Pallas kernels: 11.5 us -> 7.29 us  [inner_rows(): pl.pallas_call(body, grid=(len(cols), 3), in_specs=[pl.BlockSpec((cells,...]
    pallas_call x1, Pallas kernels: 5.85 us -> 2.91 us  [outer_rows(): pl.pallas_call(body, grid=(2, 3), in_specs=[pl.BlockSpec((cells, channels...]
    pallas_call x1, Pallas kernels: 5.01 us -> 2.13 us  [group_windows(): pl.pallas_call(body, grid_spec=pltpu.PrefetchScalarGridSpec(num_scalar_pr...]
    pallas_call x1, Pallas kernels: 12.5 us -> 9.83 us  [grad_kernel(): pl.pallas_call(body, grid=(3,), in_specs=[pl.BlockSpec((1,) + d_all.shape...]
    all_to_all x1, waiting for transfers between devices: 19.3 us -> 16.7 us  [shards(): got = lax.all_to_all(blocks, ('lat', 'lon'), 0, 0)]
    ppermute x10, starting transfers between devices: 22.3 us -> 24.2 us  [swap(): return lax.ppermute(x, 'lon', [(i, i ^ mask) for i in range(count)])]
  transfers between devices with their start and end apart: 23 -> 23, of which waited for: 7 -> 7; matrix products, arithmetic and copies ran while one was open for 7% -> 10% of each run, Pallas kernels for 17% -> 12%
where the time goes in v6:
time: 181 us; the launch traced here: 180 us
  starting transfers between devices  65 us (36%)
  waiting for transfers between devices  46.1 us (25%)
  Pallas kernels  35.3 us (20%)
  local copies, waits for them, and re-layouts  20.6 us (11%)
  other arithmetic  8.34 us (5%)
  matrix products  3.78 us (2%)
    ppermute x10, starting transfers between devices, swap(): return lax.ppermute(x, 'lon', [(i, i ^ mask) for i in range(count)])  24.2 us
    ppermute x8, starting transfers between devices, ring(): return lax.ppermute(x, axis, pairs)  19.7 us
    all_to_all x1, waiting for transfers between devices, shards(): got = lax.all_to_all(blocks, ('lat', 'lon'), 0, 0)  16.7 us
    all_to_all x2, waiting for transfers between devices, total(): lax.all_to_all(spread, ('lat', 'lon'), 0, 0, axis_index_groups=groups)  15.6 us
    all_to_all x2, starting transfers between devices, total(): lax.all_to_all(spread, ('lat', 'lon'), 0, 0, axis_index_groups=groups)  14.9 us
    unnamed x47, local copies, waits for them, and re-layouts  10.2 us
    pallas_call x1, Pallas kernels, grad_kernel(): pl.pallas_call(body, grid=(3,), in_specs=[pl.BlockSpec((1,) + d_all.shape...  9.83 us
    pallas_call x1, Pallas kernels, grad_input(): pl.pallas_call(body, grid=(channels // block,), in_specs=[pl.BlockSpec(dc...  9.64 us
  transfers between devices with their start and end apart: 23, of which 7 were waited for; matrix products, arithmetic and copies ran while one was open for 10% of the time, Pallas kernels for 12%

profile of v6, /device:TPU:1, one launch (start us, length us, event | category | flops | bytes accessed | tf_op | source)
XLA Modules:
  0.0 180.4 jit_solution(3819469205009080738)
XLA Ops:
  0.7 3.7 %copy-done.1 = bf16[3,3,2048,256]{3,2,1,0:T(8,128)(2,1)S(1)} copy-done((bf16[3,3,2048,256]{3,2,1,0:T(8,128)(2,1)S(1)}, bf16[3,3,2048,256]{3,2,1,0:T(8,128)(2,1)}, u32[]{:S(2)}) %copy-start.1) | copy-done | bytes 9437208
  6.2 2.9 %shard_map.109 = f32[2,3,288,256]{3,2,1,0:T(8,128)S(1)} custom-call(bf16[768,2048]{1,0:T(8,128)(2,1)S(1)} %bitcast.103, bf16[9,2048,256]{2,1,0:T(8,128)(2,1)S(1)} %bitcast.99), custom_call_target="tpu_custom_call" | custom-call | flops 1811939328 | bytes 12582912 | tf_op jit(solution)/shard_map/pallas_call | solution.py:59
  9.2 2.8 %collective-permute-start.2 = (f32[2,12,12,256]{3,2,1,0:T(8,128)S(1)}, f32[2,12,12,256]{3,2,1,0:T(8,128)S(1)}, u32[]{:S(2)}, u32[]{:S(2)}) collective-permute-start(f32[2,12,12,256]{3,2,1,0:T(8,128)S(1)} %get-tuple-element.51), channel_id=1, source_target_pairs={{0,1},{1,2},{2,3},{3,4},{4,5},{5,6},{6,7},{7,8},{8,9},{9,10},{10,1... | collective-permute-start | bytes 884744 | tf_op jit(solution)/shard_map/ppermute | solution.py:21
  12.0 4.9 %shard_map.111 = f32[2,768,256]{2,1,0:T(8,128)S(1)} custom-call(bf16[768,2048]{1,0:T(8,128)(2,1)S(1)} %bitcast.104, bf16[9,2048,256]{2,1,0:T(8,128)(2,1)S(1)} %bitcast.100), custom_call_target="tpu_custom_call" | custom-call | flops 4831838208 | bytes 3145728 | tf_op jit(solution)/shard_map/pallas_call | solution.py:96
  18.1 3.4 %collective-permute-start.1 = (f32[32,12,256]{2,1,0:T(8,128)}, f32[32,12,256]{2,1,0:T(8,128)}, u32[]{:S(2)}, u32[]{:S(2)}) collective-permute-start(f32[32,12,256]{2,1,0:T(8,128)} %get-tuple-element.55), channel_id=1, source_target_pairs={{0,15},{1,0},{2,1},{3,2},{4,3},{5,4},{6,5},{7,6},{8,7},{9,8},{10,9... | collective-permute-start | bytes 1179656 | tf_op jit(solution)/shard_map/ppermute | solution.py:21
  21.5 2.4 %shard_map.110 = f32[1,768,256]{2,1,0:T(8,128)S(1)} custom-call(bf16[768,2048]{1,0:T(8,128)(2,1)S(1)} %bitcast.105, bf16[9,2048,256]{2,1,0:T(8,128)(2,1)S(1)} %bitcast.101), custom_call_target="tpu_custom_call" | custom-call | flops 2415919104 | bytes 3145728 | tf_op jit(solution)/shard_map/pallas_call | solution.py:96
  25.7 4.5 %collective-permute-start.4 = (f32[12,24,256]{2,1,0:T(8,128)}, f32[12,24,256]{2,1,0:T(8,128)S(1)}, u32[]{:S(2)}, u32[]{:S(2)}) collective-permute-start(f32[12,24,256]{2,1,0:T(8,128)} %get-tuple-element.57), channel_id=1, source_target_pairs={{0,16},{16,32},{32,48},{48,64},{64,80},{80,96},{96,112},{1,17},{17... | collective-permute-start | bytes 884744 | tf_op jit(solution)/shard_map/ppermute | solution.py:21
  31.6 3.5 %shard_map.112 = (bf16[512,768]{1,0:T(8,128)(2,1)S(1)}, bf16[512,768]{1,0:T(8,128)(2,1)S(1)}, bf16[512,768]{1,0:T(8,128)(2,1)}, bf16[512,768]{1,0:T(8,128)(2,1)S(1)}) custom-call(s32[1]{0:T(128)} %bitcast.8.where_ref.place_ref, bf16[768,2048]{1,0:T(8,128)(2,1)S(1)} %bitcast.106), custom_call_target="tpu_custom_call" | custom-call | bytes 6291456 | tf_op jit(solution)/shard_map/pallas_call | solution.py:127
  37.5 6.9 %collective-permute-done.4 = f32[12,24,256]{2,1,0:T(8,128)S(1)} collective-permute-done((f32[12,24,256]{2,1,0:T(8,128)}, f32[12,24,256]{2,1,0:T(8,128)S(1)}, u32[]{:S(2)}, u32[]{:S(2)}) %collective-permute-start.4) | collective-permute-done | bytes 294944 | tf_op jit(solution)/shard_map/ppermute | solution.py:21
  46.5 3.9 %collective-permute-start.6 = (f32[4,128]{1,0:T(4,128)S(1)}, f32[4,128]{1,0:T(4,128)S(1)}, u32[]{:S(2)}, u32[]{:S(2)}) collective-permute-start(f32[4,128]{1,0:T(4,128)S(1)} %reshape.151), channel_id=1, source_target_pairs={{0,1},{1,0},{2,3},{3,2},{4,5},{5,4},{6,7},{7,6},{8,9},{9,8},{10,11... | collective-permute-start | bytes 6152 | tf_op jit(solution)/shard_map/ppermute | solution.py:26
  52.0 10.1 %all-to-all-start = ((f32[64,4,128]{2,1,0:T(4,128)}), f32[64,4,128]{2,1,0:T(4,128)S(1)}, u32[]{:S(2)}, u32[]{:S(2)}) async-start(f32[64,4,128]{2,1,0:T(4,128)} %broadcast_in_dim.32), calls=%async_computation | async-start | bytes 262144 | tf_op jit(solution)/shard_map/all_to_all | solution.py:48
  64.0 6.8 %all-to-all-done = f32[64,4,128]{2,1,0:T(4,128)S(1)} async-done(((f32[64,4,128]{2,1,0:T(4,128)}), f32[64,4,128]{2,1,0:T(4,128)S(1)}, u32[]{:S(2)}, u32[]{:S(2)}) %all-to-all-start) | async-done | bytes 131104 | tf_op jit(solution)/shard_map/all_to_all | solution.py:48
  79.2 6.4 %collective-permute-start.10 = (bf16[13,24,256]{2,1,0:T(8,128)(2,1)S(1)}, bf16[13,24,256]{2,1,0:T(8,128)(2,1)}, u32[]{:S(2)}, u32[]{:S(2)}) collective-permute-start(bf16[13,24,256]{2,1,0:T(8,128)(2,1)S(1)} %pad_maximum_fusion.2), channel_id=1, source_target_pairs={{0,16},{16,32},{32,48},{48,64},{64,80},{80,96},{96,112},{1,17},{17... | collective-permute-start | bytes 479240 | tf_op jit(solution)/shard_map/ppermute | solution.py:21
  86.5 4.8 %all-to-all-start.1 = ((f32[64,3,4,128]{3,2,1,0:T(4,128)}), f32[64,3,4,128]{3,2,1,0:T(4,128)S(1)}, u32[]{:S(2)}, u32[]{:S(2)}) async-start(f32[64,3,4,128]{3,2,1,0:T(4,128)} %broadcast_in_dim.36), calls=%async_computation.1 | async-start | bytes 786432 | tf_op jit(solution)/shard_map/all_to_all | solution.py:48
  93.6 8.8 %all-to-all-done.1 = f32[64,3,4,128]{3,2,1,0:T(4,128)S(1)} async-done(((f32[64,3,4,128]{3,2,1,0:T(4,128)}), f32[64,3,4,128]{3,2,1,0:T(4,128)S(1)}, u32[]{:S(2)}, u32[]{:S(2)}) %all-to-all-start.1) | async-done | bytes 393248 | tf_op jit(solution)/shard_map/all_to_all | solution.py:48
  108.9 6.7 %collective-permute-start.15 = (bf16[56,24,256]{2,1,0:T(8,128)(2,1)S(1)}, bf16[56,24,256]{2,1,0:T(8,128)(2,1)S(1)}, u32[]{:S(2)}, u32[]{:S(2)}) collective-permute-start(bf16[56,24,256]{2,1,0:T(8,128)(2,1)S(1)} %bitcast.112), channel_id=1, source_target_pairs={{0,1},{1,0},{2,3},{3,2},{4,5},{5,4},{6,7},{7,6},{8,9},{9,8},{10,11... | collective-permute-start | bytes 2064392 | tf_op jit(solution)/shard_map/ppermute | solution.py:26
  115.6 4.7 %collective-permute-done.12.refs_1_ = bf16[56,24,256]{2,1,0:T(8,128)(2,1)S(1)} collective-permute-done((bf16[56,24,256]{2,1,0:T(8,128)(2,1)S(1)}, bf16[56,24,256]{2,1,0:T(8,128)(2,1)S(1)}, u32[]{:S(2)}, u32[]{:S(2)}) %collective-permute-start.12) | collective-permute-done | bytes 688160 | tf_op jit(solution)/shard_map/ppermute | solution.py:26
  120.3 5.0 %collective-permute-start.16 = (bf16[56,24,256]{2,1,0:T(8,128)(2,1)S(1)}, bf16[56,24,256]{2,1,0:T(8,128)(2,1)S(1)}, u32[]{:S(2)}, u32[]{:S(2)}) collective-permute-start(bf16[56,24,256]{2,1,0:T(8,128)(2,1)S(1)} %collective-permute-done.12.refs_1_), channel_id=1, source_target_pairs={{0,1},{1,0},{2,3},{3,2},{4,5},{5,4},{6,7},{7,6},{8,9},{9,8},{10,11... | collective-permute-start | bytes 2064392 | tf_op jit(solution)/shard_map/ppermute | solution.py:26
  125.3 2.5 %collective-permute-start.17 = (bf16[56,12,256]{2,1,0:T(8,128)(2,1)S(1)}, bf16[56,12,256]{2,1,0:T(8,128)(2,1)S(1)}, u32[]{:S(2)}, u32[]{:S(2)}) collective-permute-start(bf16[56,12,256]{2,1,0:T(8,128)(2,1)S(1)} %collective-permute-done.13.refs_2_), channel_id=1, source_target_pairs={{0,1},{1,0},{2,3},{3,2},{4,5},{5,4},{6,7},{7,6},{8,9},{9,8},{10,11... | collective-permute-start | bytes 1032200 | tf_op jit(solution)/shard_map/ppermute | solution.py:26
  131.4 9.8 %shard_map.115 = bf16[8,16,3,3,8,128]{5,4,3,2,1,0:T(8,128)(2,1)} custom-call(bf16[3,4,1344,256]{3,2,1,0:T(8,128)(2,1)S(1)} %shard_map.113.d_ref, bf16[512,768]{1,0:T(8,128)(2,1)S(1)} %copy-done.12, bf16[512,768]{1,0:T(8,128)(2,1)S(1)} %collective-permute-done.19.refs_1_, bf16[512,768]{1,0:T(8,128)(2,1)S(1)} %collective-permute-done.7.refs_2_, ...), custom_call_target="tpu_custom_call" | custom-call | flops 7247757312 | bytes 11403264 | tf_op jit(solution)/shard_map/pallas_call | solution.py:208
  141.2 4.7 %all-to-all-start.2 = ((bf16[128,72,128]{2,1,0:T(8,128)(2,1)}), bf16[128,72,128]{2,1,0:T(8,128)(2,1)S(1)}, u32[]{:S(2)}, u32[]{:S(2)}) async-start(bf16[128,72,128]{2,1,0:T(8,128)(2,1)} %bitcast.42), calls=%async_computation.2 | async-start | bytes 4718592 | tf_op jit(solution)/shard_map/all_to_all | solution.py:359
  148.8 3.7 %copy-done.3 = bf16[3,3,2048,256]{3,2,1,0:T(8,128)(2,1)S(1)} copy-done((bf16[3,3,2048,256]{3,2,1,0:T(8,128)(2,1)S(1)}, bf16[3,3,2048,256]{3,2,1,0:T(8,128)(2,1)}, u32[]{:S(2)}) %copy-start.3) | copy-done | bytes 9437208
  152.5 9.6 %shard_map.114 = bf16[768,2048]{1,0:T(8,128)(2,1)} custom-call(bf16[3,1344,256]{2,1,0:T(8,128)(2,1)S(1)} %slice_bitcast_fusion.d_ref, bf16[9,2048,256]{2,1,0:T(8,128)(2,1)S(1)} %bitcast.102), custom_call_target="tpu_custom_call" | custom-call | flops 7247757312 | bytes 9437184 | tf_op jit(solution)/shard_map/pallas_call | solution.py:237
  162.1 16.7 %all-to-all-done.2 = bf16[128,72,128]{2,1,0:T(8,128)(2,1)S(1)} async-done(((bf16[128,72,128]{2,1,0:T(8,128)(2,1)}), bf16[128,72,128]{2,1,0:T(8,128)(2,1)S(1)}, u32[]{:S(2)}, u32[]{:S(2)}) %all-to-all-start.2) | async-done | bytes 2359328 | tf_op jit(solution)/shard_map/all_to_all | solution.py:359
  (136 shorter events, 40.0 us)
Async XLA Ops:
  0.6 71.5 %copy-start = (f32[3,256]{1,0:T(4,128)S(1)}, f32[3,256]{1,0:T(4,128)}, u32[]{:S(2)}) copy-start(f32[3,256]{1,0:T(4,128)} %param.10) | copy-start | bytes 9220
  9.2 14.7 %collective-permute-start.2 = (f32[2,12,12,256]{3,2,1,0:T(8,128)S(1)}, f32[2,12,12,256]{3,2,1,0:T(8,128)S(1)}, u32[]{:S(2)}, u32[]{:S(2)}) collective-permute-start(f32[2,12,12,256]{3,2,1,0:T(8,128)S(1)} %get-tuple-element.51), channel_id=1, source_target_pairs={{0,1},{1,2},{2,3},{3,4},{4,5},{5,6},{6,7},{7,8},{8,9},{9,10},{10,1... | collective-permute-start | bytes 884744 | tf_op jit(solution)/shard_map/ppermute | solution.py:21
  12.0 12.0 %collective-permute-start.3 = (f32[2,12,12,256]{3,2,1,0:T(8,128)S(1)}, f32[2,12,12,256]{3,2,1,0:T(8,128)S(1)}, u32[]{:S(2)}, u32[]{:S(2)}) collective-permute-start(f32[2,12,12,256]{3,2,1,0:T(8,128)S(1)} %get-tuple-element.52), channel_id=1, source_target_pairs={{0,15},{1,0},{2,1},{3,2},{4,3},{5,4},{6,5},{7,6},{8,7},{9,8},{10,9... | collective-permute-start | bytes 884744 | tf_op jit(solution)/shard_map/ppermute | solution.py:21
  18.1 17.0 %collective-permute-start.1 = (f32[32,12,256]{2,1,0:T(8,128)}, f32[32,12,256]{2,1,0:T(8,128)}, u32[]{:S(2)}, u32[]{:S(2)}) collective-permute-start(f32[32,12,256]{2,1,0:T(8,128)} %get-tuple-element.55), channel_id=1, source_target_pairs={{0,15},{1,0},{2,1},{3,2},{4,3},{5,4},{6,5},{7,6},{8,7},{9,8},{10,9... | collective-permute-start | bytes 1179656 | tf_op jit(solution)/shard_map/ppermute | solution.py:21
  21.4 13.7 %collective-permute-start = (f32[32,12,256]{2,1,0:T(8,128)}, f32[32,12,256]{2,1,0:T(8,128)}, u32[]{:S(2)}, u32[]{:S(2)}) collective-permute-start(f32[32,12,256]{2,1,0:T(8,128)} %get-tuple-element.56), channel_id=1, source_target_pairs={{0,1},{1,2},{2,3},{3,4},{4,5},{5,6},{6,7},{7,8},{8,9},{9,10},{10,1... | collective-permute-start | bytes 1179656 | tf_op jit(solution)/shard_map/ppermute | solution.py:21
  25.7 18.7 %collective-permute-start.4 = (f32[12,24,256]{2,1,0:T(8,128)}, f32[12,24,256]{2,1,0:T(8,128)S(1)}, u32[]{:S(2)}, u32[]{:S(2)}) collective-permute-start(f32[12,24,256]{2,1,0:T(8,128)} %get-tuple-element.57), channel_id=1, source_target_pairs={{0,16},{16,32},{32,48},{48,64},{64,80},{80,96},{96,112},{1,17},{17... | collective-permute-start | bytes 884744 | tf_op jit(solution)/shard_map/ppermute | solution.py:21
  30.3 14.1 %collective-permute-start.5 = (f32[12,24,256]{2,1,0:T(8,128)}, f32[12,24,256]{2,1,0:T(8,128)}, u32[]{:S(2)}, u32[]{:S(2)}) collective-permute-start(f32[12,24,256]{2,1,0:T(8,128)} %get-tuple-element.58), channel_id=1, source_target_pairs={{16,0},{32,16},{48,32},{64,48},{80,64},{96,80},{112,96},{17,1},{33... | collective-permute-start | bytes 884744 | tf_op jit(solution)/shard_map/ppermute | solution.py:21
  35.1 35.7 %collective-permute-start.7 = (bf16[512,768]{1,0:T(8,128)(2,1)}, bf16[512,768]{1,0:T(8,128)(2,1)S(1)}, u32[]{:S(2)}, u32[]{:S(2)}) collective-permute-start(bf16[512,768]{1,0:T(8,128)(2,1)} %get-tuple-element.30), channel_id=1, source_target_pairs={{0,2},{1,3},{2,0},{3,1},{4,6},{5,7},{6,4},{7,5},{8,10},{9,11},{10,... | collective-permute-start | bytes 2359304 | tf_op jit(solution)/shard_map/ppermute | solution.py:26
  46.5 4.8 %collective-permute-start.6 = (f32[4,128]{1,0:T(4,128)S(1)}, f32[4,128]{1,0:T(4,128)S(1)}, u32[]{:S(2)}, u32[]{:S(2)}) collective-permute-start(f32[4,128]{1,0:T(4,128)S(1)} %reshape.151), channel_id=1, source_target_pairs={{0,1},{1,0},{2,3},{3,2},{4,5},{5,4},{6,7},{7,6},{8,9},{9,8},{10,11... | collective-permute-start | bytes 6152 | tf_op jit(solution)/shard_map/ppermute | solution.py:26
  52.0 18.8 %all-to-all-start = ((f32[64,4,128]{2,1,0:T(4,128)}), f32[64,4,128]{2,1,0:T(4,128)S(1)}, u32[]{:S(2)}, u32[]{:S(2)}) async-start(f32[64,4,128]{2,1,0:T(4,128)} %broadcast_in_dim.32), calls=%async_computation | async-start | bytes 262144 | tf_op jit(solution)/shard_map/all_to_all | solution.py:48
  62.3 40.2 %collective-permute-start.9 = (bf16[512,768]{1,0:T(8,128)(2,1)}, bf16[512,768]{1,0:T(8,128)(2,1)S(1)}, u32[]{:S(2)}, u32[]{:S(2)}) collective-permute-start(bf16[512,768]{1,0:T(8,128)(2,1)} %copy-done.17), channel_id=1, source_target_pairs={{0,3},{1,2},{2,1},{3,0},{4,7},{5,6},{6,5},{7,4},{8,11},{9,10},{10,... | collective-permute-start | bytes 2359304 | tf_op jit(solution)/shard_map/ppermute | solution.py:26
  75.5 15.8 %collective-permute-start.11 = (bf16[13,24,256]{2,1,0:T(8,128)(2,1)S(1)}, bf16[13,24,256]{2,1,0:T(8,128)(2,1)S(1)}, u32[]{:S(2)}, u32[]{:S(2)}) collective-permute-start(bf16[13,24,256]{2,1,0:T(8,128)(2,1)S(1)} %pad_maximum_fusion.3), channel_id=1, source_target_pairs={{16,0},{32,16},{48,32},{64,48},{80,64},{96,80},{112,96},{17,1},{33... | collective-permute-start | bytes 479240 | tf_op jit(solution)/shard_map/ppermute | solution.py:21
  77.6 8.1 %collective-permute-start.8 = (f32[3,4,128]{2,1,0:T(4,128)S(1)}, f32[3,4,128]{2,1,0:T(4,128)S(1)}, u32[]{:S(2)}, u32[]{:S(2)}) collective-permute-start(f32[3,4,128]{2,1,0:T(4,128)S(1)} %reshape.152), channel_id=1, source_target_pairs={{0,1},{1,0},{2,3},{3,2},{4,5},{5,4},{6,7},{7,6},{8,9},{9,8},{10,11... | collective-permute-start | bytes 18440 | tf_op jit(solution)/shard_map/ppermute | solution.py:26
  79.2 12.1 %collective-permute-start.10 = (bf16[13,24,256]{2,1,0:T(8,128)(2,1)S(1)}, bf16[13,24,256]{2,1,0:T(8,128)(2,1)}, u32[]{:S(2)}, u32[]{:S(2)}) collective-permute-start(bf16[13,24,256]{2,1,0:T(8,128)(2,1)S(1)} %pad_maximum_fusion.2), channel_id=1, source_target_pairs={{0,16},{16,32},{32,48},{48,64},{64,80},{80,96},{96,112},{1,17},{17... | collective-permute-start | bytes 479240 | tf_op jit(solution)/shard_map/ppermute | solution.py:21
  86.5 15.9 %all-to-all-start.1 = ((f32[64,3,4,128]{3,2,1,0:T(4,128)}), f32[64,3,4,128]{3,2,1,0:T(4,128)S(1)}, u32[]{:S(2)}, u32[]{:S(2)}) async-start(f32[64,3,4,128]{3,2,1,0:T(4,128)} %broadcast_in_dim.36), calls=%async_computation.1 | async-start | bytes 786432 | tf_op jit(solution)/shard_map/all_to_all | solution.py:48
  105.0 15.3 %collective-permute-start.12 = (bf16[56,24,256]{2,1,0:T(8,128)(2,1)S(1)}, bf16[56,24,256]{2,1,0:T(8,128)(2,1)S(1)}, u32[]{:S(2)}, u32[]{:S(2)}) collective-permute-start(bf16[56,24,256]{2,1,0:T(8,128)(2,1)S(1)} %bitcast.110), channel_id=1, source_target_pairs={{0,2},{1,3},{2,0},{3,1},{4,6},{5,7},{6,4},{7,5},{8,10},{9,11},{10,... | collective-permute-start | bytes 2064392 | tf_op jit(solution)/shard_map/ppermute | solution.py:26
  105.2 26.1 %collective-permute-start.19 = (bf16[512,768]{1,0:T(8,128)(2,1)S(1)}, bf16[512,768]{1,0:T(8,128)(2,1)S(1)}, u32[]{:S(2)}, u32[]{:S(2)}) collective-permute-start(bf16[512,768]{1,0:T(8,128)(2,1)S(1)} %copy-done.14), channel_id=1, source_target_pairs={{0,1},{1,0},{2,3},{3,2},{4,5},{5,4},{6,7},{7,6},{8,9},{9,8},{10,11... | collective-permute-start | bytes 2359304 | tf_op jit(solution)/shard_map/ppermute | solution.py:26
  107.4 17.9 %collective-permute-start.14 = (bf16[56,12,256]{2,1,0:T(8,128)(2,1)S(1)}, bf16[56,12,256]{2,1,0:T(8,128)(2,1)S(1)}, u32[]{:S(2)}, u32[]{:S(2)}) collective-permute-start(bf16[56,12,256]{2,1,0:T(8,128)(2,1)S(1)} %slice_select_fusion), channel_id=1, source_target_pairs={{3,7},{0,12},{7,11},{4,0},{11,15},{8,4},{15,3},{12,8},{19,23},{16,... | collective-permute-start | bytes 1032200 | tf_op jit(solution)/shard_map/ppermute | solution.py:35
  108.2 17.0 %collective-permute-start.13 = (bf16[56,12,256]{2,1,0:T(8,128)(2,1)S(1)}, bf16[56,12,256]{2,1,0:T(8,128)(2,1)S(1)}, u32[]{:S(2)}, u32[]{:S(2)}) collective-permute-start(bf16[56,12,256]{2,1,0:T(8,128)(2,1)S(1)} %slice_select_fusion), channel_id=1, source_target_pairs={{3,4},{0,15},{7,8},{4,3},{11,12},{8,7},{15,0},{12,11},{19,20},{16,... | collective-permute-start | bytes 1032200 | tf_op jit(solution)/shard_map/ppermute | solution.py:35
  108.9 20.3 %collective-permute-start.15 = (bf16[56,24,256]{2,1,0:T(8,128)(2,1)S(1)}, bf16[56,24,256]{2,1,0:T(8,128)(2,1)S(1)}, u32[]{:S(2)}, u32[]{:S(2)}) collective-permute-start(bf16[56,24,256]{2,1,0:T(8,128)(2,1)S(1)} %bitcast.112), channel_id=1, source_target_pairs={{0,1},{1,0},{2,3},{3,2},{4,5},{5,4},{6,7},{7,6},{8,9},{9,8},{10,11... | collective-permute-start | bytes 2064392 | tf_op jit(solution)/shard_map/ppermute | solution.py:26
  120.3 8.9 %collective-permute-start.16 = (bf16[56,24,256]{2,1,0:T(8,128)(2,1)S(1)}, bf16[56,24,256]{2,1,0:T(8,128)(2,1)S(1)}, u32[]{:S(2)}, u32[]{:S(2)}) collective-permute-start(bf16[56,24,256]{2,1,0:T(8,128)(2,1)S(1)} %collective-permute-done.12.refs_1_), channel_id=1, source_target_pairs={{0,1},{1,0},{2,3},{3,2},{4,5},{5,4},{6,7},{7,6},{8,9},{9,8},{10,11... | collective-permute-start | bytes 2064392 | tf_op jit(solution)/shard_map/ppermute | solution.py:26
  125.3 2.5 %collective-permute-start.18 = (bf16[56,12,256]{2,1,0:T(8,128)(2,1)S(1)}, bf16[56,12,256]{2,1,0:T(8,128)(2,1)S(1)}, u32[]{:S(2)}, u32[]{:S(2)}) collective-permute-start(bf16[56,12,256]{2,1,0:T(8,128)(2,1)S(1)} %collective-permute-done.14.refs_3_), channel_id=1, source_target_pairs={{0,1},{1,0},{2,3},{3,2},{4,5},{5,4},{6,7},{7,6},{8,9},{9,8},{10,11... | collective-permute-start | bytes 1032200 | tf_op jit(solution)/shard_map/ppermute | solution.py:26
  125.3 4.0 %collective-permute-start.17 = (bf16[56,12,256]{2,1,0:T(8,128)(2,1)S(1)}, bf16[56,12,256]{2,1,0:T(8,128)(2,1)S(1)}, u32[]{:S(2)}, u32[]{:S(2)}) collective-permute-start(bf16[56,12,256]{2,1,0:T(8,128)(2,1)S(1)} %collective-permute-done.13.refs_2_), channel_id=1, source_target_pairs={{0,1},{1,0},{2,3},{3,2},{4,5},{5,4},{6,7},{7,6},{8,9},{9,8},{10,11... | collective-permute-start | bytes 1032200 | tf_op jit(solution)/shard_map/ppermute | solution.py:26
  141.2 37.6 %all-to-all-start.2 = ((bf16[128,72,128]{2,1,0:T(8,128)(2,1)}), bf16[128,72,128]{2,1,0:T(8,128)(2,1)S(1)}, u32[]{:S(2)}, u32[]{:S(2)}) async-start(bf16[128,72,128]{2,1,0:T(8,128)(2,1)} %bitcast.42), calls=%async_computation.2 | async-start | bytes 4718592 | tf_op jit(solution)/shard_map/all_to_all | solution.py:359
  (22 other events, 197.7 us)
